TPU v7x, 128 devices: a whole 4x4x4 slice. The times are simulated.
128 devices in a mesh: tx: 8 (over z_hi, y), ty: 16 (over x, z_lo, core).
Axes of the slice: x: 4, y: 4, z: 4 (z_hi: 2, z_lo: 2; z = z_hi * 2 + z_lo), core: 2. Of those that a mesh axis runs over, the one named last changes fastest.
Arguments:
- states: bfloat16 [2, 256, 16384], P(None, 'ty', 'tx')
- norm_gain: bfloat16 [16384], P('tx'), may hold values from 0.099609375 to 1.8984375
- w_gate: bfloat16 [16384, 26624], P('tx', 'ty'), may hold values from -0.046875 to 0.046875
- w_up: bfloat16 [16384, 26624], P('tx', 'ty'), may hold values from -0.046875 to 0.046875
- w_down: bfloat16 [26624, 16384], P('ty', 'tx'), may hold values from -0.0390625 to 0.0390625
- w_qkv: bfloat16 [16384, 3, 4096], P('tx', None, 'ty'), may hold values from -0.046875 to 0.046875
- w_class: bfloat16 [4096, 14], P('ty'), may hold values from -0.375 to 0.375
- cache_keys: bfloat16 [256, 64, 4096], P('tx', None, 'ty')
- cache_values: bfloat16 [256, 64, 4096], P('tx', None, 'ty'), may hold values from -6 to 6
- cache_lengths: int32 [256], P('tx'), may hold values from 1 to 64, as said below
- row_slots: int32 [256], replicated, may hold values from 0 to 255, each once
Outputs:
- stream_out: bfloat16 [2, 256, 16384], P(None, 'ty', 'tx')
- category_logits: float32 [2, 256, 14], replicated
Inputs may be any that keep to these rules, and one draw needn't show every extreme that they name: `cache_lengths`: some slot has exactly 64 live positions. `row_slots`: each cache slot belongs to exactly one row.
All inputs are finite; a program needn't handle non-finite values.
Results may differ from a plain program's by a relative error of at most 0.015.
The roundings to bfloat16 on the way count: a program that leaves them out, or rounds other values in their place, can miss the bound.
Values may be sent and summed in bfloat16 or wider, within the bound.
No kernel may reach another device: no remote copies, remote signals or barrier semaphores. Data moves between devices by JAX's collectives and lax.ppermute only.
A program may use at most 128 MiB of HBM per device.

v0:
```python
import jax
import jax.numpy as jnp
from jax import lax
from jax.sharding import PartitionSpec as P

D = 16384
HEAD_DIM = 128


def per_device(
    states,
    norm_gain,
    w_gate,
    w_up,
    w_down,
    w_qkv,
    w_class,
    cache_keys,
    cache_values,
    cache_lengths,
    row_slots,
):
    steps_count = states.shape[0]
    local_rows = states.shape[1]
    total_rows = row_slots.shape[0]
    owner_rows = cache_keys.shape[0]
    history = cache_keys.shape[1]
    local_width = w_qkv.shape[2]
    heads_here = local_width // HEAD_DIM
    values_f = states.astype(jnp.float32)
    squares = lax.psum(jnp.sum(values_f * values_f, axis=2), "tx")
    scale = lax.rsqrt(squares / D + 1e-05)
    normed_local = (values_f * scale[:, :, None] * norm_gain.astype(jnp.float32)).astype(
        jnp.bfloat16
    )
    normed = lax.all_gather(normed_local, "ty", axis=1, tiled=True)
    slot_rows = (
        jnp.zeros((total_rows,), jnp.int32)
        .at[row_slots]
        .set(jnp.arange(total_rows, dtype=jnp.int32))
    )
    qkv_weight = w_qkv.reshape(w_qkv.shape[0], 3 * local_width)
    outputs = []
    partials = []
    new_keys = []
    new_values = []
    for step in range(steps_count):
        normed_step = normed[step]
        gate, up = lax.psum(
            (
                jnp.dot(normed_step, w_gate, preferred_element_type=jnp.float32),
                jnp.dot(normed_step, w_up, preferred_element_type=jnp.float32),
            ),
            "tx",
        )
        hidden = (jax.nn.silu(gate) * up).astype(jnp.bfloat16)

        def down_term(start, count, source=hidden):
            return jnp.dot(source, w_down, preferred_element_type=jnp.float32)

        mixed = lax.psum_scatter(
            down_term(jnp.int32(0), local_rows * lax.axis_size("ty")),
            "ty",
            scatter_dimension=0,
            tiled=True,
        )
        stream = (values_f[step] + mixed).astype(jnp.bfloat16)
        outputs.append(stream)
        stream_all = lax.all_gather(stream, "ty", axis=0, tiled=True)
        ordered = jnp.take(stream_all, slot_rows, axis=0)
        full = lax.psum(jnp.dot(ordered, qkv_weight, preferred_element_type=jnp.float32), "tx")
        owned = lax.dynamic_slice_in_dim(full, lax.axis_index("tx") * owner_rows, owner_rows, 0)
        triple = owned.astype(jnp.bfloat16).reshape(owner_rows, 3, local_width)
        query = triple[:, 0]
        new_keys.append(triple[:, 1])
        new_values.append(triple[:, 2])
        keys = jnp.concatenate([cache_keys, jnp.stack(new_keys, axis=1)], axis=1)
        vals = jnp.concatenate([cache_values, jnp.stack(new_values, axis=1)], axis=1)
        count_keys = keys.shape[1]
        query_h = query.reshape(owner_rows, heads_here, HEAD_DIM)
        keys_h = keys.reshape(owner_rows, count_keys, heads_here, HEAD_DIM)
        vals_h = vals.reshape(owner_rows, count_keys, heads_here, HEAD_DIM)
        scores = jnp.einsum(
            "shd,slhd->shl", query_h, keys_h, preferred_element_type=jnp.float32
        ) * HEAD_DIM ** (-0.5)
        where_pos = jnp.arange(count_keys, dtype=jnp.int32)
        valid = (where_pos[None, :] < cache_lengths[:, None]) | (where_pos[None, :] >= history)
        scores = jnp.where(valid[:, None, :], scores, jnp.float32(-1e30))
        top = jnp.max(scores, axis=2, keepdims=True)
        expo = jnp.exp(scores - top)
        weights = (expo / jnp.sum(expo, axis=2, keepdims=True)).astype(jnp.bfloat16)
        attended = jnp.einsum("shl,slhd->shd", weights, vals_h, preferred_element_type=jnp.float32)
        attended = attended.reshape(owner_rows, local_width).astype(jnp.bfloat16)
        partials.append(jnp.dot(attended, w_class, preferred_element_type=jnp.float32))
    stacked = jnp.stack(partials, axis=0)
    summed = lax.psum(stacked, "ty")
    by_slot = lax.all_gather(summed, "tx", axis=1, tiled=True)
    category_logits = jnp.take(by_slot, row_slots, axis=1)
    return (jnp.stack(outputs, axis=0), category_logits)


def solution(mesh):
    return jax.shard_map(
        per_device,
        mesh=mesh,
        in_specs=(
            P(None, "ty", "tx"),
            P("tx"),
            P("tx", "ty"),
            P("tx", "ty"),
            P("ty", "tx"),
            P("tx", None, "ty"),
            P("ty", None),
            P("tx", None, "ty"),
            P("tx", None, "ty"),
            P("tx"),
            P(),
        ),
        out_specs=(P(None, "ty", "tx"), P()),
        check_vma=False,
    )
```

profile of v0, /device:TPU:1, one launch (start us, length us, event | category | flops | bytes accessed | tf_op | source)
XLA Modules:
  0.0 634.2 jit_solution(3496387815426926068)
XLA Ops:
  7.9 1.0 multiply_reduce_fusion
  8.9 22.3 %psum.56 = f32[2,16]{1,0:T(2,128)S(1)} all-reduce(f32[2,16]{1,0:T(2,128)S(1)} %multiply_reduce_fusion), channel_id=1, replica_groups=mesh['tx'=8,'ty'=16] {'tx'}, use_global_device_ids=true, to_apply=%region_1.0 | all-reduce | flops 32 | bytes 256 | tf_op jit(solution)/shard_map/psum | solution.py:31
  31.3 1.7 multiply_convert_fusion.4
  33.0 35.0 %all-gather.4.cloned.1.call-done = bf16[2,256,2048]{2,1,0:T(8,128)(2,1)} async-done(((bf16[2,16,2048]{2,1,0:T(8,128)(2,1)}), bf16[2,256,2048]{2,1,0:T(8,128)(2,1)}) %all-gather.4.cloned.1.call-update) | async-done | bytes 2097168 | tf_op jit(solution)/shard_map/all_gather | solution.py:36
  68.0 6.7 %fusion.28 = f32[256,1664]{1,0:T(8,128)} fusion(bf16[2048,1664]{1,0:T(8,128)(2,1)} %param.16, bf16[2,256,2048]{2,1,0:T(8,128)(2,1)} %all-gather.4.cloned.1.call-done), kind=kOutput, calls=%fused_computation.42 | convolution fusion | flops 1744830464 | bytes 9568256 | tf_op jit(solution)/shard_map/dot_general | solution.py:52
  74.7 6.4 %fusion.30 = f32[256,1664]{1,0:T(8,128)} fusion(bf16[2048,1664]{1,0:T(8,128)(2,1)} %param.16, bf16[2,256,2048]{2,1,0:T(8,128)(2,1)S(1)} %copy-done.10), kind=kOutput, calls=%fused_computation.44 | convolution fusion | flops 1744830464 | bytes 9568256 | tf_op jit(solution)/shard_map/dot_general | solution.py:52
  81.1 3.3 fusion.29
  84.4 3.3 fusion.31
  87.8 157.2 %all-reduce.5.cloned.1.call-done = (f32[256,1664]{1,0:T(8,128)}, f32[256,1664]{1,0:T(8,128)}, f32[256,1664]{1,0:T(8,128)}, f32[256,1664]{1,0:T(8,128)}) async-done(((f32[256,1664]{1,0:T(8,128)}, f32[256,1664]{1,0:T(8,128)}, f32[256,1664]{1,0:T(8,128)}, f32[256,1664]{1,0:T(8,128)}), (f32[256,1664]{1,0:T(8,128)}, f32[256,1664]{1,0:T(8,128)}, f32[256,1664]{1,0:T(8,128)}, ...) | async-done | bytes 6815760 | tf_op jit(solution)/shard_map/psum | solution.py:49
  244.9 7.5 %fusion.33 = f32[256,2048]{1,0:T(8,128)} fusion(bf16[1664,2048]{1,0:T(8,128)(2,1)} %param.17, f32[256,1664]{1,0:T(8,128)} %get-tuple-element.13, f32[256,1664]{1,0:T(8,128)} %get-tuple-element.14), kind=kOutput, calls=%fused_computation.47 | convolution fusion | flops 1747386368 | bytes 12320768 | tf_op jit(solution)/shard_map/dot_general | solution.py:59
  252.5 1.4 copy-done.11
  253.9 7.0 %fusion.32 = f32[256,2048]{1,0:T(8,128)} fusion(bf16[1664,2048]{1,0:T(8,128)(2,1)} %param.17, f32[256,1664]{1,0:T(8,128)S(1)} %copy-done.11, f32[256,1664]{1,0:T(8,128)} %get-tuple-element.16), kind=kOutput, calls=%fused_computation.46 | convolution fusion | flops 1747386368 | bytes 12320768 | tf_op jit(solution)/shard_map/dot_general | solution.py:59
  261.0 49.2 %reduce-scatter.5.cloned.1.call-done = f32[16,2048]{1,0:T(8,128)} async-done(((f32[256,2048]{1,0:T(8,128)}), f32[16,2048]{1,0:T(8,128)}) %reduce-scatter.5.cloned.1.call-update) | async-done | bytes 131088 | tf_op jit(solution)/shard_map/reduce_scatter | solution.py:61
  310.2 64.4 %reduce-scatter.3.cloned.1.call-done = f32[16,2048]{1,0:T(8,128)} async-done(((f32[256,2048]{1,0:T(8,128)}), f32[16,2048]{1,0:T(8,128)}) %reduce-scatter.3.cloned.1.call-update) | async-done | bytes 131088 | tf_op jit(solution)/shard_map/reduce_scatter | solution.py:61
  374.6 1.7 fusion.41
  377.0 3.1 copy.28
  380.1 1.4 scatter_custom_fusion
  382.4 28.9 %all-gather.8.cloned.1.call-done = bf16[256,2048]{1,0:T(8,128)(2,1)} async-done(((bf16[16,2048]{1,0:T(8,128)(2,1)}), bf16[256,2048]{1,0:T(8,128)(2,1)}) %all-gather.8.cloned.1.call-update) | async-done | bytes 1048592 | tf_op jit(solution)/shard_map/all_gather | solution.py:69
  411.4 4.7 gather_fusion.2
  416.1 3.2 fusion.22
  419.3 26.1 %all-gather.6.cloned.1.call-done = bf16[256,2048]{1,0:T(8,128)(2,1)} async-done(((bf16[16,2048]{1,0:T(8,128)(2,1)}), bf16[256,2048]{1,0:T(8,128)(2,1)}) %all-gather.6.cloned.1.call-update) | async-done | bytes 1048592 | tf_op jit(solution)/shard_map/all_gather | solution.py:69
  445.5 4.7 gather_fusion.1
  450.2 3.2 fusion.24
  453.3 71.5 %all-reduce.6 = (bf16[256,768]{1,0:T(8,128)(2,1)S(1)}, bf16[256,768]{1,0:T(8,128)(2,1)S(1)}) all-reduce(f32[256,768]{1,0:T(8,128)} %fusion.22, f32[256,768]{1,0:T(8,128)} %fusion.24), channel_id=1, replica_groups=mesh['tx'=8,'ty'=16] {'tx'}, use_global_device_ids=true, to_apply=%region_12.14 | all-reduce | flops 393216 | bytes 2359296 | tf_op jit(solution)/shard_map/psum | solution.py:71
  525.1 1.4 reshape.167
  526.4 1.9 fusion.10
  528.5 1.4 reshape.168
  530.1 1.7 fusion.8
  532.0 1.2 reshape.170
  533.2 1.9 fusion.6
  536.7 60.5 %psum.63 = f32[2,32,14]{1,2,0:T(8,128)S(1)} all-reduce(f32[2,32,14]{1,2,0:T(8,128)S(1)} %pad_maximum_fusion.5), channel_id=1, replica_groups=mesh['tx'=8,'ty'=16] {'ty'}, use_global_device_ids=true, to_apply=%region_15.17 | all-reduce | flops 896 | bytes 7168 | tf_op jit(solution)/shard_map/psum | solution.py:96
  597.2 28.0 %all_gather.15 = f32[2,256,14]{2,0,1:T(2,128)S(1)} all-gather(f32[2,32,14]{2,0,1:T(2,128)S(1)} %copy.33), channel_id=1, replica_groups=mesh['tx'=8,'ty'=16] {'tx'}, dimensions={1}, use_global_device_ids=true | all-gather | bytes 32256 | tf_op jit(solution)/shard_map/all_gather | solution.py:97
  (77 shorter events, 6.8 us)
Async XLA Ops:
  7.2 529.2 %copy-start = (bf16[256,14]{0,1:T(8,128)(2,1)S(1)}, bf16[256,14]{0,1:T(8,128)(2,1)}, u32[]{:S(2)}) copy-start(bf16[256,14]{0,1:T(8,128)(2,1)} %param.19) | copy-start | bytes 21508
  7.2 60.8 %all-gather.4.cloned.1.call-start = ((), (), s32[]{:S(2)}) async-start(), calls=%async_computation.2 | async-start | bytes 2228224 | tf_op jit(solution)/shard_map/all_gather | solution.py:36
  33.0 212.0 %all-reduce.5.cloned.1.call-start = ((), (), s32[]{:S(2)}) async-start(), calls=%async_computation.7 | async-start | bytes 13631488 | tf_op jit(solution)/shard_map/psum | solution.py:49
  68.0 6.7 %copy-start.10 = (bf16[2,256,2048]{2,1,0:T(8,128)(2,1)S(1)}, bf16[2,256,2048]{2,1,0:T(8,128)(2,1)}, u32[]{:S(2)}) copy-start(bf16[2,256,2048]{2,1,0:T(8,128)(2,1)} %all-gather.4.cloned.1.call-done) | copy-start | bytes 6291460
  68.0 13.1 %slice-start = ((s8[6815744]{0:T(1024)(128)(4,1)}), s8[4194304]{0:T(1024)(128)(4,1)S(1)}, s32[]{:S(2)}) async-start(s8[6815744]{0:T(1024)(128)(4,1)} %bitcast.87), calls=%async_computation.8 | async-start | bytes 8388608
  74.7 6.4 %slice-start.1 = ((s8[6815744]{0:T(1024)(128)(4,1)}), s8[2621440]{0:T(1024)(128)(4,1)S(1)}, s32[]{:S(2)}) async-start(s8[6815744]{0:T(1024)(128)(4,1)} %bitcast.87), calls=%async_computation.9 | async-start | bytes 5242880
  87.7 222.5 %reduce-scatter.5.cloned.1.call-start = ((), (), s32[]{:S(2)}) async-start(), calls=%async_computation.4 | async-start | bytes 2228224 | tf_op jit(solution)/shard_map/reduce_scatter | solution.py:61
  252.4 1.5 copy-start.11
  252.4 122.2 %reduce-scatter.3.cloned.1.call-start = ((), (), s32[]{:S(2)}) async-start(), calls=%async_computation.3 | async-start | bytes 2228224 | tf_op jit(solution)/shard_map/reduce_scatter | solution.py:61
  253.9 7.1 %copy-start.5 = (bf16[2,16,2048]{2,1,0:T(8,128)(2,1)S(1)}, bf16[2,16,2048]{2,1,0:T(8,128)(2,1)}, u32[]{:S(2)}) copy-start(bf16[2,16,2048]{2,1,0:T(8,128)(2,1)} %param.13) | copy-start | bytes 393220
  260.9 115.7 %copy-start.9 = (s32[256]{0:T(256)S(1)}, s32[256]{0:T(256)}, u32[]{:S(2)}) copy-start(s32[256]{0:T(256)} %param.23) | copy-start | bytes 3076
  260.9 116.0 %copy-start.3 = (bf16[2048,3,256]{2,0,1:T(8,128)(2,1)S(1)}, bf16[2048,3,256]{2,0,1:T(8,128)(2,1)}, u32[]{:S(2)}) copy-start(bf16[2048,3,256]{2,0,1:T(8,128)(2,1)} %param.18) | copy-start | bytes 9437188
  260.9 150.4 %all-gather.8.cloned.1.call-start = ((), (), s32[]{:S(2)}) async-start(), calls=%async_computation.6 | async-start | bytes 1114112 | tf_op jit(solution)/shard_map/all_gather | solution.py:69
  376.3 69.1 %all-gather.6.cloned.1.call-start = ((), (), s32[]{:S(2)}) async-start(), calls=%async_computation.5 | async-start | bytes 1114112 | tf_op jit(solution)/shard_map/all_gather | solution.py:69
  376.9 4.6 copy-start.8
  376.9 4.8 copy-start.6
  377.0 4.8 copy-start.7
  382.4 33.7 %copy-start.4 = (bf16[2048,3,256]{0,2,1:T(8,128)(2,1)S(1)}, bf16[2048,3,256]{0,2,1:T(8,128)(2,1)}, u32[]{:S(2)}) copy-start(bf16[2048,3,256]{0,2,1:T(8,128)(2,1)} %copy.28) | copy-start | bytes 9437188
  453.3 71.6 %copy-start.1 = (bf16[32,64,256]{2,1,0:T(8,128)(2,1)S(1)}, bf16[32,64,256]{2,1,0:T(8,128)(2,1)}, u32[]{:S(2)}) copy-start(bf16[32,64,256]{2,1,0:T(8,128)(2,1)} %param.20) | copy-start | bytes 3145732
  525.1 3.3 copy-start.2
Sparse Core Ops, SparseCore 0:
  33.1 34.8 all-gather.3
  87.8 157.0 all-reduce.4
  252.6 57.5 reduce-scatter.4
  312.4 62.1 reduce-scatter.2
  376.4 34.8 all-gather.7
  412.9 32.4 all-gather.5
where the time goes:
time: 644 us; the launch traced here: 634 us
  waiting for transfers between devices  361 us (56%)
  blocking collectives  182 us (28%)
  matrix products  46.8 us (7%)
  local copies, waits for them, and re-layouts  21.8 us (3%)
  between operations  14.4 us (2%)
  other arithmetic  7.17 us (1%)
    psum x1, waiting for transfers between devices, per_device(): lax.psum((jnp.dot(normed_step, w_gate, preferred_element_type=jnp.float32...  157 us
    reduce_scatter x2, waiting for transfers between devices, per_device(): lax.psum_scatter(down_term(jnp.int32(0), local_rows * lax.axis_size('ty')...  114 us
    psum x1, blocking collectives, per_device(): lax.psum(jnp.dot(ordered, qkv_weight, preferred_element_type=jnp.float32)...  71.5 us
    psum x1, blocking collectives, per_device(): summed = lax.psum(stacked, 'ty')  60.5 us
    all_gather x2, waiting for transfers between devices, per_device(): stream_all = lax.all_gather(stream, 'ty', axis=0, tiled=True)  55.1 us
    all_gather x1, waiting for transfers between devices, per_device(): normed = lax.all_gather(normed_local, 'ty', axis=1, tiled=True)  35 us
    all_gather x1, blocking collectives, per_device(): by_slot = lax.all_gather(summed, 'tx', axis=1, tiled=True)  28 us
    psum x1, blocking collectives, per_device(): squares = lax.psum(jnp.sum(values_f * values_f, axis=2), 'tx')  22.3 us
  transfers between devices with their start and end apart: 6, of which 6 were waited for; matrix products, arithmetic and copies ran while one was open for 3% of the time, Pallas kernels for 0%

commit v1 on v0

v1 whole, which is shorter than its diff:
```python
import functools

import jax
import jax.numpy as jnp
from jax import lax
from jax.experimental import pallas as pl
from jax.experimental.pallas import tpu as pltpu
from jax.sharding import PartitionSpec as P

D = 16384
HEAD_DIM = 128
DOWN = 2.0 ** -24
UP = 2.0 ** 24
MOVES = [(d, dz) for dz in range(2) for d in range(4)]
LIMIT = 24 * 1024 * 1024


def tx_move(array, dy, dz):
    pairs = [(z * 4 + y, (z ^ dz) * 4 + (y + dy) % 4) for z in range(2) for y in range(4)]
    return lax.ppermute(array, "tx", pairs)


def ty_move(array, dx, dz, dc):
    pairs = [
        (x * 4 + z * 2 + c, ((x + dx) % 4) * 4 + (z ^ dz) * 2 + (c ^ dc))
        for x in range(4)
        for z in range(2)
        for c in range(2)
    ]
    return lax.ppermute(array, "ty", pairs)


def gather_ty(rows):
    pieces = [rows] + [ty_move(rows, dx, dz, 0) for dx, dz in MOVES[1:]]
    mine = jnp.concatenate(pieces, axis=0)
    return mine, ty_move(mine, 0, 0, 1)


def f32(array):
    return array.astype(jnp.float32)


def total(blocks):
    out = f32(blocks[0])
    for block in blocks[1:]:
        out = out + f32(block)
    return out


def gate_up_kernel(order, x_ref, gain_ref, wg_ref, wu_ref, *refs):
    outs, scaled = refs[:-1], refs[-1]
    step = pl.program_id(0)
    hidden = 128 * pl.num_programs(0)
    rows = outs[0].shape[0]
    unit = x_ref.shape[0] // 8

    @pl.when(step == 0)
    def _():
        gain = gain_ref[...].astype(jnp.float32) * DOWN
        lane = lax.broadcasted_iota(jnp.int32, (unit, 128), 1)
        for n in range(8):
            start = pl.multiple_of(order[n] * unit, unit)
            values = x_ref[pl.ds(start, unit), :].astype(jnp.float32)
            scaled[n * unit : (n + 1) * unit, :] = (values * gain).astype(jnp.bfloat16)
            squares = jnp.sum(values * values, axis=1, keepdims=True)
            first = squares.astype(jnp.bfloat16).astype(jnp.float32)
            second = (squares - first).astype(jnp.bfloat16).astype(jnp.float32)
            third = squares - first - second
            columns = jnp.where(lane == 0, first, jnp.where(lane == 1, second, jnp.where(lane == 2, third, 0.0)))
            at = (n * unit) % rows
            outs[n * unit // rows][at : at + unit, 2 * hidden :] = columns.astype(jnp.bfloat16)

    weights = jnp.concatenate([wg_ref[...], wu_ref[...]], axis=1)
    result = jnp.dot(scaled[...], weights, preferred_element_type=jnp.float32).astype(jnp.bfloat16)
    at_gate = pl.multiple_of(step * 128, 128)
    at_up = pl.multiple_of(hidden + step * 128, 128)
    for n, out in enumerate(outs):
        out[:, pl.ds(at_gate, 128)] = result[n * rows : (n + 1) * rows, :128]
        out[:, pl.ds(at_up, 128)] = result[n * rows : (n + 1) * rows, 128:]


def gate_up(order, x, gain, w_gate, w_up, blocks):
    rows, width = x.shape
    hidden = w_gate.shape[1]
    out = jax.ShapeDtypeStruct((rows // blocks, 2 * hidden + 128), jnp.bfloat16)
    return pl.pallas_call(
        gate_up_kernel,
        out_shape=[out] * blocks,
        grid_spec=pltpu.PrefetchScalarGridSpec(
            num_scalar_prefetch=1,
            grid=(hidden // 128,),
            in_specs=[
                pl.BlockSpec((rows, width), lambda n, o: (0, 0)),
                pl.BlockSpec((1, width), lambda n, o: (0, 0)),
                pl.BlockSpec((width, 128), lambda n, o: (0, n)),
                pl.BlockSpec((width, 128), lambda n, o: (0, n)),
            ],
            out_specs=[pl.BlockSpec(out.shape, lambda n, o: (0, 0))] * blocks,
            scratch_shapes=[pltpu.VMEM((rows, width), jnp.bfloat16)],
        ),
        compiler_params=pltpu.CompilerParams(
            dimension_semantics=("arbitrary",), vmem_limit_bytes=LIMIT
        ),
        cost_estimate=pl.CostEstimate(
            flops=4 * rows * width * hidden, transcendentals=0, bytes_accessed=4 * width * hidden + 4 * rows * hidden
        ),
    )(order, x, gain, w_gate, w_up)


def down_kernel(order, *refs):
    pieces, w_ref, out_ref, hidden = refs[:-3], refs[-3], refs[-2], refs[-1]
    unit = hidden.shape[0] // 8

    @pl.when(pl.program_id(0) == 0)
    def _():
        per = pieces[0].shape[0] // unit
        for n in range(8):
            start = pl.multiple_of(order[n] * unit, unit)
            at = (n % per) * unit
            hidden[pl.ds(start, unit), :] = pieces[n // per][at : at + unit, :]

    out_ref[...] = jnp.dot(hidden[...], w_ref[...], preferred_element_type=jnp.float32).astype(jnp.bfloat16)


def down(order, pieces, w_down):
    rows = sum(piece.shape[0] for piece in pieces)
    inner, width = w_down.shape
    tile = 256
    return pl.pallas_call(
        down_kernel,
        out_shape=jax.ShapeDtypeStruct((rows, width), jnp.bfloat16),
        grid_spec=pltpu.PrefetchScalarGridSpec(
            num_scalar_prefetch=1,
            grid=(width // tile,),
            in_specs=[pl.BlockSpec(piece.shape, lambda n, o: (0, 0)) for piece in pieces]
            + [pl.BlockSpec((inner, tile), lambda n, o: (0, n))],
            out_specs=pl.BlockSpec((rows, tile), lambda n, o: (0, n)),
            scratch_shapes=[pltpu.VMEM((rows, inner), jnp.bfloat16)],
        ),
        compiler_params=pltpu.CompilerParams(
            dimension_semantics=("arbitrary",), vmem_limit_bytes=LIMIT
        ),
        cost_estimate=pl.CostEstimate(
            flops=2 * rows * inner * width, transcendentals=0, bytes_accessed=2 * width * (inner + rows)
        ),
    )(order, *pieces, w_down)


def qkv_kernel(mine_ref, other_ref, src_ref, dst_ref, w_ref, *refs):
    outs, ordered = refs[:-1], refs[-1]
    half = mine_ref.shape[0]
    part = pl.program_id(0)

    @pl.when(part == 0)
    def _():
        pick = jnp.where(dst_ref[...] == src_ref[...], 1.0, 0.0).astype(jnp.bfloat16)
        rows = jnp.dot(pick[:, :half], mine_ref[...], preferred_element_type=jnp.float32)
        rows = rows + jnp.dot(pick[:, half:], other_ref[...], preferred_element_type=jnp.float32)
        ordered[...] = rows.astype(jnp.bfloat16)

    result = jnp.dot(ordered[...], w_ref[0], preferred_element_type=jnp.float32).astype(jnp.bfloat16)
    block, wide = outs[0].shape[0], w_ref.shape[2]
    at = pl.multiple_of(part * wide, wide)
    for n, out in enumerate(outs):
        out[:, pl.ds(at, wide)] = result[n * block : (n + 1) * block, :]


def slot_qkv(mine, other, key_src, key_dst, w_parts, blocks):
    half, width = mine.shape
    rows = 2 * half
    parts, _, wide = w_parts.shape
    out = jax.ShapeDtypeStruct((rows // blocks, parts * wide), jnp.bfloat16)
    return pl.pallas_call(
        qkv_kernel,
        out_shape=[out] * blocks,
        grid_spec=pltpu.PrefetchScalarGridSpec(
            num_scalar_prefetch=0,
            grid=(parts,),
            in_specs=[
                pl.BlockSpec((half, width), lambda n: (0, 0)),
                pl.BlockSpec((half, width), lambda n: (0, 0)),
                pl.BlockSpec((1, rows), lambda n: (0, 0)),
                pl.BlockSpec((rows, 1), lambda n: (0, 0)),
                pl.BlockSpec((1, width, wide), lambda n: (n, 0, 0)),
            ],
            out_specs=[pl.BlockSpec(out.shape, lambda n: (0, 0))] * blocks,
            scratch_shapes=[pltpu.VMEM((rows, width), jnp.bfloat16)],
        ),
        compiler_params=pltpu.CompilerParams(
            dimension_semantics=("arbitrary",), vmem_limit_bytes=LIMIT
        ),
        cost_estimate=pl.CostEstimate(
            flops=2 * rows * width * (parts * wide + rows),
            transcendentals=0,
            bytes_accessed=2 * width * (parts * wide + rows),
        ),
    )(mine, other, key_src, key_dst, w_parts)


def per_device(
    states,
    norm_gain,
    w_gate,
    w_up,
    w_down,
    w_qkv,
    w_class,
    cache_keys,
    cache_values,
    cache_lengths,
    row_slots,
):
    steps = states.shape[0]
    local_rows = states.shape[1]
    width = states.shape[2]
    hidden_here = w_gate.shape[1]
    owner_rows = cache_keys.shape[0]
    history = cache_keys.shape[1]
    local_width = w_qkv.shape[2]
    heads_here = local_width // HEAD_DIM
    total_rows = row_slots.shape[0]
    rows = steps * total_rows
    per = steps * local_rows
    block = rows // 8
    unit = block // 2
    tx = lax.axis_index("tx")
    ty = lax.axis_index("ty")
    my_y, my_zh = tx % 4, tx // 4
    my_x, my_zl, my_c = ty // 4, (ty // 2) % 2, ty % 2

    def to(dy, dz):
        return (my_zh ^ dz) * 4 + (my_y + dy) % 4

    def source(dy, dz):
        return (my_zh ^ dz) * 4 + (my_y - dy + 4) % 4

    y_major = [(dy, dz) for dy in range(4) for dz in range(2)]
    z_major = [(dy, dz) for dz in range(2) for dy in range(4)]
    send_a = jnp.stack([to(*m) for m in y_major])
    send_b = jnp.stack([to(*m) for m in z_major])
    from_a = jnp.stack([source(*m) for m in y_major])
    from_b = jnp.stack([source(*m) for m in z_major])

    pos = jnp.arange(rows, dtype=jnp.int32)
    chunk = pos // per
    dc, dzl, dx = chunk // 8, (chunk // 4) % 2, chunk % 4
    source_ty = ((my_x - dx + 4) % 4) * 4 + (my_zl ^ dzl) * 2 + (my_c ^ dc)
    row_of = source_ty * local_rows + pos % local_rows
    hit = row_of[:, None] == jnp.arange(total_rows, dtype=jnp.int32)[None, :]
    slot_of = jnp.sum(jnp.where(hit, row_slots[None, :], 0), axis=1)
    key_src = (((pos % per) // local_rows) * total_rows + slot_of)[None, :]
    target = jnp.zeros((rows,), jnp.int32)
    for n, move in enumerate(MOVES):
        target = jnp.where(pos // block == n, to(*move), target)
    key_dst = (((pos % block) // owner_rows) * total_rows + target * owner_rows + pos % owner_rows)[:, None]

    own = states.reshape(per, width)
    gain = norm_gain[None, :]
    mine, other = gather_ty(own)
    part_a = gate_up(send_a, mine, gain, w_gate, w_up, 4)
    part_b = gate_up(send_b, other, gain, w_gate, w_up, 2)
    sum_a = total([part_a[0]] + [tx_move(part_a[dy], dy, 0) for dy in range(1, 4)])
    sum_b = total([part_b[0], tx_move(part_b[1], 0, 1)])
    sum_a = sum_a[:unit] + f32(tx_move(sum_a[unit:].astype(jnp.bfloat16), 0, 1))
    sum_b = sum_b[:unit] + total(
        [tx_move(sum_b[dy * unit : (dy + 1) * unit].astype(jnp.bfloat16), dy, 0) for dy in range(1, 4)]
    )

    def activate(summed):
        sq = summed[:, 2 * hidden_here :]
        scale = lax.rsqrt((sq[:, 0:1] + sq[:, 1:2] + sq[:, 2:3]) / D + 1e-05) * UP
        gate = summed[:, :hidden_here] * scale
        up = summed[:, hidden_here : 2 * hidden_here] * scale
        return (jax.nn.silu(gate) * up).astype(jnp.bfloat16)

    hidden_a = activate(sum_a)
    hidden_b = activate(sum_b)
    pair_a = jnp.concatenate([hidden_a, tx_move(hidden_a, 0, 1)], axis=0)
    line_b = jnp.concatenate([hidden_b] + [tx_move(hidden_b, dy, 0) for dy in range(1, 4)], axis=0)
    pieces_a = [pair_a] + [tx_move(pair_a, dy, 0) for dy in range(1, 4)]
    pieces_b = [line_b, tx_move(line_b, 0, 1)]
    mixed_b = down(from_b, pieces_b, w_down)
    mixed_a = down(from_a, pieces_a, w_down)
    pair = ty_move(mixed_b, 0, 0, 1)
    chip = (f32(mixed_a) + f32(pair)).astype(jnp.bfloat16)
    parts = []
    for n, (dx, dz) in enumerate(MOVES):
        piece = chip[n * per : (n + 1) * per]
        parts.append(piece if n == 0 else ty_move(piece, (4 - dx) % 4, dz, 0))
    stream = (f32(own) + total(parts)).astype(jnp.bfloat16)
    stream_out = stream.reshape(steps, local_rows, width)

    mine, other = gather_ty(stream)
    qkv = slot_qkv(mine, other, key_src, key_dst, jnp.transpose(w_qkv, (1, 0, 2)), 8)
    received = [piece if n == 0 else tx_move(piece, *MOVES[n]) for n, piece in enumerate(qkv)]
    triple = total(received).astype(jnp.bfloat16).reshape(steps, owner_rows, 3, heads_here, HEAD_DIM)
    query, new_keys, new_vals = triple[:, :, 0], triple[:, :, 1], triple[:, :, 2]
    keys_h = cache_keys.reshape(owner_rows, history, heads_here, HEAD_DIM)
    vals_h = cache_values.reshape(owner_rows, history, heads_here, HEAD_DIM)
    old = jnp.einsum("tshd,slhd->tshl", query, keys_h, preferred_element_type=jnp.float32)
    new = jnp.einsum("tshd,ushd->tshu", query, new_keys, preferred_element_type=jnp.float32)
    old = old * HEAD_DIM ** (-0.5)
    new = new * HEAD_DIM ** (-0.5)
    where_pos = jnp.arange(history, dtype=jnp.int32)
    old = jnp.where((where_pos[None, :] < cache_lengths[:, None])[None, :, None, :], old, jnp.float32(-1e30))
    causal = jnp.arange(steps)[:, None] >= jnp.arange(steps)[None, :]
    new = jnp.where(causal[:, None, None, :], new, jnp.float32(-1e30))
    top = jnp.maximum(jnp.max(old, axis=3, keepdims=True), jnp.max(new, axis=3, keepdims=True))
    old = jnp.exp(old - top)
    new = jnp.exp(new - top)
    denom = jnp.sum(old, axis=3, keepdims=True) + jnp.sum(new, axis=3, keepdims=True)
    old = (old / denom).astype(jnp.bfloat16)
    new = (new / denom).astype(jnp.bfloat16)
    attended = jnp.einsum("tshl,slhd->tshd", old, vals_h, preferred_element_type=jnp.float32)
    attended = attended + jnp.einsum("tshu,ushd->tshd", new, new_vals, preferred_element_type=jnp.float32)
    attended = attended.reshape(steps * owner_rows, local_width).astype(jnp.bfloat16)
    part = jnp.einsum("rf,fk->kr", attended, w_class, preferred_element_type=jnp.float32)
    classes = part.shape[0]
    packed = jnp.concatenate([part[: classes // 2], part[classes // 2 :]], axis=1)
    packed = jnp.pad(packed, ((0, 1), (0, 0)))
    spread = lax.all_to_all(jnp.broadcast_to(packed[None], (128,) + packed.shape), ("tx", "ty"), 0, 0)
    by_tx = jnp.sum(spread.reshape(8, 16, 8, 128), axis=1)[:, : classes // 2]
    by_tx = by_tx.reshape(8, classes // 2, 2, steps, owner_rows)
    by_slot = by_tx.transpose(2, 1, 3, 0, 4).reshape(classes * steps, total_rows)
    pick = (jnp.arange(total_rows)[:, None] == row_slots[None, :]).astype(jnp.float32)
    logits = jnp.dot(by_slot, pick, precision=lax.Precision.HIGHEST, preferred_element_type=jnp.float32)
    category_logits = logits.reshape(classes, steps, total_rows).transpose(1, 2, 0)
    return (stream_out, category_logits)


def solution(mesh):
    return jax.shard_map(
        per_device,
        mesh=mesh,
        in_specs=(
            P(None, "ty", "tx"),
            P("tx"),
            P("tx", "ty"),
            P("tx", "ty"),
            P("ty", "tx"),
            P("tx", None, "ty"),
            P("ty", None),
            P("tx", None, "ty"),
            P("tx", None, "ty"),
            P("tx"),
            P(),
        ),
        out_specs=(P(None, "ty", "tx"), P()),
        check_vma=False,
    )
```

time: 644 us -> 255 us (0.40); the launches traced: 634 us -> 254 us
  waiting for transfers between devices: 361 us -> 87 us
  blocking collectives: 182 us -> 20.7 us
  starting transfers between devices: 0.43 us -> 81.6 us
  matrix products: 46.8 us -> 3.15 us
  Pallas kernels: 0 us -> 33.1 us
  between operations: 14.4 us -> 1.17 us
    psum x1 -> x0, waiting for transfers between devices: 157 us -> none  [per_device(): lax.psum((jnp.dot(normed_step, w_gate, preferred_element_type=jnp.float32...]
    psum x3 -> x0, blocking collectives: 154 us -> none  [the longest x1 71.5 us: per_device(): lax.psum(jnp.dot(ordered, qkv_weight, preferred_element_type=jnp.float32)...]
    reduce_scatter x2 -> x0, waiting for transfers between devices: 114 us -> none  [per_device(): lax.psum_scatter(down_term(jnp.int32(0), local_rows * lax.axis_size('ty')...]
    all_gather x3 -> x0, waiting for transfers between devices: 90 us -> none  [the longest x2 55.1 us: per_device(): stream_all = lax.all_gather(stream, 'ty', axis=0, tiled=True)]
    ppermute x0 -> x47, waiting for transfers between devices: none -> 87 us  [the longest x23 65.4 us: tx_move(): return lax.ppermute(array, 'tx', pairs)]
    ppermute x0 -> x47, starting transfers between devices: none -> 81.6 us  [the longest x24 42.2 us: ty_move(): return lax.ppermute(array, 'ty', pairs)]
    dot_general x14 -> x6, matrix products: 46.8 us -> 3.15 us  [the longest x1 1.98 us: per_device(): jnp.einsum('tshd,slhd->tshl', query, keys_h, preferred_element_type=jnp.f...]
    pallas_call x0 -> x5, Pallas kernels: none -> 33.1 us  [the longest x2 19.5 us: gate_up(): pl.pallas_call(gate_up_kernel, out_shape=[out] * blocks, grid_spec=pltpu....]
  transfers between devices with their start and end apart: 6 -> 47, of which waited for: 6 -> 22; matrix products, arithmetic and copies ran while one was open for 3% -> 1% of each run, Pallas kernels for 0% -> 6%
where the time goes in v1:
time: 255 us; the launch traced here: 254 us
  waiting for transfers between devices  87 us (34%)
  starting transfers between devices  81.6 us (32%)
  Pallas kernels  33.1 us (13%)
  local copies, waits for them, and re-layouts  21.7 us (9%)
  blocking collectives  20.7 us (8%)
  other arithmetic  5.85 us (2%)
  matrix products  3.15 us (1%)
    ppermute x23, waiting for transfers between devices, tx_move(): return lax.ppermute(array, 'tx', pairs)  65.4 us
    ppermute x24, starting transfers between devices, ty_move(): return lax.ppermute(array, 'ty', pairs)  42.2 us
    ppermute x23, starting transfers between devices, tx_move(): return lax.ppermute(array, 'tx', pairs)  39.4 us
    ppermute x24, waiting for transfers between devices, ty_move(): return lax.ppermute(array, 'ty', pairs)  21.6 us
    all_to_all x1, blocking collectives, per_device(): lax.all_to_all(jnp.broadcast_to(packed[None], (128,) + packed.shape), ('t...  20.7 us
    unnamed x48, local copies, waits for them, and re-layouts  20.2 us
    pallas_call x2, Pallas kernels, gate_up(): pl.pallas_call(gate_up_kernel, out_shape=[out] * blocks, grid_spec=pltpu....  19.5 us
    pallas_call x2, Pallas kernels, down(): pl.pallas_call(down_kernel, out_shape=jax.ShapeDtypeStruct((rows, width),...  10.1 us
  transfers between devices with their start and end apart: 47, of which 22 were waited for; matrix products, arithmetic and copies ran while one was open for 1% of the time, Pallas kernels for 6%

profile of v1, /device:TPU:1, one launch (start us, length us, event | category | flops | bytes accessed | tf_op | source)
XLA Modules:
  0.0 254.3 jit_solution(10712795598243069739)
XLA Ops:
  15.1 4.3 %collective-permute-done.5 = bf16[32,2048]{1,0:T(8,128)(2,1)S(1)} collective-permute-done((bf16[32,2048]{1,0:T(8,128)(2,1)}, bf16[32,2048]{1,0:T(8,128)(2,1)S(1)}, u32[]{:S(2)}, u32[]{:S(2)}) %collective-permute-start.5) | collective-permute-done | bytes 131104 | tf_op jit(solution)/shard_map/ppermute | solution.py:30
  19.4 3.5 %collective-permute-start.15 = (bf16[256,2048]{1,0:T(8,128)(2,1)S(1)}, bf16[256,2048]{1,0:T(8,128)(2,1)S(1)}, u32[]{:S(2)}, u32[]{:S(2)}) collective-permute-start(bf16[256,2048]{1,0:T(8,128)(2,1)S(1)} %constant_dynamic-update-slice_fusion.x_ref), channel_id=1, source_target_pairs={{0,1},{1,0},{2,3},{3,2},{4,5},{5,4},{6,7},{7,6},{8,9},{9,8},{10,11... | collective-permute-start | bytes 3145736 | tf_op jit(solution)/shard_map/ppermute | solution.py:30
  25.1 2.9 %copy-done.2 = bf16[2048,1664]{1,0:T(8,128)(2,1)S(1)} copy-done((bf16[2048,1664]{1,0:T(8,128)(2,1)S(1)}, bf16[2048,1664]{1,0:T(8,128)(2,1)}, u32[]{:S(2)}) %copy-start.2) | copy-done | bytes 6815768
  28.1 2.9 %copy-done.4 = bf16[2048,1664]{1,0:T(8,128)(2,1)S(1)} copy-done((bf16[2048,1664]{1,0:T(8,128)(2,1)S(1)}, bf16[2048,1664]{1,0:T(8,128)(2,1)}, u32[]{:S(2)}) %copy-start.4) | copy-done | bytes 6815768
  31.0 10.2 %shard_map.124 = (bf16[128,3456]{1,0:T(8,128)(2,1)S(1)}, bf16[128,3456]{1,0:T(8,128)(2,1)}) custom-call(s32[8]{0:T(128)S(1)} %stack.77.order, bf16[256,2048]{1,0:T(8,128)(2,1)S(1)} %collective-permute-done.15.x_ref, bf16[1,2048]{1,0:T(2,128)(2,1)S(1)} %broadcast_in_dim.87.gain_ref, bf16[2048,1664]{1,0:T(8,128)(2,1)S(1)} %copy-done.2, ...), custom_call_target="tpu_custom_call" | custom-call | flops 3489660928 | bytes 15335424 | tf_op jit(solution)/shard_map/pallas_call | solution.py:86
  42.2 3.3 %collective-permute-start.16 = (bf16[128,3456]{1,0:T(8,128)(2,1)}, bf16[128,3456]{1,0:T(8,128)(2,1)S(1)}, u32[]{:S(2)}, u32[]{:S(2)}) collective-permute-start(bf16[128,3456]{1,0:T(8,128)(2,1)} %get-tuple-element.21), channel_id=1, source_target_pairs={{0,64},{16,80},{32,96},{48,112},{64,0},{80,16},{96,32},{112,48},{1... | collective-permute-start | bytes 2654216 | tf_op jit(solution)/shard_map/ppermute | solution.py:20
  45.6 19.8 %collective-permute-done.16 = bf16[128,3456]{1,0:T(8,128)(2,1)S(1)} collective-permute-done((bf16[128,3456]{1,0:T(8,128)(2,1)}, bf16[128,3456]{1,0:T(8,128)(2,1)S(1)}, u32[]{:S(2)}, u32[]{:S(2)}) %collective-permute-start.16) | collective-permute-done | bytes 884768 | tf_op jit(solution)/shard_map/ppermute | solution.py:20
  69.4 2.6 %collective-permute-start.18 = (bf16[32,3456]{1,0:T(8,128)(2,1)S(1)}, bf16[32,3456]{1,0:T(8,128)(2,1)S(1)}, u32[]{:S(2)}, u32[]{:S(2)}) collective-permute-start(bf16[32,3456]{1,0:T(8,128)(2,1)S(1)} %get-tuple-element.53), channel_id=1, source_target_pairs={{0,32},{16,48},{32,0},{48,16},{64,96},{80,112},{96,64},{112,80},{1... | collective-permute-start | bytes 663560 | tf_op jit(solution)/shard_map/ppermute | solution.py:20
  73.1 2.9 %copy-done.3 = bf16[2048,1664]{1,0:T(8,128)(2,1)S(1)} copy-done((bf16[2048,1664]{1,0:T(8,128)(2,1)S(1)}, bf16[2048,1664]{1,0:T(8,128)(2,1)}, u32[]{:S(2)}) %copy-start.3) | copy-done | bytes 6815768
  76.0 2.9 %copy-done.5 = bf16[2048,1664]{1,0:T(8,128)(2,1)S(1)} copy-done((bf16[2048,1664]{1,0:T(8,128)(2,1)S(1)}, bf16[2048,1664]{1,0:T(8,128)(2,1)}, u32[]{:S(2)}) %copy-start.5) | copy-done | bytes 6815768
  79.0 9.3 %shard_map.122 = (bf16[64,3456]{1,0:T(8,128)(2,1)S(1)}, bf16[64,3456]{1,0:T(8,128)(2,1)S(1)}, bf16[64,3456]{1,0:T(8,128)(2,1)S(1)}, bf16[64,3456]{1,0:T(8,128)(2,1)S(1)}) custom-call(s32[8]{0:T(128)S(1)} %stack.75.order, bf16[256,2048]{1,0:T(8,128)(2,1)S(1)} %constant_dynamic-update-slice_fusion.x_ref, bf16[1,2048]{1,0:T(2,128)(2,1)S(1)} %broadcast_in_dim.87.gain_ref, ...), custom_call_target="tpu_custom_call" | custom-call | flops 3489660928 | bytes 15335424 | tf_op jit(solution)/shard_map/pallas_call | solution.py:86
  94.0 6.5 %collective-permute-done.7 = bf16[64,3456]{1,0:T(8,128)(2,1)S(1)} collective-permute-done((bf16[64,3456]{1,0:T(8,128)(2,1)S(1)}, bf16[64,3456]{1,0:T(8,128)(2,1)S(1)}, u32[]{:S(2)}, u32[]{:S(2)}) %collective-permute-start.7) | collective-permute-done | bytes 442400 | tf_op jit(solution)/shard_map/ppermute | solution.py:20
  100.5 7.4 %collective-permute-done.8 = bf16[64,3456]{1,0:T(8,128)(2,1)S(1)} collective-permute-done((bf16[64,3456]{1,0:T(8,128)(2,1)S(1)}, bf16[64,3456]{1,0:T(8,128)(2,1)S(1)}, u32[]{:S(2)}, u32[]{:S(2)}) %collective-permute-start.8) | collective-permute-done | bytes 442400 | tf_op jit(solution)/shard_map/ppermute | solution.py:20
  107.9 3.6 %collective-permute-done.9 = bf16[64,3456]{1,0:T(8,128)(2,1)S(1)} collective-permute-done((bf16[64,3456]{1,0:T(8,128)(2,1)S(1)}, bf16[64,3456]{1,0:T(8,128)(2,1)S(1)}, u32[]{:S(2)}, u32[]{:S(2)}) %collective-permute-start.9) | collective-permute-done | bytes 442400 | tf_op jit(solution)/shard_map/ppermute | solution.py:20
  111.7 2.7 %collective-permute-start.10 = (bf16[32,3456]{1,0:T(8,128)(2,1)S(1)}, bf16[32,3456]{1,0:T(8,128)(2,1)S(1)}, u32[]{:S(2)}, u32[]{:S(2)}) collective-permute-start(bf16[32,3456]{1,0:T(8,128)(2,1)S(1)} %slice.212), channel_id=1, source_target_pairs={{0,64},{16,80},{32,96},{48,112},{64,0},{80,16},{96,32},{112,48},{1... | collective-permute-start | bytes 663560 | tf_op jit(solution)/shard_map/ppermute | solution.py:20
  118.4 8.4 %collective-permute-done.23.refs_1_ = bf16[128,1664]{1,0:T(8,128)(2,1)S(1)} collective-permute-done((bf16[128,1664]{1,0:T(8,128)(2,1)S(1)}, bf16[128,1664]{1,0:T(8,128)(2,1)S(1)}, u32[]{:S(2)}, u32[]{:S(2)}) %collective-permute-start.23) | collective-permute-done | bytes 426016 | tf_op jit(solution)/shard_map/ppermute | solution.py:20
  126.7 5.1 %shard_map.125 = bf16[256,2048]{1,0:T(8,128)(2,1)S(1)} custom-call(s32[8]{0:T(128)S(1)} %stack.76.order, bf16[128,1664]{1,0:T(8,128)(2,1)S(1)} %pad_maximum_fusion.refs_0_, bf16[128,1664]{1,0:T(8,128)(2,1)S(1)} %collective-permute-done.23.refs_1_, bf16[1664,2048]{1,0:T(8,128)(2,1)S(1)} %bitcast.85), custom_call_target="tpu_custom_call" | custom-call | flops 1744830464 | bytes 7864320 | tf_op jit(solution)/shard_map/pallas_call | solution.py:129
  131.8 4.1 %collective-permute-start.24 = (bf16[256,2048]{1,0:T(8,128)(2,1)S(1)}, bf16[256,2048]{1,0:T(8,128)(2,1)}, u32[]{:S(2)}, u32[]{:S(2)}) collective-permute-start(bf16[256,2048]{1,0:T(8,128)(2,1)S(1)} %shard_map.125), channel_id=1, source_target_pairs={{0,1},{1,0},{2,3},{3,2},{4,5},{5,4},{6,7},{7,6},{8,9},{9,8},{10,11... | collective-permute-start | bytes 3145736 | tf_op jit(solution)/shard_map/ppermute | solution.py:30
  138.3 3.9 %collective-permute-done.11 = bf16[32,1664]{1,0:T(8,128)(2,1)S(1)} collective-permute-done((bf16[32,1664]{1,0:T(8,128)(2,1)S(1)}, bf16[32,1664]{1,0:T(8,128)(2,1)S(1)}, u32[]{:S(2)}, u32[]{:S(2)}) %collective-permute-start.11) | collective-permute-done | bytes 106528 | tf_op jit(solution)/shard_map/ppermute | solution.py:20
  146.8 3.5 %collective-permute-done.12.refs_1_ = bf16[64,1664]{1,0:T(8,128)(2,1)S(1)} collective-permute-done((bf16[64,1664]{1,0:T(8,128)(2,1)S(1)}, bf16[64,1664]{1,0:T(8,128)(2,1)S(1)}, u32[]{:S(2)}, u32[]{:S(2)}) %collective-permute-start.12) | collective-permute-done | bytes 213024 | tf_op jit(solution)/shard_map/ppermute | solution.py:20
  150.3 5.4 %collective-permute-done.13.refs_2_ = bf16[64,1664]{1,0:T(8,128)(2,1)S(1)} collective-permute-done((bf16[64,1664]{1,0:T(8,128)(2,1)S(1)}, bf16[64,1664]{1,0:T(8,128)(2,1)S(1)}, u32[]{:S(2)}, u32[]{:S(2)}) %collective-permute-start.13) | collective-permute-done | bytes 213024 | tf_op jit(solution)/shard_map/ppermute | solution.py:20
  155.7 2.9 %copy-done.1 = bf16[1664,2048]{1,0:T(8,128)(2,1)S(1)} copy-done((bf16[1664,2048]{1,0:T(8,128)(2,1)S(1)}, bf16[1664,2048]{1,0:T(8,128)(2,1)}, u32[]{:S(2)}) %copy-start.1) | copy-done | bytes 6815768
  158.6 5.1 %shard_map.123 = bf16[256,2048]{1,0:T(8,128)(2,1)S(1)} custom-call(s32[8]{0:T(128)S(1)} %stack.72.order, bf16[64,1664]{1,0:T(8,128)(2,1)S(1)} %pad_maximum_fusion.1.refs_0_, bf16[64,1664]{1,0:T(8,128)(2,1)S(1)} %collective-permute-done.12.refs_1_, bf16[64,1664]{1,0:T(8,128)(2,1)S(1)} %collective-permute-done.13.refs_2_, ...), custom_call_target="tpu_custom_call" | custom-call | flops 1744830464 | bytes 7864320 | tf_op jit(solution)/shard_map/pallas_call | solution.py:129
  167.0 3.6 %collective-permute-start.29 = (bf16[32,2048]{1,0:T(8,128)(2,1)S(1)}, bf16[32,2048]{1,0:T(8,128)(2,1)S(1)}, u32[]{:S(2)}, u32[]{:S(2)}) collective-permute-start(bf16[32,2048]{1,0:T(8,128)(2,1)S(1)} %get-tuple-element.47), channel_id=1, source_target_pairs={{0,14},{1,15},{2,12},{3,13},{4,2},{5,3},{6,0},{7,1},{8,6},{9,7},{1... | collective-permute-start | bytes 393224 | tf_op jit(solution)/shard_map/ppermute | solution.py:30
  174.1 3.6 %collective-permute-done.30 = bf16[32,2048]{1,0:T(8,128)(2,1)S(1)} collective-permute-done((bf16[32,2048]{1,0:T(8,128)(2,1)S(1)}, bf16[32,2048]{1,0:T(8,128)(2,1)S(1)}, u32[]{:S(2)}, u32[]{:S(2)}) %collective-permute-start.30) | collective-permute-done | bytes 131104 | tf_op jit(solution)/shard_map/ppermute | solution.py:30
  189.2 4.6 %collective-permute-done.36 = bf16[32,2048]{1,0:T(8,128)(2,1)S(1)} collective-permute-done((bf16[32,2048]{1,0:T(8,128)(2,1)S(1)}, bf16[32,2048]{1,0:T(8,128)(2,1)S(1)}, u32[]{:S(2)}, u32[]{:S(2)}) %collective-permute-start.36) | collective-permute-done | bytes 131104 | tf_op jit(solution)/shard_map/ppermute | solution.py:30
  194.6 5.8 %collective-permute-start.39 = (bf16[256,2048]{1,0:T(8,128)(2,1)S(1)}, bf16[256,2048]{1,0:T(8,128)(2,1)S(1)}, u32[]{:S(2)}, u32[]{:S(2)}) collective-permute-start(bf16[256,2048]{1,0:T(8,128)(2,1)S(1)} %constant_dynamic-update-slice_fusion.8.mine_ref), channel_id=1, source_target_pairs={{0,1},{1,0},{2,3},{3,2},{4,5},{5,4},{6,7},{7,6},{8,9},{9,8},{10,11... | collective-permute-start | bytes 3145736 | tf_op jit(solution)/shard_map/ppermute | solution.py:30
  204.6 3.5 %shard_map.126 = (bf16[64,768]{1,0:T(8,128)(2,1)S(1)}, bf16[64,768]{1,0:T(8,128)(2,1)S(1)}, bf16[64,768]{1,0:T(8,128)(2,1)S(1)}, bf16[64,768]{1,0:T(8,128)(2,1)S...) custom-call(bf16[256,2048]{1,0:T(8,128)(2,1)S(1)} %constant_dynamic-, ...), custom_call_target="tpu_custom_call" | custom-call | flops 2684354560 | bytes 5242880 | tf_op jit(solution)/shard_map/pallas_call | solution.py:173
  208.1 2.7 %collective-permute-start.40 = (bf16[64,768]{1,0:T(8,128)(2,1)S(1)}, bf16[64,768]{1,0:T(8,128)(2,1)S(1)}, u32[]{:S(2)}, u32[]{:S(2)}) collective-permute-start(bf16[64,768]{1,0:T(8,128)(2,1)S(1)} %get-tuple-element.23), channel_id=1, source_target_pairs={{0,16},{16,32},{32,48},{48,0},{64,80},{80,96},{96,112},{112,64},{1... | collective-permute-start | bytes 294920 | tf_op jit(solution)/shard_map/ppermute | solution.py:20
  213.3 3.1 %collective-permute-start.43 = (bf16[64,768]{1,0:T(8,128)(2,1)S(1)}, bf16[64,768]{1,0:T(8,128)(2,1)S(1)}, u32[]{:S(2)}, u32[]{:S(2)}) collective-permute-start(bf16[64,768]{1,0:T(8,128)(2,1)S(1)} %get-tuple-element.26), channel_id=1, source_target_pairs={{0,64},{16,80},{32,96},{48,112},{64,0},{80,16},{96,32},{112,48},{1... | collective-permute-start | bytes 294920 | tf_op jit(solution)/shard_map/ppermute | solution.py:20
  217.5 3.3 %collective-permute-start.45 = (bf16[64,768]{1,0:T(8,128)(2,1)S(1)}, bf16[64,768]{1,0:T(8,128)(2,1)S(1)}, u32[]{:S(2)}, u32[]{:S(2)}) collective-permute-start(bf16[64,768]{1,0:T(8,128)(2,1)S(1)} %get-tuple-element.28), channel_id=1, source_target_pairs={{0,96},{16,112},{32,64},{48,80},{64,32},{80,48},{96,0},{112,16},{1... | collective-permute-start | bytes 294920 | tf_op jit(solution)/shard_map/ppermute | solution.py:20
  232.5 20.7 %all_to_all.5 = f32[128,8,128]{2,1,0:T(8,128)S(1)} all-to-all(f32[128,8,128]{2,1,0:T(8,128)S(1)} %broadcast_in_dim.102), channel_id=1, replica_groups=mesh['tx'=8,'ty'=16] {'tx','ty'}, dimensions={0} | all-to-all | bytes 1048576 | tf_op jit(solution)/shard_map/all_to_all | solution.py:321
  (176 shorter events, 79.3 us)
Async XLA Ops:
  0.7 8.3 %collective-permute-start = (bf16[32,2048]{1,0:T(8,128)(2,1)}, bf16[32,2048]{1,0:T(8,128)(2,1)S(1)}, u32[]{:S(2)}, u32[]{:S(2)}) collective-permute-start(bf16[32,2048]{1,0:T(8,128)(2,1)} %bitcast.87), channel_id=1, source_target_pairs={{0,4},{1,5},{2,6},{3,7},{4,8},{5,9},{6,10},{7,11},{8,12},{9,13},{1... | collective-permute-start | bytes 393224 | tf_op jit(solution)/shard_map/ppermute | solution.py:30
  2.8 8.4 %collective-permute-start.1 = (bf16[32,2048]{1,0:T(8,128)(2,1)}, bf16[32,2048]{1,0:T(8,128)(2,1)S(1)}, u32[]{:S(2)}, u32[]{:S(2)}) collective-permute-start(bf16[32,2048]{1,0:T(8,128)(2,1)} %bitcast.88), channel_id=1, source_target_pairs={{0,8},{1,9},{2,10},{3,11},{4,12},{5,13},{6,14},{7,15},{8,0},{9,1},... | collective-permute-start | bytes 393224 | tf_op jit(solution)/shard_map/ppermute | solution.py:30
  5.2 7.6 %collective-permute-start.2 = (bf16[32,2048]{1,0:T(8,128)(2,1)}, bf16[32,2048]{1,0:T(8,128)(2,1)S(1)}, u32[]{:S(2)}, u32[]{:S(2)}) collective-permute-start(bf16[32,2048]{1,0:T(8,128)(2,1)} %bitcast.89), channel_id=1, source_target_pairs={{0,12},{1,13},{2,14},{3,15},{4,0},{5,1},{6,2},{7,3},{8,4},{9,5},{1... | collective-permute-start | bytes 393224 | tf_op jit(solution)/shard_map/ppermute | solution.py:30
  9.0 10.3 %collective-permute-start.5 = (bf16[32,2048]{1,0:T(8,128)(2,1)}, bf16[32,2048]{1,0:T(8,128)(2,1)S(1)}, u32[]{:S(2)}, u32[]{:S(2)}) collective-permute-start(bf16[32,2048]{1,0:T(8,128)(2,1)} %bitcast.93), channel_id=1, source_target_pairs={{0,10},{1,11},{2,8},{3,9},{4,14},{5,15},{6,12},{7,13},{8,2},{9,3},... | collective-permute-start | bytes 393224 | tf_op jit(solution)/shard_map/ppermute | solution.py:30
  11.2 8.2 %collective-permute-start.6 = (bf16[32,2048]{1,0:T(8,128)(2,1)}, bf16[32,2048]{1,0:T(8,128)(2,1)S(1)}, u32[]{:S(2)}, u32[]{:S(2)}) collective-permute-start(bf16[32,2048]{1,0:T(8,128)(2,1)} %bitcast.94), channel_id=1, source_target_pairs={{0,14},{1,15},{2,12},{3,13},{4,2},{5,3},{6,0},{7,1},{8,6},{9,7},{1... | collective-permute-start | bytes 393224 | tf_op jit(solution)/shard_map/ppermute | solution.py:30
  42.2 23.2 %collective-permute-start.16 = (bf16[128,3456]{1,0:T(8,128)(2,1)}, bf16[128,3456]{1,0:T(8,128)(2,1)S(1)}, u32[]{:S(2)}, u32[]{:S(2)}) collective-permute-start(bf16[128,3456]{1,0:T(8,128)(2,1)} %get-tuple-element.21), channel_id=1, source_target_pairs={{0,64},{16,80},{32,96},{48,112},{64,0},{80,16},{96,32},{112,48},{1... | collective-permute-start | bytes 2654216 | tf_op jit(solution)/shard_map/ppermute | solution.py:20
  68.0 21.6 %collective-permute-start.17 = (bf16[32,3456]{1,0:T(8,128)(2,1)S(1)}, bf16[32,3456]{1,0:T(8,128)(2,1)S(1)}, u32[]{:S(2)}, u32[]{:S(2)}) collective-permute-start(bf16[32,3456]{1,0:T(8,128)(2,1)S(1)} %get-tuple-element.51), channel_id=1, source_target_pairs={{0,16},{16,32},{32,48},{48,0},{64,80},{80,96},{96,112},{112,64},{1... | collective-permute-start | bytes 663560 | tf_op jit(solution)/shard_map/ppermute | solution.py:20
  69.4 21.8 %collective-permute-start.18 = (bf16[32,3456]{1,0:T(8,128)(2,1)S(1)}, bf16[32,3456]{1,0:T(8,128)(2,1)S(1)}, u32[]{:S(2)}, u32[]{:S(2)}) collective-permute-start(bf16[32,3456]{1,0:T(8,128)(2,1)S(1)} %get-tuple-element.53), channel_id=1, source_target_pairs={{0,32},{16,48},{32,0},{48,16},{64,96},{80,112},{96,64},{112,80},{1... | collective-permute-start | bytes 663560 | tf_op jit(solution)/shard_map/ppermute | solution.py:20
  72.0 19.2 %collective-permute-start.19 = (bf16[32,3456]{1,0:T(8,128)(2,1)S(1)}, bf16[32,3456]{1,0:T(8,128)(2,1)S(1)}, u32[]{:S(2)}, u32[]{:S(2)}) collective-permute-start(bf16[32,3456]{1,0:T(8,128)(2,1)S(1)} %get-tuple-element.52), channel_id=1, source_target_pairs={{0,48},{16,0},{32,16},{48,32},{64,112},{80,64},{96,80},{112,96},{1... | collective-permute-start | bytes 663560 | tf_op jit(solution)/shard_map/ppermute | solution.py:20
  88.2 12.3 %collective-permute-start.7 = (bf16[64,3456]{1,0:T(8,128)(2,1)S(1)}, bf16[64,3456]{1,0:T(8,128)(2,1)S(1)}, u32[]{:S(2)}, u32[]{:S(2)}) collective-permute-start(bf16[64,3456]{1,0:T(8,128)(2,1)S(1)} %get-tuple-element.17), channel_id=1, source_target_pairs={{0,16},{16,32},{32,48},{48,0},{64,80},{80,96},{96,112},{112,64},{1... | collective-permute-start | bytes 1327112 | tf_op jit(solution)/shard_map/ppermute | solution.py:20
  88.7 19.2 %collective-permute-start.8 = (bf16[64,3456]{1,0:T(8,128)(2,1)S(1)}, bf16[64,3456]{1,0:T(8,128)(2,1)S(1)}, u32[]{:S(2)}, u32[]{:S(2)}) collective-permute-start(bf16[64,3456]{1,0:T(8,128)(2,1)S(1)} %get-tuple-element.18), channel_id=1, source_target_pairs={{0,32},{16,48},{32,0},{48,16},{64,96},{80,112},{96,64},{112,80},{1... | collective-permute-start | bytes 1327112 | tf_op jit(solution)/shard_map/ppermute | solution.py:20
  89.6 21.8 %collective-permute-start.9 = (bf16[64,3456]{1,0:T(8,128)(2,1)S(1)}, bf16[64,3456]{1,0:T(8,128)(2,1)S(1)}, u32[]{:S(2)}, u32[]{:S(2)}) collective-permute-start(bf16[64,3456]{1,0:T(8,128)(2,1)S(1)} %get-tuple-element.19), channel_id=1, source_target_pairs={{0,48},{16,0},{32,16},{48,32},{64,112},{80,64},{96,80},{112,96},{1... | collective-permute-start | bytes 1327112 | tf_op jit(solution)/shard_map/ppermute | solution.py:20
  91.7 22.8 %collective-permute-start.20 = (bf16[32,1664]{1,0:T(8,128)(2,1)S(1)}, bf16[32,1664]{1,0:T(8,128)(2,1)S(1)}, u32[]{:S(2)}, u32[]{:S(2)}) collective-permute-start(bf16[32,1664]{1,0:T(8,128)(2,1)S(1)} %fusion.31), channel_id=1, source_target_pairs={{0,16},{16,32},{32,48},{48,0},{64,80},{80,96},{96,112},{112,64},{1... | collective-permute-start | bytes 319496 | tf_op jit(solution)/shard_map/ppermute | solution.py:20
  92.1 22.4 %collective-permute-start.21 = (bf16[32,1664]{1,0:T(8,128)(2,1)S(1)}, bf16[32,1664]{1,0:T(8,128)(2,1)S(1)}, u32[]{:S(2)}, u32[]{:S(2)}) collective-permute-start(bf16[32,1664]{1,0:T(8,128)(2,1)S(1)} %fusion.31), channel_id=1, source_target_pairs={{0,32},{16,48},{32,0},{48,16},{64,96},{80,112},{96,64},{112,80},{1... | collective-permute-start | bytes 319496 | tf_op jit(solution)/shard_map/ppermute | solution.py:20
  100.5 14.0 %collective-permute-start.22 = (bf16[32,1664]{1,0:T(8,128)(2,1)S(1)}, bf16[32,1664]{1,0:T(8,128)(2,1)S(1)}, u32[]{:S(2)}, u32[]{:S(2)}) collective-permute-start(bf16[32,1664]{1,0:T(8,128)(2,1)S(1)} %fusion.31), channel_id=1, source_target_pairs={{0,48},{16,0},{32,16},{48,32},{64,112},{80,64},{96,80},{112,96},{1... | collective-permute-start | bytes 319496 | tf_op jit(solution)/shard_map/ppermute | solution.py:20
  114.5 12.2 %collective-permute-start.23 = (bf16[128,1664]{1,0:T(8,128)(2,1)S(1)}, bf16[128,1664]{1,0:T(8,128)(2,1)S(1)}, u32[]{:S(2)}, u32[]{:S(2)}) collective-permute-start(bf16[128,1664]{1,0:T(8,128)(2,1)S(1)} %pad_maximum_fusion.refs_0_), channel_id=1, source_target_pairs={{0,64},{16,80},{32,96},{48,112},{64,0},{80,16},{96,32},{112,48},{1... | collective-permute-start | bytes 1277960 | tf_op jit(solution)/shard_map/ppermute | solution.py:20
  131.8 31.9 %collective-permute-start.24 = (bf16[256,2048]{1,0:T(8,128)(2,1)S(1)}, bf16[256,2048]{1,0:T(8,128)(2,1)}, u32[]{:S(2)}, u32[]{:S(2)}) collective-permute-start(bf16[256,2048]{1,0:T(8,128)(2,1)S(1)} %shard_map.125), channel_id=1, source_target_pairs={{0,1},{1,0},{2,3},{3,2},{4,5},{5,4},{6,7},{7,6},{8,9},{9,8},{10,11... | collective-permute-start | bytes 3145736 | tf_op jit(solution)/shard_map/ppermute | solution.py:30
  142.2 8.0 %collective-permute-start.12 = (bf16[64,1664]{1,0:T(8,128)(2,1)S(1)}, bf16[64,1664]{1,0:T(8,128)(2,1)S(1)}, u32[]{:S(2)}, u32[]{:S(2)}) collective-permute-start(bf16[64,1664]{1,0:T(8,128)(2,1)S(1)} %pad_maximum_fusion.1.refs_0_), channel_id=1, source_target_pairs={{0,16},{16,32},{32,48},{48,0},{64,80},{80,96},{96,112},{112,64},{1... | collective-permute-start | bytes 638984 | tf_op jit(solution)/shard_map/ppermute | solution.py:20
  144.2 11.5 %collective-permute-start.13 = (bf16[64,1664]{1,0:T(8,128)(2,1)S(1)}, bf16[64,1664]{1,0:T(8,128)(2,1)S(1)}, u32[]{:S(2)}, u32[]{:S(2)}) collective-permute-start(bf16[64,1664]{1,0:T(8,128)(2,1)S(1)} %pad_maximum_fusion.1.refs_0_), channel_id=1, source_target_pairs={{0,32},{16,48},{32,0},{48,16},{64,96},{80,112},{96,64},{112,80},{1... | collective-permute-start | bytes 638984 | tf_op jit(solution)/shard_map/ppermute | solution.py:20
  146.6 9.1 %collective-permute-start.14 = (bf16[64,1664]{1,0:T(8,128)(2,1)S(1)}, bf16[64,1664]{1,0:T(8,128)(2,1)S(1)}, u32[]{:S(2)}, u32[]{:S(2)}) collective-permute-start(bf16[64,1664]{1,0:T(8,128)(2,1)S(1)} %pad_maximum_fusion.1.refs_0_), channel_id=1, source_target_pairs={{0,48},{16,0},{32,16},{48,32},{64,112},{80,64},{96,80},{112,96},{1... | collective-permute-start | bytes 638984 | tf_op jit(solution)/shard_map/ppermute | solution.py:20
  167.0 7.1 %collective-permute-start.29 = (bf16[32,2048]{1,0:T(8,128)(2,1)S(1)}, bf16[32,2048]{1,0:T(8,128)(2,1)S(1)}, u32[]{:S(2)}, u32[]{:S(2)}) collective-permute-start(bf16[32,2048]{1,0:T(8,128)(2,1)S(1)} %get-tuple-element.47), channel_id=1, source_target_pairs={{0,14},{1,15},{2,12},{3,13},{4,2},{5,3},{6,0},{7,1},{8,6},{9,7},{1... | collective-permute-start | bytes 393224 | tf_op jit(solution)/shard_map/ppermute | solution.py:30
  171.8 7.4 %collective-permute-start.31 = (bf16[32,2048]{1,0:T(8,128)(2,1)S(1)}, bf16[32,2048]{1,0:T(8,128)(2,1)S(1)}, u32[]{:S(2)}, u32[]{:S(2)}) collective-permute-start(bf16[32,2048]{1,0:T(8,128)(2,1)S(1)} %get-tuple-element.45), channel_id=1, source_target_pairs={{0,6},{1,7},{2,4},{3,5},{4,10},{5,11},{6,8},{7,9},{8,14},{9,15},{1... | collective-permute-start | bytes 393224 | tf_op jit(solution)/shard_map/ppermute | solution.py:30
  184.3 9.5 %collective-permute-start.36 = (bf16[32,2048]{1,0:T(8,128)(2,1)S(1)}, bf16[32,2048]{1,0:T(8,128)(2,1)S(1)}, u32[]{:S(2)}, u32[]{:S(2)}) collective-permute-start(bf16[32,2048]{1,0:T(8,128)(2,1)S(1)} %get-tuple-element.60), channel_id=1, source_target_pairs={{0,6},{1,7},{2,4},{3,5},{4,10},{5,11},{6,8},{7,9},{8,14},{9,15},{1... | collective-permute-start | bytes 393224 | tf_op jit(solution)/shard_map/ppermute | solution.py:30
  185.1 8.7 %collective-permute-start.37 = (bf16[32,2048]{1,0:T(8,128)(2,1)S(1)}, bf16[32,2048]{1,0:T(8,128)(2,1)S(1)}, u32[]{:S(2)}, u32[]{:S(2)}) collective-permute-start(bf16[32,2048]{1,0:T(8,128)(2,1)S(1)} %get-tuple-element.60), channel_id=1, source_target_pairs={{0,10},{1,11},{2,8},{3,9},{4,14},{5,15},{6,12},{7,13},{8,2},{9,3},... | collective-permute-start | bytes 393224 | tf_op jit(solution)/shard_map/ppermute | solution.py:30
  186.8 7.8 %collective-permute-start.38 = (bf16[32,2048]{1,0:T(8,128)(2,1)S(1)}, bf16[32,2048]{1,0:T(8,128)(2,1)S(1)}, u32[]{:S(2)}, u32[]{:S(2)}) collective-permute-start(bf16[32,2048]{1,0:T(8,128)(2,1)S(1)} %get-tuple-element.60), channel_id=1, source_target_pairs={{0,14},{1,15},{2,12},{3,13},{4,2},{5,3},{6,0},{7,1},{8,6},{9,7},{1... | collective-permute-start | bytes 393224 | tf_op jit(solution)/shard_map/ppermute | solution.py:30
  194.6 8.1 %collective-permute-start.39 = (bf16[256,2048]{1,0:T(8,128)(2,1)S(1)}, bf16[256,2048]{1,0:T(8,128)(2,1)S(1)}, u32[]{:S(2)}, u32[]{:S(2)}) collective-permute-start(bf16[256,2048]{1,0:T(8,128)(2,1)S(1)} %constant_dynamic-update-slice_fusion.8.mine_ref), channel_id=1, source_target_pairs={{0,1},{1,0},{2,3},{3,2},{4,5},{5,4},{6,7},{7,6},{8,9},{9,8},{10,11... | collective-permute-start | bytes 3145736 | tf_op jit(solution)/shard_map/ppermute | solution.py:30
  208.1 9.4 %collective-permute-start.40 = (bf16[64,768]{1,0:T(8,128)(2,1)S(1)}, bf16[64,768]{1,0:T(8,128)(2,1)S(1)}, u32[]{:S(2)}, u32[]{:S(2)}) collective-permute-start(bf16[64,768]{1,0:T(8,128)(2,1)S(1)} %get-tuple-element.23), channel_id=1, source_target_pairs={{0,16},{16,32},{32,48},{48,0},{64,80},{80,96},{96,112},{112,64},{1... | collective-permute-start | bytes 294920 | tf_op jit(solution)/shard_map/ppermute | solution.py:20
  210.8 10.0 %collective-permute-start.41 = (bf16[64,768]{1,0:T(8,128)(2,1)S(1)}, bf16[64,768]{1,0:T(8,128)(2,1)S(1)}, u32[]{:S(2)}, u32[]{:S(2)}) collective-permute-start(bf16[64,768]{1,0:T(8,128)(2,1)S(1)} %get-tuple-element.24), channel_id=1, source_target_pairs={{0,32},{16,48},{32,0},{48,16},{64,96},{80,112},{96,64},{112,80},{1... | collective-permute-start | bytes 294920 | tf_op jit(solution)/shard_map/ppermute | solution.py:20
  213.2 9.4 %collective-permute-start.42 = (bf16[64,768]{1,0:T(8,128)(2,1)S(1)}, bf16[64,768]{1,0:T(8,128)(2,1)S(1)}, u32[]{:S(2)}, u32[]{:S(2)}) collective-permute-start(bf16[64,768]{1,0:T(8,128)(2,1)S(1)} %get-tuple-element.25), channel_id=1, source_target_pairs={{0,48},{16,0},{32,16},{48,32},{64,112},{80,64},{96,80},{112,96},{1... | collective-permute-start | bytes 294920 | tf_op jit(solution)/shard_map/ppermute | solution.py:20
  213.3 9.2 %collective-permute-start.43 = (bf16[64,768]{1,0:T(8,128)(2,1)S(1)}, bf16[64,768]{1,0:T(8,128)(2,1)S(1)}, u32[]{:S(2)}, u32[]{:S(2)}) collective-permute-start(bf16[64,768]{1,0:T(8,128)(2,1)S(1)} %get-tuple-element.26), channel_id=1, source_target_pairs={{0,64},{16,80},{32,96},{48,112},{64,0},{80,16},{96,32},{112,48},{1... | collective-permute-start | bytes 294920 | tf_op jit(solution)/shard_map/ppermute | solution.py:20
  217.5 8.5 %collective-permute-start.45 = (bf16[64,768]{1,0:T(8,128)(2,1)S(1)}, bf16[64,768]{1,0:T(8,128)(2,1)S(1)}, u32[]{:S(2)}, u32[]{:S(2)}) collective-permute-start(bf16[64,768]{1,0:T(8,128)(2,1)S(1)} %get-tuple-element.28), channel_id=1, source_target_pairs={{0,96},{16,112},{32,64},{48,80},{64,32},{80,48},{96,0},{112,16},{1... | collective-permute-start | bytes 294920 | tf_op jit(solution)/shard_map/ppermute | solution.py:20
  220.7 7.1 %collective-permute-start.46 = (bf16[64,768]{1,0:T(8,128)(2,1)S(1)}, bf16[64,768]{1,0:T(8,128)(2,1)S(1)}, u32[]{:S(2)}, u32[]{:S(2)}) collective-permute-start(bf16[64,768]{1,0:T(8,128)(2,1)S(1)} %get-tuple-element.29), channel_id=1, source_target_pairs={{0,112},{16,64},{32,80},{48,96},{64,48},{80,0},{96,16},{112,32},{1... | collective-permute-start | bytes 294920 | tf_op jit(solution)/shard_map/ppermute | solution.py:20
  (32 other events, 569.1 us)

commit v2 on v1

v2 whole, which is shorter than its diff:
```python
import functools

import jax
import jax.numpy as jnp
from jax import lax
from jax.experimental import pallas as pl
from jax.experimental.pallas import tpu as pltpu
from jax.sharding import PartitionSpec as P

D = 16384
HEAD_DIM = 128
DOWN = 2.0 ** -24
UP = 2.0 ** 24


def tx_move(array, dy, dz):
    pairs = [(z * 4 + y, (z ^ dz) * 4 + (y + dy) % 4) for z in range(2) for y in range(4)]
    return lax.ppermute(array, "tx", pairs)


def core_swap(array):
    return lax.ppermute(array, "ty", [(n, n ^ 1) for n in range(16)])


def chip_exchange(blocks):
    groups = [[2 * n + c for n in range(8)] for c in range(2)]
    return lax.all_to_all(blocks, "ty", 0, 0, axis_index_groups=groups)


def gather_ty(rows):
    mine = chip_exchange(jnp.broadcast_to(rows[None], (8,) + rows.shape))
    mine = mine.reshape(8 * rows.shape[0], rows.shape[1])
    return mine, core_swap(mine)


def f32(array):
    return array.astype(jnp.float32)


VM = pl.BlockSpec(memory_space=pltpu.VMEM)
ANY = pl.BlockSpec(memory_space=pl.ANY)


def fetch_kernel(source, *refs):
    target, sems = refs[-2:]
    copies = []
    part = source.shape[0] // sems.shape[0]
    for n in range(sems.shape[0]):
        at = pl.ds(n * part, part)
        copies.append(pltpu.make_async_copy(source.at[at], target.at[at], sems.at[n]))
    for copy in copies:
        copy.start()
    for copy in copies:
        copy.wait()


def fetch(array, pieces, *after):
    return pl.pallas_call(
        fetch_kernel,
        out_shape=pltpu.VMEM(array.shape, array.dtype),
        in_specs=[ANY] * (1 + len(after)),
        out_specs=VM,
        scratch_shapes=[pltpu.SemaphoreType.DMA((pieces,))],
        compiler_params=pltpu.CompilerParams(vmem_limit_bytes=2 * 1024 * 1024),
    )(pltpu.with_memory_space_constraint(array, pltpu.HBM), *after)


def scale_rows(order, x_ref, gain_ref, hidden, outs, scaled):
    rows = outs[0].shape[0]
    unit = x_ref.shape[0] // 8
    gain = gain_ref[...].astype(jnp.float32) * DOWN
    lane = lax.broadcasted_iota(jnp.int32, (unit, 128), 1)
    for n in range(8):
        start = pl.multiple_of(order[n] * unit, unit)
        values = x_ref[pl.ds(start, unit), :].astype(jnp.float32)
        scaled[n * unit : (n + 1) * unit, :] = (values * gain).astype(jnp.bfloat16)
        squares = jnp.sum(values * values, axis=1, keepdims=True)
        first = squares.astype(jnp.bfloat16).astype(jnp.float32)
        second = (squares - first).astype(jnp.bfloat16).astype(jnp.float32)
        third = squares - first - second
        columns = jnp.where(lane == 0, first, jnp.where(lane == 1, second, jnp.where(lane == 2, third, 0.0)))
        at = (n * unit) % rows
        outs[n * unit // rows][at : at + unit, 2 * hidden :] = columns.astype(jnp.bfloat16)


def spread(outs, result, start):
    rows = outs[0].shape[0]
    for n, out in enumerate(outs):
        out[:, start : start + result.shape[1]] = result[n * rows : (n + 1) * rows]


def project(scaled, w_ref, outs, base):
    hidden = w_ref.shape[1]
    for start in range(0, hidden, 256):
        stop = min(start + 256, hidden)
        result = jnp.dot(scaled[...], w_ref[:, start:stop], preferred_element_type=jnp.float32)
        spread(outs, result.astype(jnp.bfloat16), base + start)


def load_gate_up_kernel(order, x_ref, gain_ref, wg_hbm, wu_hbm, *refs):
    outs, wg_ref, wu_ref, scaled, half_sum, sems = refs[:-5], *refs[-5:]
    width, hidden = wg_ref.shape
    part = width // 4
    copies = [
        pltpu.make_async_copy(source.at[pl.ds(m * part, part)], target.at[pl.ds(m * part, part)], sems.at[4 * n + m])
        for n, (source, target) in enumerate(((wg_hbm, wg_ref), (wu_hbm, wu_ref)))
        for m in range(4)
    ]
    for copy in copies[:4]:
        copy.start()
    scale_rows(order, x_ref, gain_ref, hidden, outs, scaled)
    for copy in copies[:2]:
        copy.wait()
    for copy in copies[4:]:
        copy.start()
    for start in range(0, hidden, 256):
        stop = min(start + 256, hidden)
        half_sum[:, start:stop] = jnp.dot(
            scaled[:, : 2 * part], wg_ref[: 2 * part, start:stop], preferred_element_type=jnp.float32
        )
    for copy in copies[2:4]:
        copy.wait()
    for start in range(0, hidden, 256):
        stop = min(start + 256, hidden)
        result = half_sum[:, start:stop] + jnp.dot(
            scaled[:, 2 * part :], wg_ref[2 * part :, start:stop], preferred_element_type=jnp.float32
        )
        spread(outs, result.astype(jnp.bfloat16), start)
    for copy in copies[4:]:
        copy.wait()
    project(scaled, wu_ref, outs, hidden)


def gate_up_kernel(order, x_ref, gain_ref, wg_ref, wu_ref, *refs):
    outs, scaled = refs[:-1], refs[-1]
    hidden = wg_ref.shape[1]
    scale_rows(order, x_ref, gain_ref, hidden, outs, scaled)
    project(scaled, wg_ref, outs, 0)
    project(scaled, wu_ref, outs, hidden)


def gate_up(order, x, gain, w_gate, w_up, blocks, load):
    rows, width = x.shape
    hidden = w_gate.shape[1]
    out = jax.ShapeDtypeStruct((rows // blocks, 2 * hidden + 128), jnp.bfloat16)
    scratch = [pltpu.VMEM((rows, width), jnp.bfloat16)]
    held = []
    if load:
        scratch += [pltpu.VMEM((rows, hidden), jnp.float32), pltpu.SemaphoreType.DMA((8,))]
        held = [pltpu.VMEM(w_gate.shape, w_gate.dtype)] * 2
        w_gate = pltpu.with_memory_space_constraint(w_gate, pltpu.HBM)
        w_up = pltpu.with_memory_space_constraint(w_up, pltpu.HBM)
    return pl.pallas_call(
        load_gate_up_kernel if load else gate_up_kernel,
        out_shape=[out] * blocks + held,
        in_specs=[pl.BlockSpec(memory_space=pltpu.SMEM)] + [VM] * 2 + [ANY if load else VM] * 2,
        out_specs=[VM] * (blocks + len(held)),
        scratch_shapes=scratch,
        compiler_params=pltpu.CompilerParams(vmem_limit_bytes=12 * 1024 * 1024),
        cost_estimate=pl.CostEstimate(
            flops=4 * rows * width * hidden, transcendentals=0, bytes_accessed=4 * width * hidden + 4 * rows * hidden
        ),
    )(order, x, gain, w_gate, w_up)


def small_call(kernel, outs, *arrays):
    return pl.pallas_call(
        kernel,
        out_shape=[jax.ShapeDtypeStruct(shape, dtype) for shape, dtype in outs],
        in_specs=[VM] * len(arrays),
        out_specs=[VM] * len(outs),
        compiler_params=pltpu.CompilerParams(vmem_limit_bytes=8 * 1024 * 1024),
    )(*arrays)


def first_sums_kernel(a0, a1, a2, a3, b0, b1, keep_a, go_a, keep_b, go_b1, go_b2, go_b3):
    unit, wide = keep_a.shape
    for start in range(0, wide, 128):
        at = slice(start, start + 128)
        for lo, out in ((0, keep_a), (unit, go_a)):
            rows = slice(lo, lo + unit)
            total = f32(a0[rows, at]) + f32(a1[rows, at]) + f32(a2[rows, at]) + f32(a3[rows, at])
            out[:, at] = total.astype(out.dtype)
        for n, out in enumerate((keep_b, go_b1, go_b2, go_b3)):
            rows = slice(n * unit, (n + 1) * unit)
            out[:, at] = (f32(b0[rows, at]) + f32(b1[rows, at])).astype(out.dtype)


def activate_kernel(keep_a, a1, keep_b, b1, b2, b3, out_a, out_b):
    hidden = out_a.shape[1]
    for keep, others, out in ((keep_a, (a1,), out_a), (keep_b, (b1, b2, b3), out_b)):

        def summed(start):
            at = slice(start, start + 128)
            value = keep[:, at]
            for other in others:
                value = value + f32(other[:, at])
            return value

        squares = jnp.sum(summed(2 * hidden), axis=1, keepdims=True)
        scale = lax.rsqrt(squares / D + 1e-05) * UP
        for start in range(0, hidden, 128):
            gate = summed(start) * scale
            up = summed(hidden + start) * scale
            out[:, start : start + 128] = (gate / (1.0 + jnp.exp(-gate)) * up).astype(jnp.bfloat16)


def stack_kernel(a0, a1, b0, b1, b2, b3, out_a, out_b):
    unit = a0.shape[0]
    for out, parts in ((out_a, (a0, a1)), (out_b, (b0, b1, b2, b3))):
        for n, part in enumerate(parts):
            out[n * unit : (n + 1) * unit, :] = part[...]


def down_kernel(count, order_a, order_b, *refs):
    pieces, w_ref, out_a, out_b, hidden = refs[:-4], *refs[-4:]
    half = hidden.shape[0] // 2
    unit = half // 8
    for base, order, group in ((0, order_a, pieces[:count]), (half, order_b, pieces[count:])):
        per = group[0].shape[0] // unit
        for n in range(8):
            start = pl.multiple_of(order[n] * unit, unit)
            at = (n % per) * unit
            hidden[pl.ds(base + start, unit), :] = group[n // per][at : at + unit, :]
    for start in range(0, w_ref.shape[1], 256):
        result = jnp.dot(hidden[...], w_ref[:, start : start + 256], preferred_element_type=jnp.float32)
        result = result.astype(jnp.bfloat16)
        out_a[:, start : start + 256] = result[:half]
        out_b[:, start : start + 256] = result[half:]


def down(order_a, order_b, pieces_a, pieces_b, w_down):
    rows = sum(piece.shape[0] for piece in pieces_a)
    inner, width = w_down.shape
    pieces = [*pieces_a, *pieces_b]
    return pl.pallas_call(
        functools.partial(down_kernel, len(pieces_a)),
        out_shape=[jax.ShapeDtypeStruct((rows, width), jnp.bfloat16)] * 2,
        in_specs=[pl.BlockSpec(memory_space=pltpu.SMEM)] * 2 + [VM] * (len(pieces) + 1),
        out_specs=[VM] * 2,
        scratch_shapes=[pltpu.VMEM((2 * rows, inner), jnp.bfloat16)],
        compiler_params=pltpu.CompilerParams(vmem_limit_bytes=10 * 1024 * 1024),
    )(order_a, order_b, *pieces, w_down)


def qkv_kernel(mine_ref, other_ref, src_ref, dst_ref, w_ref, out, ordered):
    half = mine_ref.shape[0]
    pick = jnp.where(dst_ref[...] == src_ref[...], 1.0, 0.0).astype(jnp.bfloat16)
    for start in range(0, mine_ref.shape[1], 512):
        at = slice(start, start + 512)
        rows = jnp.dot(pick[:, :half], mine_ref[:, at], preferred_element_type=jnp.float32)
        rows = rows + jnp.dot(pick[:, half:], other_ref[:, at], preferred_element_type=jnp.float32)
        ordered[:, at] = rows.astype(jnp.bfloat16)
    wide = w_ref.shape[2]
    for part in range(w_ref.shape[0]):
        result = jnp.dot(ordered[...], w_ref[part], preferred_element_type=jnp.float32).astype(jnp.bfloat16)
        out[:, part * wide : (part + 1) * wide] = result


def slot_qkv(mine, other, key_src, key_dst, w_parts):
    half, width = mine.shape
    rows = 2 * half
    parts, _, wide = w_parts.shape
    return pl.pallas_call(
        qkv_kernel,
        out_shape=jax.ShapeDtypeStruct((rows, parts * wide), jnp.bfloat16),
        in_specs=[VM] * 5,
        out_specs=VM,
        scratch_shapes=[pltpu.VMEM((rows, width), jnp.bfloat16)],
        compiler_params=pltpu.CompilerParams(vmem_limit_bytes=12 * 1024 * 1024),
        cost_estimate=pl.CostEstimate(
            flops=2 * rows * width * (parts * wide + rows),
            transcendentals=0,
            bytes_accessed=2 * width * (parts * wide + rows),
        ),
    )(mine, other, key_src, key_dst, w_parts)


def per_device(
    states,
    norm_gain,
    w_gate,
    w_up,
    w_down,
    w_qkv,
    w_class,
    cache_keys,
    cache_values,
    cache_lengths,
    row_slots,
):
    steps = states.shape[0]
    local_rows = states.shape[1]
    width = states.shape[2]
    hidden_here = w_gate.shape[1]
    owner_rows = cache_keys.shape[0]
    history = cache_keys.shape[1]
    local_width = w_qkv.shape[2]
    heads_here = local_width // HEAD_DIM
    total_rows = row_slots.shape[0]
    rows = steps * total_rows
    per = steps * local_rows
    block = rows // 8
    unit = block // 2
    tx = lax.axis_index("tx")
    ty = lax.axis_index("ty")
    my_y, my_zh = tx % 4, tx // 4

    def to(dy, dz):
        return (my_zh ^ dz) * 4 + (my_y + dy) % 4

    def source(dy, dz):
        return (my_zh ^ dz) * 4 + (my_y - dy + 4) % 4

    y_major = [(dy, dz) for dy in range(4) for dz in range(2)]
    z_major = [(dy, dz) for dz in range(2) for dy in range(4)]
    send_a = jnp.stack([to(*m) for m in y_major])
    send_b = jnp.stack([to(*m) for m in z_major])
    from_a = jnp.stack([source(*m) for m in y_major])
    from_b = jnp.stack([source(*m) for m in z_major])

    pos = jnp.arange(rows, dtype=jnp.int32)
    chunk = pos // per
    source_ty = 2 * (chunk % 8) + ((ty % 2) ^ (chunk // 8))
    row_of = source_ty * local_rows + pos % local_rows
    hit = row_of[:, None] == jnp.arange(total_rows, dtype=jnp.int32)[None, :]
    slot_of = jnp.sum(jnp.where(hit, row_slots[None, :], 0), axis=1)
    key_src = (((pos % per) // local_rows) * total_rows + slot_of)[None, :]
    key_dst = ((pos % block) // owner_rows) * total_rows + pos // block * owner_rows + pos % owner_rows
    key_dst = key_dst[:, None]

    own = states.reshape(per, width)
    gain = norm_gain[None, :]
    mine, other = gather_ty(own)
    *part_a, w_gate, w_up = gate_up(send_a, mine, gain, w_gate, w_up, 4, True)
    part_b = gate_up(send_b, other, gain, w_gate, w_up, 2, False)
    half_send = (unit, part_a[0].shape[1])
    came_a = [tx_move(part_a[dy], dy, 0) for dy in (2, 1, 3)]
    came_b = tx_move(part_b[1], 0, 1)
    keep_a, go_a, keep_b, *go_b = small_call(
        first_sums_kernel,
        [(half_send, jnp.float32), (half_send, jnp.bfloat16), (half_send, jnp.float32)] + [(half_send, jnp.bfloat16)] * 3,
        part_a[0], *came_a, part_b[0], came_b,
    )
    came_b = [tx_move(go_b[dy - 1], dy, 0) for dy in (2, 1, 3)]
    came_a = tx_move(go_a, 0, 1)
    half_hidden = ((unit, hidden_here), jnp.bfloat16)
    hidden_a, hidden_b = small_call(activate_kernel, [half_hidden] * 2, keep_a, came_a, keep_b, *came_b)
    came_b = [tx_move(hidden_b, dy, 0) for dy in (1, 2, 3)]
    came_a = tx_move(hidden_a, 0, 1)
    pair_a, line_b = small_call(
        stack_kernel,
        [((2 * unit, hidden_here), jnp.bfloat16), ((4 * unit, hidden_here), jnp.bfloat16)],
        hidden_a, came_a, hidden_b, *came_b,
    )
    pieces_a = [pair_a] + [tx_move(pair_a, dy, 0) for dy in (1, 2, 3)]
    pieces_b = [line_b, tx_move(line_b, 0, 1)]
    w_down = fetch(w_down, 4, pair_a)
    mixed_a, mixed_b = down(from_a, from_b, pieces_a, pieces_b, w_down)
    chip = (f32(mixed_a) + f32(core_swap(mixed_b))).astype(jnp.bfloat16)
    parts = chip_exchange(chip.reshape(8, per, width))
    stream = (f32(own) + jnp.sum(f32(parts), axis=0)).astype(jnp.bfloat16)
    stream_out = stream.reshape(steps, local_rows, width)

    mine, other = gather_ty(stream)
    w_parts = fetch(jnp.transpose(w_qkv, (1, 0, 2)), 3, mine)
    qkv = slot_qkv(mine, other, key_src, key_dst, w_parts)
    received = lax.all_to_all(qkv.reshape(8, block, 3 * local_width), "tx", 0, 0)
    triple = jnp.sum(f32(received), axis=0).astype(jnp.bfloat16)
    triple = triple.reshape(steps, owner_rows, 3, heads_here, HEAD_DIM)
    query, new_keys, new_vals = triple[:, :, 0], triple[:, :, 1], triple[:, :, 2]
    keys_h = cache_keys.reshape(owner_rows, history, heads_here, HEAD_DIM)
    vals_h = cache_values.reshape(owner_rows, history, heads_here, HEAD_DIM)
    old = jnp.einsum("tshd,slhd->tshl", query, keys_h, preferred_element_type=jnp.float32)
    new = jnp.einsum("tshd,ushd->tshu", query, new_keys, preferred_element_type=jnp.float32)
    old = old * HEAD_DIM ** (-0.5)
    new = new * HEAD_DIM ** (-0.5)
    where_pos = jnp.arange(history, dtype=jnp.int32)
    old = jnp.where((where_pos[None, :] < cache_lengths[:, None])[None, :, None, :], old, jnp.float32(-1e30))
    causal = jnp.arange(steps)[:, None] >= jnp.arange(steps)[None, :]
    new = jnp.where(causal[:, None, None, :], new, jnp.float32(-1e30))
    top = jnp.maximum(jnp.max(old, axis=3, keepdims=True), jnp.max(new, axis=3, keepdims=True))
    old = jnp.exp(old - top)
    new = jnp.exp(new - top)
    denom = jnp.sum(old, axis=3, keepdims=True) + jnp.sum(new, axis=3, keepdims=True)
    old = (old / denom).astype(jnp.bfloat16)
    new = (new / denom).astype(jnp.bfloat16)
    attended = jnp.einsum("tshl,slhd->tshd", old, vals_h, preferred_element_type=jnp.float32)
    attended = attended + jnp.einsum("tshu,ushd->tshd", new, new_vals, preferred_element_type=jnp.float32)
    attended = attended.reshape(steps * owner_rows, local_width).astype(jnp.bfloat16)
    part = jnp.einsum("rf,fk->kr", attended, w_class, preferred_element_type=jnp.float32)
    classes = part.shape[0]
    packed = jnp.concatenate([part[: classes // 2], part[classes // 2 :]], axis=1)
    packed = jnp.pad(packed, ((0, 1), (0, 0)))
    spread = lax.all_to_all(jnp.broadcast_to(packed[None], (128,) + packed.shape), ("tx", "ty"), 0, 0)
    by_tx = jnp.sum(spread.reshape(8, 16, 8, 128), axis=1)[:, : classes // 2]
    by_tx = by_tx.reshape(8, classes // 2, 2, steps, owner_rows)
    by_slot = by_tx.transpose(2, 1, 3, 0, 4).reshape(classes * steps, total_rows)
    pick = (jnp.arange(total_rows)[:, None] == row_slots[None, :]).astype(jnp.float32)
    logits = jnp.dot(by_slot, pick, precision=lax.Precision.HIGHEST, preferred_element_type=jnp.float32)
    category_logits = logits.reshape(classes, steps, total_rows).transpose(1, 2, 0)
    return (stream_out, category_logits)


def solution(mesh):
    return jax.shard_map(
        per_device,
        mesh=mesh,
        in_specs=(
            P(None, "ty", "tx"),
            P("tx"),
            P("tx", "ty"),
            P("tx", "ty"),
            P("ty", "tx"),
            P("tx", None, "ty"),
            P("ty", None),
            P("tx", None, "ty"),
            P("tx", None, "ty"),
            P("tx"),
            P(),
        ),
        out_specs=(P(None, "ty", "tx"), P()),
        check_vma=False,
    )
```

time: 255 us -> 201 us (0.79)
  starting transfers between devices: 81.6 us -> 42.1 us
  blocking collectives: 20.7 us -> 54.1 us
  waiting for transfers between devices: 87 us -> 66 us
  local copies, waits for them, and re-layouts: 21.7 us -> 4.75 us
  Pallas kernels: 33.1 us -> 26.9 us
  other arithmetic: 5.85 us -> 2.52 us
    ppermute x24 -> x3, starting transfers between devices: 42.2 us -> 7.2 us  [core_swap(): return lax.ppermute(array, 'ty', [(n, n ^ 1) for n in range(16)])]
    all_to_all x1 -> x3, blocking collectives: 20.7 us -> 54.1 us  [chip_exchange(): return lax.all_to_all(blocks, 'ty', 0, 0, axis_index_groups=groups)]
    ppermute x23 -> x16, waiting for transfers between devices: 65.4 us -> 36.3 us  [tx_move(): return lax.ppermute(array, 'tx', pairs)]
    all_to_all x0 -> x2, waiting for transfers between devices: none -> 27.4 us  [the longest x1 14.5 us: per_device(): lax.all_to_all(qkv.reshape(8, block, 3 * local_width), 'tx', 0, 0)]
    unnamed x48 -> x11, local copies, waits for them, and re-layouts: 20.2 us -> 0.66 us
    ppermute x24 -> x3, waiting for transfers between devices: 21.6 us -> 2.29 us  [core_swap(): return lax.ppermute(array, 'ty', [(n, n ^ 1) for n in range(16)])]
    ppermute x23 -> x16, starting transfers between devices: 39.4 us -> 24.3 us  [tx_move(): return lax.ppermute(array, 'tx', pairs)]
    all_to_all x0 -> x2, starting transfers between devices: none -> 10.6 us  [the longest x1 6.38 us: per_device(): lax.all_to_all(qkv.reshape(8, block, 3 * local_width), 'tx', 0, 0)]
  transfers between devices with their start and end apart: 47 -> 21, of which waited for: 22 -> 13; matrix products, arithmetic and copies ran while one was open for 1% -> 1% of each run, Pallas kernels for 6% -> 6%
where the time goes in v2:
time: 201 us
  waiting for transfers between devices  66 us (33%)
  blocking collectives  54.1 us (27%)
  starting transfers between devices  42.1 us (21%)
  Pallas kernels  26.9 us (13%)
  local copies, waits for them, and re-layouts  4.75 us (2%)
  matrix products  3.17 us (2%)
  other arithmetic  2.52 us (1%)
    all_to_all x3, blocking collectives, chip_exchange(): return lax.all_to_all(blocks, 'ty', 0, 0, axis_index_groups=groups)  54.1 us
    ppermute x16, waiting for transfers between devices, tx_move(): return lax.ppermute(array, 'tx', pairs)  36.3 us
    ppermute x16, starting transfers between devices, tx_move(): return lax.ppermute(array, 'tx', pairs)  24.3 us
    all_to_all x1, waiting for transfers between devices, per_device(): lax.all_to_all(qkv.reshape(8, block, 3 * local_width), 'tx', 0, 0)  14.5 us
    all_to_all x1, waiting for transfers between devices, per_device(): lax.all_to_all(jnp.broadcast_to(packed[None], (128,) + packed.shape), ('t...  13 us
    pallas_call x2, Pallas kernels, gate_up(): pl.pallas_call(load_gate_up_kernel if load else gate_up_kernel, out_shape...  12.6 us
    ppermute x3, starting transfers between devices, core_swap(): return lax.ppermute(array, 'ty', [(n, n ^ 1) for n in range(16)])  7.2 us
    all_to_all x1, starting transfers between devices, per_device(): lax.all_to_all(qkv.reshape(8, block, 3 * local_width), 'tx', 0, 0)  6.38 us
  transfers between devices with their start and end apart: 21, of which 13 were waited for; matrix products, arithmetic and copies ran while one was open for 1% of the time, Pallas kernels for 6%

profile of v2, /device:TPU:1, one launch (start us, length us, event | category | flops | bytes accessed | tf_op | source)
XLA Modules:
  0.0 200.5 jit_solution(3747729712469493329)
XLA Ops:
  1.8 20.3 %all_to_all.25 = bf16[8,32,2048]{2,1,0:T(8,128)(2,1)S(1)} all-to-all(bf16[8,32,2048]{2,1,0:T(8,128)(2,1)S(1)} %broadcast_in_dim.47), channel_id=1, replica_groups={{0,2,4,6,8,10,12,14},{1,3,5,7,9,11,13,15},{16,18,20,22,24,26,28,30},{17..., dimensions={0} | all-to-all | bytes 2097152 | tf_op jit(solution)/shard_map/all_to_all | solution.py:27
  22.1 2.0 collective-permute-start.3
  24.9 8.0 %shard_map.122 = (bf16[64,3456]{1,0:T(8,128)(2,1)S(1)}, bf16[64,3456]{1,0:T(8,128)(2,1)S(1)}, bf16[64,3456]{1,0:T(8,128)(2,1)S(1)}, bf16[64,3456]{1,0:T(8,128)(2...) custom-call(s32[8]{0:T(128)S(1)} %stack.76.order, bf16[256,2048]{1,0:T(8,128)(2,1)S(1)} %bitcast.92, ...), custom_call_target="tpu_custom_call" | custom-call | flops 3489660928 | bytes 15335424 | tf_op jit(solution)/shard_map/pallas_call | solution.py:153
  32.9 4.6 %shard_map.123 = (bf16[128,3456]{1,0:T(8,128)(2,1)S(1)}, bf16[128,3456]{1,0:T(8,128)(2,1)S(1)}) custom-call(s32[8]{0:T(128)S(1)} %stack.77.order, bf16[256,2048]{1,0:T(8,128)(2,1)S(1)} %collective-permute-done.3.x_ref, bf16[1,2048]{1,0:T(2,128)(2,1)S(1)} %broadcast_in_dim.48.gain_ref, bf16[2048,1664]{1,0:T(8,128)(2,1)S(1)} %get-tuple-element.26.wg_ref, ...), custom_call_target="tpu_custom_call" | custom-call | flops 3489660928 | bytes 15335424 | tf_op jit(solution)/shard_map/pallas_call | solution.py:153
  37.5 3.4 %collective-permute-start.4 = (bf16[128,3456]{1,0:T(8,128)(2,1)S(1)}, bf16[128,3456]{1,0:T(8,128)(2,1)S(1)}, u32[]{:S(2)}, u32[]{:S(2)}) collective-permute-start(bf16[128,3456]{1,0:T(8,128)(2,1)S(1)} %get-tuple-element.29), channel_id=1, source_target_pairs={{0,64},{16,80},{32,96},{48,112},{64,0},{80,16},{96,32},{112,48},{1... | collective-permute-start | bytes 2654216 | tf_op jit(solution)/shard_map/ppermute | solution.py:18
  40.9 2.9 %collective-permute-start = (bf16[64,3456]{1,0:T(8,128)(2,1)S(1)}, bf16[64,3456]{1,0:T(8,128)(2,1)S(1)}, u32[]{:S(2)}, u32[]{:S(2)}) collective-permute-start(bf16[64,3456]{1,0:T(8,128)(2,1)S(1)} %get-tuple-element.23), channel_id=1, source_target_pairs={{0,32},{16,48},{32,0},{48,16},{64,96},{80,112},{96,64},{112,80},{1... | collective-permute-start | bytes 1327112 | tf_op jit(solution)/shard_map/ppermute | solution.py:18
  44.2 2.3 %collective-permute-start.2 = (bf16[64,3456]{1,0:T(8,128)(2,1)S(1)}, bf16[64,3456]{1,0:T(8,128)(2,1)S(1)}, u32[]{:S(2)}, u32[]{:S(2)}) collective-permute-start(bf16[64,3456]{1,0:T(8,128)(2,1)S(1)} %get-tuple-element.25), channel_id=1, source_target_pairs={{0,48},{16,0},{32,16},{48,32},{64,112},{80,64},{96,80},{112,96},{1... | collective-permute-start | bytes 1327112 | tf_op jit(solution)/shard_map/ppermute | solution.py:18
  46.5 7.4 %collective-permute-done.a1 = bf16[64,3456]{1,0:T(8,128)(2,1)S(1)} collective-permute-done((bf16[64,3456]{1,0:T(8,128)(2,1)S(1)}, bf16[64,3456]{1,0:T(8,128)(2,1)S(1)}, u32[]{:S(2)}, u32[]{:S(2)}) %collective-permute-start) | collective-permute-done | bytes 442400 | tf_op jit(solution)/shard_map/ppermute | solution.py:18
  53.9 10.0 %collective-permute-done.1.a2 = bf16[64,3456]{1,0:T(8,128)(2,1)S(1)} collective-permute-done((bf16[64,3456]{1,0:T(8,128)(2,1)S(1)}, bf16[64,3456]{1,0:T(8,128)(2,1)S(1)}, u32[]{:S(2)}, u32[]{:S(2)}) %collective-permute-start.1) | collective-permute-done | bytes 442400 | tf_op jit(solution)/shard_map/ppermute | solution.py:18
  64.7 2.4 %collective-permute-start.6 = (bf16[32,3456]{1,0:T(8,128)(2,1)S(1)}, bf16[32,3456]{1,0:T(8,128)(2,1)S(1)}, u32[]{:S(2)}, u32[]{:S(2)}) collective-permute-start(bf16[32,3456]{1,0:T(8,128)(2,1)S(1)} %get-tuple-element.33), channel_id=1, source_target_pairs={{0,32},{16,48},{32,0},{48,16},{64,96},{80,112},{96,64},{112,80},{1... | collective-permute-start | bytes 663560 | tf_op jit(solution)/shard_map/ppermute | solution.py:18
  67.9 1.9 collective-permute-start.8
  69.8 2.3 %collective-permute-done.5.a1 = bf16[32,3456]{1,0:T(8,128)(2,1)S(1)} collective-permute-done((bf16[32,3456]{1,0:T(8,128)(2,1)S(1)}, bf16[32,3456]{1,0:T(8,128)(2,1)S(1)}, u32[]{:S(2)}, u32[]{:S(2)}) %collective-permute-start.5) | collective-permute-done | bytes 221216 | tf_op jit(solution)/shard_map/ppermute | solution.py:18
  72.1 5.8 %collective-permute-done.7.b2 = bf16[32,3456]{1,0:T(8,128)(2,1)S(1)} collective-permute-done((bf16[32,3456]{1,0:T(8,128)(2,1)S(1)}, bf16[32,3456]{1,0:T(8,128)(2,1)S(1)}, u32[]{:S(2)}, u32[]{:S(2)}) %collective-permute-start.7) | collective-permute-done | bytes 221216 | tf_op jit(solution)/shard_map/ppermute | solution.py:18
  78.3 3.2 %collective-permute-start.9 = (bf16[32,1664]{1,0:T(8,128)(2,1)S(1)}, bf16[32,1664]{1,0:T(8,128)(2,1)S(1)}, u32[]{:S(2)}, u32[]{:S(2)}) collective-permute-start(bf16[32,1664]{1,0:T(8,128)(2,1)S(1)} %get-tuple-element.36.a0), channel_id=1, source_target_pairs={{0,64},{16,80},{32,96},{48,112},{64,0},{80,16},{96,32},{112,48},{1... | collective-permute-start | bytes 319496 | tf_op jit(solution)/shard_map/ppermute | solution.py:18
  82.8 2.6 %collective-permute-start.11 = (bf16[32,1664]{1,0:T(8,128)(2,1)S(1)}, bf16[32,1664]{1,0:T(8,128)(2,1)S(1)}, u32[]{:S(2)}, u32[]{:S(2)}) collective-permute-start(bf16[32,1664]{1,0:T(8,128)(2,1)S(1)} %get-tuple-element.37.b0), channel_id=1, source_target_pairs={{0,32},{16,48},{32,0},{48,16},{64,96},{80,112},{96,64},{112,80},{1... | collective-permute-start | bytes 319496 | tf_op jit(solution)/shard_map/ppermute | solution.py:18
  86.3 3.3 %collective-permute-done.11.b2 = bf16[32,1664]{1,0:T(8,128)(2,1)S(1)} collective-permute-done((bf16[32,1664]{1,0:T(8,128)(2,1)S(1)}, bf16[32,1664]{1,0:T(8,128)(2,1)S(1)}, u32[]{:S(2)}, u32[]{:S(2)}) %collective-permute-start.11) | collective-permute-done | bytes 106528 | tf_op jit(solution)/shard_map/ppermute | solution.py:18
  90.7 2.5 %collective-permute-start.14 = (bf16[64,1664]{1,0:T(8,128)(2,1)S(1)}, bf16[64,1664]{1,0:T(8,128)(2,1)S(1)}, u32[]{:S(2)}, u32[]{:S(2)}) collective-permute-start(bf16[64,1664]{1,0:T(8,128)(2,1)S(1)} %get-tuple-element.38.refs_0_), channel_id=1, source_target_pairs={{0,32},{16,48},{32,0},{48,16},{64,96},{80,112},{96,64},{112,80},{1... | collective-permute-start | bytes 638984 | tf_op jit(solution)/shard_map/ppermute | solution.py:18
  93.5 3.0 %shard_map.127.refs_6_ = bf16[1664,2048]{1,0:T(8,128)(2,1)S(1)} custom-call(bf16[1664,2048]{1,0:T(8,128)(2,1)} %source.1, bf16[64,1664]{1,0:T(8,128)(2,1)S(1)} %get-tuple-element.38.refs_0_), custom_call_target="tpu_custom_call" | custom-call | tf_op jit(solution)/shard_map/pallas_call | solution.py:58
  97.7 3.1 %collective-permute-done.14.refs_2_ = bf16[64,1664]{1,0:T(8,128)(2,1)S(1)} collective-permute-done((bf16[64,1664]{1,0:T(8,128)(2,1)S(1)}, bf16[64,1664]{1,0:T(8,128)(2,1)S(1)}, u32[]{:S(2)}, u32[]{:S(2)}) %collective-permute-start.14) | collective-permute-done | bytes 213024 | tf_op jit(solution)/shard_map/ppermute | solution.py:18
  102.2 4.6 %shard_map.128 = (bf16[256,2048]{1,0:T(8,128)(2,1)S(1)}, bf16[256,2048]{1,0:T(8,128)(2,1)S(1)}) custom-call(s32[8]{0:T(128)S(1)} %stack.72.order_a, s32[8]{0:T(128)S(1)} %stack.73.order_b, bf16[64,1664]{1,0:T(8,128)(2,1)S(1)} %get-tuple-element.38.refs_0_, bf16[64,1664]{1,0:T(8,128)(2,1)S(1)} %collective-permute-done.13.refs_1_, ...), custom_call_target="tpu_custom_call" | custom-call | tf_op jit(solution)/shard_map/pallas_call | solution.py:236
  106.8 2.6 %collective-permute-start.17 = (bf16[256,2048]{1,0:T(8,128)(2,1)S(1)}, bf16[256,2048]{1,0:T(8,128)(2,1)S(1)}, u32[]{:S(2)}, u32[]{:S(2)}) collective-permute-start(bf16[256,2048]{1,0:T(8,128)(2,1)S(1)} %get-tuple-element.41), channel_id=1, source_target_pairs={{0,1},{1,0},{2,3},{3,2},{4,5},{5,4},{6,7},{7,6},{8,9},{9,8},{10,11... | collective-permute-start | bytes 3145736 | tf_op jit(solution)/shard_map/ppermute | solution.py:22
  109.4 2.3 %collective-permute-done.17 = bf16[256,2048]{1,0:T(8,128)(2,1)S(1)} collective-permute-done((bf16[256,2048]{1,0:T(8,128)(2,1)S(1)}, bf16[256,2048]{1,0:T(8,128)(2,1)S(1)}, u32[]{:S(2)}, u32[]{:S(2)}) %collective-permute-start.17) | collective-permute-done | bytes 1048608 | tf_op jit(solution)/shard_map/ppermute | solution.py:22
  112.1 16.7 %all_to_all.26 = bf16[8,32,2048]{2,1,0:T(8,128)(2,1)S(1)} all-to-all(bf16[8,32,2048]{2,1,0:T(8,128)(2,1)S(1)} %bitcast.93), channel_id=1, replica_groups={{0,2,4,6,8,10,12,14},{1,3,5,7,9,11,13,15},{16,18,20,22,24,26,28,30},{17..., dimensions={0} | all-to-all | bytes 2097152 | tf_op jit(solution)/shard_map/all_to_all | solution.py:27
  129.1 17.1 %all_to_all.27 = bf16[8,32,2048]{2,1,0:T(8,128)(2,1)S(1)} all-to-all(bf16[8,32,2048]{2,1,0:T(8,128)(2,1)S(1)} %broadcast_in_dim.50), channel_id=1, replica_groups={{0,2,4,6,8,10,12,14},{1,3,5,7,9,11,13,15},{16,18,20,22,24,26,28,30},{17..., dimensions={0} | all-to-all | bytes 2097152 | tf_op jit(solution)/shard_map/all_to_all | solution.py:27
  146.2 2.6 %collective-permute-start.18 = (bf16[256,2048]{1,0:T(8,128)(2,1)S(1)}, bf16[256,2048]{1,0:T(8,128)(2,1)S(1)}, u32[]{:S(2)}, u32[]{:S(2)}) collective-permute-start(bf16[256,2048]{1,0:T(8,128)(2,1)S(1)} %bitcast.88), channel_id=1, source_target_pairs={{0,1},{1,0},{2,3},{3,2},{4,5},{5,4},{6,7},{7,6},{8,9},{9,8},{10,11... | collective-permute-start | bytes 3145736 | tf_op jit(solution)/shard_map/ppermute | solution.py:22
  149.2 1.9 shard_map.129.w_ref
  151.1 4.0 %shard_map.130 = bf16[512,768]{1,0:T(8,128)(2,1)} custom-call(bf16[256,2048]{1,0:T(8,128)(2,1)S(1)} %bitcast.90, bf16[256,2048]{1,0:T(8,128)(2,1)S(1)} %collective-permute-done.18.other_ref, s32[1,512]{1,0:T(1,128)S(1)} %multiply_add_fusion.src_ref, s32[512,1]{1,0:T(8,128)S(1)} %fusion.20.dst_ref, bf16[3,2048,256]{2,1,0:T(8,128)(2,1)S(1)} %shard_map.129.w_ref), custom_call_target="tpu_custom_call" | custom-call | flops 2684354560 | bytes 5242880 | tf_op jit(solution)/shard_map/pallas_call | solution.py:264
  155.1 6.4 %all-to-all-start.3 = ((bf16[8,64,768]{2,1,0:T(8,128)(2,1)}), bf16[8,64,768]{2,1,0:T(8,128)(2,1)S(1)}, u32[]{:S(2)}, u32[]{:S(2)}) async-start(bf16[8,64,768]{2,1,0:T(8,128)(2,1)} %bitcast.17), calls=%async_computation.3 | async-start | bytes 1572864 | tf_op jit(solution)/shard_map/all_to_all | solution.py:368
  161.6 14.5 %all-to-all-done.3 = bf16[8,64,768]{2,1,0:T(8,128)(2,1)S(1)} async-done(((bf16[8,64,768]{2,1,0:T(8,128)(2,1)}), bf16[8,64,768]{2,1,0:T(8,128)(2,1)S(1)}, u32[]{:S(2)}, u32[]{:S(2)}) %all-to-all-start.3) | async-done | bytes 786464 | tf_op jit(solution)/shard_map/all_to_all | solution.py:368
  176.8 2.0 fusion.58
  181.5 4.2 %all-to-all-start.4 = ((f32[128,8,128]{2,1,0:T(8,128)}), f32[128,8,128]{2,1,0:T(8,128)S(1)}, u32[]{:S(2)}, u32[]{:S(2)}) async-start(f32[128,8,128]{2,1,0:T(8,128)} %broadcast_in_dim.85), calls=%async_computation.4 | async-start | bytes 1048576 | tf_op jit(solution)/shard_map/all_to_all | solution.py:395
  186.4 13.0 %all-to-all-done.4 = f32[128,8,128]{2,1,0:T(8,128)S(1)} async-done(((f32[128,8,128]{2,1,0:T(8,128)}), f32[128,8,128]{2,1,0:T(8,128)S(1)}, u32[]{:S(2)}, u32[]{:S(2)}) %all-to-all-start.4) | async-done | bytes 524320 | tf_op jit(solution)/shard_map/all_to_all | solution.py:395
  (81 shorter events, 16.7 us)
Async XLA Ops:
  0.6 179.1 %copy-start = (bf16[32,64,256]{2,1,0:T(8,128)(2,1)S(1)}, bf16[32,64,256]{2,1,0:T(8,128)(2,1)}, u32[]{:S(2)}) copy-start(bf16[32,64,256]{2,1,0:T(8,128)(2,1)} %param.19) | copy-start | bytes 3145732
  22.1 10.8 %collective-permute-start.3 = (bf16[256,2048]{1,0:T(8,128)(2,1)S(1)}, bf16[256,2048]{1,0:T(8,128)(2,1)S(1)}, u32[]{:S(2)}, u32[]{:S(2)}) collective-permute-start(bf16[256,2048]{1,0:T(8,128)(2,1)S(1)} %bitcast.91), channel_id=1, source_target_pairs={{0,1},{1,0},{2,3},{3,2},{4,5},{5,4},{6,7},{7,6},{8,9},{9,8},{10,11... | collective-permute-start | bytes 3145736 | tf_op jit(solution)/shard_map/ppermute | solution.py:22
  37.5 26.5 %collective-permute-start.4 = (bf16[128,3456]{1,0:T(8,128)(2,1)S(1)}, bf16[128,3456]{1,0:T(8,128)(2,1)S(1)}, u32[]{:S(2)}, u32[]{:S(2)}) collective-permute-start(bf16[128,3456]{1,0:T(8,128)(2,1)S(1)} %get-tuple-element.29), channel_id=1, source_target_pairs={{0,64},{16,80},{32,96},{48,112},{64,0},{80,16},{96,32},{112,48},{1... | collective-permute-start | bytes 2654216 | tf_op jit(solution)/shard_map/ppermute | solution.py:18
  40.9 13.0 %collective-permute-start = (bf16[64,3456]{1,0:T(8,128)(2,1)S(1)}, bf16[64,3456]{1,0:T(8,128)(2,1)S(1)}, u32[]{:S(2)}, u32[]{:S(2)}) collective-permute-start(bf16[64,3456]{1,0:T(8,128)(2,1)S(1)} %get-tuple-element.23), channel_id=1, source_target_pairs={{0,32},{16,48},{32,0},{48,16},{64,96},{80,112},{96,64},{112,80},{1... | collective-permute-start | bytes 1327112 | tf_op jit(solution)/shard_map/ppermute | solution.py:18
  43.8 20.2 %collective-permute-start.1 = (bf16[64,3456]{1,0:T(8,128)(2,1)S(1)}, bf16[64,3456]{1,0:T(8,128)(2,1)S(1)}, u32[]{:S(2)}, u32[]{:S(2)}) collective-permute-start(bf16[64,3456]{1,0:T(8,128)(2,1)S(1)} %get-tuple-element.24), channel_id=1, source_target_pairs={{0,16},{16,32},{32,48},{48,0},{64,80},{80,96},{96,112},{112,64},{1... | collective-permute-start | bytes 1327112 | tf_op jit(solution)/shard_map/ppermute | solution.py:18
  44.2 19.8 %collective-permute-start.2 = (bf16[64,3456]{1,0:T(8,128)(2,1)S(1)}, bf16[64,3456]{1,0:T(8,128)(2,1)S(1)}, u32[]{:S(2)}, u32[]{:S(2)}) collective-permute-start(bf16[64,3456]{1,0:T(8,128)(2,1)S(1)} %get-tuple-element.25), channel_id=1, source_target_pairs={{0,48},{16,0},{32,16},{48,32},{64,112},{80,64},{96,80},{112,96},{1... | collective-permute-start | bytes 1327112 | tf_op jit(solution)/shard_map/ppermute | solution.py:18
  64.5 7.7 %collective-permute-start.5 = (bf16[32,3456]{1,0:T(8,128)(2,1)S(1)}, bf16[32,3456]{1,0:T(8,128)(2,1)S(1)}, u32[]{:S(2)}, u32[]{:S(2)}) collective-permute-start(bf16[32,3456]{1,0:T(8,128)(2,1)S(1)} %get-tuple-element.31), channel_id=1, source_target_pairs={{0,64},{16,80},{32,96},{48,112},{64,0},{80,16},{96,32},{112,48},{1... | collective-permute-start | bytes 663560 | tf_op jit(solution)/shard_map/ppermute | solution.py:18
  64.7 7.4 %collective-permute-start.6 = (bf16[32,3456]{1,0:T(8,128)(2,1)S(1)}, bf16[32,3456]{1,0:T(8,128)(2,1)S(1)}, u32[]{:S(2)}, u32[]{:S(2)}) collective-permute-start(bf16[32,3456]{1,0:T(8,128)(2,1)S(1)} %get-tuple-element.33), channel_id=1, source_target_pairs={{0,32},{16,48},{32,0},{48,16},{64,96},{80,112},{96,64},{112,80},{1... | collective-permute-start | bytes 663560 | tf_op jit(solution)/shard_map/ppermute | solution.py:18
  67.2 10.8 %collective-permute-start.7 = (bf16[32,3456]{1,0:T(8,128)(2,1)S(1)}, bf16[32,3456]{1,0:T(8,128)(2,1)S(1)}, u32[]{:S(2)}, u32[]{:S(2)}) collective-permute-start(bf16[32,3456]{1,0:T(8,128)(2,1)S(1)} %get-tuple-element.34), channel_id=1, source_target_pairs={{0,16},{16,32},{32,48},{48,0},{64,80},{80,96},{96,112},{112,64},{1... | collective-permute-start | bytes 663560 | tf_op jit(solution)/shard_map/ppermute | solution.py:18
  67.9 10.0 %collective-permute-start.8 = (bf16[32,3456]{1,0:T(8,128)(2,1)S(1)}, bf16[32,3456]{1,0:T(8,128)(2,1)S(1)}, u32[]{:S(2)}, u32[]{:S(2)}) collective-permute-start(bf16[32,3456]{1,0:T(8,128)(2,1)S(1)} %get-tuple-element.35), channel_id=1, source_target_pairs={{0,48},{16,0},{32,16},{48,32},{64,112},{80,64},{96,80},{112,96},{1... | collective-permute-start | bytes 663560 | tf_op jit(solution)/shard_map/ppermute | solution.py:18
  78.3 7.1 %collective-permute-start.9 = (bf16[32,1664]{1,0:T(8,128)(2,1)S(1)}, bf16[32,1664]{1,0:T(8,128)(2,1)S(1)}, u32[]{:S(2)}, u32[]{:S(2)}) collective-permute-start(bf16[32,1664]{1,0:T(8,128)(2,1)S(1)} %get-tuple-element.36.a0), channel_id=1, source_target_pairs={{0,64},{16,80},{32,96},{48,112},{64,0},{80,16},{96,32},{112,48},{1... | collective-permute-start | bytes 319496 | tf_op jit(solution)/shard_map/ppermute | solution.py:18
  81.5 4.9 %collective-permute-start.10 = (bf16[32,1664]{1,0:T(8,128)(2,1)S(1)}, bf16[32,1664]{1,0:T(8,128)(2,1)S(1)}, u32[]{:S(2)}, u32[]{:S(2)}) collective-permute-start(bf16[32,1664]{1,0:T(8,128)(2,1)S(1)} %get-tuple-element.37.b0), channel_id=1, source_target_pairs={{0,16},{16,32},{32,48},{48,0},{64,80},{80,96},{96,112},{112,64},{1... | collective-permute-start | bytes 319496 | tf_op jit(solution)/shard_map/ppermute | solution.py:18
  82.8 6.9 %collective-permute-start.11 = (bf16[32,1664]{1,0:T(8,128)(2,1)S(1)}, bf16[32,1664]{1,0:T(8,128)(2,1)S(1)}, u32[]{:S(2)}, u32[]{:S(2)}) collective-permute-start(bf16[32,1664]{1,0:T(8,128)(2,1)S(1)} %get-tuple-element.37.b0), channel_id=1, source_target_pairs={{0,32},{16,48},{32,0},{48,16},{64,96},{80,112},{96,64},{112,80},{1... | collective-permute-start | bytes 319496 | tf_op jit(solution)/shard_map/ppermute | solution.py:18
  85.4 5.0 %collective-permute-start.12 = (bf16[32,1664]{1,0:T(8,128)(2,1)S(1)}, bf16[32,1664]{1,0:T(8,128)(2,1)S(1)}, u32[]{:S(2)}, u32[]{:S(2)}) collective-permute-start(bf16[32,1664]{1,0:T(8,128)(2,1)S(1)} %get-tuple-element.37.b0), channel_id=1, source_target_pairs={{0,48},{16,0},{32,16},{48,32},{64,112},{80,64},{96,80},{112,96},{1... | collective-permute-start | bytes 319496 | tf_op jit(solution)/shard_map/ppermute | solution.py:18
  90.5 11.7 %collective-permute-start.16 = (bf16[128,1664]{1,0:T(8,128)(2,1)S(1)}, bf16[128,1664]{1,0:T(8,128)(2,1)S(1)}, u32[]{:S(2)}, u32[]{:S(2)}) collective-permute-start(bf16[128,1664]{1,0:T(8,128)(2,1)S(1)} %get-tuple-element.39.refs_4_), channel_id=1, source_target_pairs={{0,64},{16,80},{32,96},{48,112},{64,0},{80,16},{96,32},{112,48},{1... | collective-permute-start | bytes 1277960 | tf_op jit(solution)/shard_map/ppermute | solution.py:18
  90.6 7.2 %collective-permute-start.13 = (bf16[64,1664]{1,0:T(8,128)(2,1)S(1)}, bf16[64,1664]{1,0:T(8,128)(2,1)S(1)}, u32[]{:S(2)}, u32[]{:S(2)}) collective-permute-start(bf16[64,1664]{1,0:T(8,128)(2,1)S(1)} %get-tuple-element.38.refs_0_), channel_id=1, source_target_pairs={{0,16},{16,32},{32,48},{48,0},{64,80},{80,96},{96,112},{112,64},{1... | collective-permute-start | bytes 638984 | tf_op jit(solution)/shard_map/ppermute | solution.py:18
  90.7 10.2 %collective-permute-start.14 = (bf16[64,1664]{1,0:T(8,128)(2,1)S(1)}, bf16[64,1664]{1,0:T(8,128)(2,1)S(1)}, u32[]{:S(2)}, u32[]{:S(2)}) collective-permute-start(bf16[64,1664]{1,0:T(8,128)(2,1)S(1)} %get-tuple-element.38.refs_0_), channel_id=1, source_target_pairs={{0,32},{16,48},{32,0},{48,16},{64,96},{80,112},{96,64},{112,80},{1... | collective-permute-start | bytes 638984 | tf_op jit(solution)/shard_map/ppermute | solution.py:18
  93.1 9.1 %collective-permute-start.15 = (bf16[64,1664]{1,0:T(8,128)(2,1)S(1)}, bf16[64,1664]{1,0:T(8,128)(2,1)S(1)}, u32[]{:S(2)}, u32[]{:S(2)}) collective-permute-start(bf16[64,1664]{1,0:T(8,128)(2,1)S(1)} %get-tuple-element.38.refs_0_), channel_id=1, source_target_pairs={{0,48},{16,0},{32,16},{48,32},{64,112},{80,64},{96,80},{112,96},{1... | collective-permute-start | bytes 638984 | tf_op jit(solution)/shard_map/ppermute | solution.py:18
  96.5 32.4 %copy-start.1 = (bf16[2,16,2048]{2,1,0:T(8,128)(2,1)S(1)}, bf16[2,16,2048]{2,1,0:T(8,128)(2,1)}, u32[]{:S(2)}) copy-start(bf16[2,16,2048]{2,1,0:T(8,128)(2,1)} %param.11) | copy-start | bytes 393220
  106.8 42.1 %copy-start.3 = (s32[256]{0:T(256)S(1)}, s32[256]{0:T(256)}, u32[]{:S(2)}) copy-start(s32[256]{0:T(256)} %param.21) | copy-start | bytes 3076
  106.8 4.9 %collective-permute-start.17 = (bf16[256,2048]{1,0:T(8,128)(2,1)S(1)}, bf16[256,2048]{1,0:T(8,128)(2,1)S(1)}, u32[]{:S(2)}, u32[]{:S(2)}) collective-permute-start(bf16[256,2048]{1,0:T(8,128)(2,1)S(1)} %get-tuple-element.41), channel_id=1, source_target_pairs={{0,1},{1,0},{2,3},{3,2},{4,5},{5,4},{6,7},{7,6},{8,9},{9,8},{10,11... | collective-permute-start | bytes 3145736 | tf_op jit(solution)/shard_map/ppermute | solution.py:22
  146.2 4.9 %collective-permute-start.18 = (bf16[256,2048]{1,0:T(8,128)(2,1)S(1)}, bf16[256,2048]{1,0:T(8,128)(2,1)S(1)}, u32[]{:S(2)}, u32[]{:S(2)}) collective-permute-start(bf16[256,2048]{1,0:T(8,128)(2,1)S(1)} %bitcast.88), channel_id=1, source_target_pairs={{0,1},{1,0},{2,3},{3,2},{4,5},{5,4},{6,7},{7,6},{8,9},{9,8},{10,11... | collective-permute-start | bytes 3145736 | tf_op jit(solution)/shard_map/ppermute | solution.py:22
  151.1 10.4 %copy-start.4 = (s32[32]{0:T(128)S(1)}, s32[32]{0:T(128)}, u32[]{:S(2)}) copy-start(s32[32]{0:T(128)} %param.20) | copy-start | bytes 388
  155.1 25.3 %copy-start.2 = (bf16[256,14]{0,1:T(8,128)(2,1)S(1)}, bf16[256,14]{0,1:T(8,128)(2,1)}, u32[]{:S(2)}) copy-start(bf16[256,14]{0,1:T(8,128)(2,1)} %param.17) | copy-start | bytes 21508
  155.1 20.9 %all-to-all-start.3 = ((bf16[8,64,768]{2,1,0:T(8,128)(2,1)}), bf16[8,64,768]{2,1,0:T(8,128)(2,1)S(1)}, u32[]{:S(2)}, u32[]{:S(2)}) async-start(bf16[8,64,768]{2,1,0:T(8,128)(2,1)} %bitcast.17), calls=%async_computation.3 | async-start | bytes 1572864 | tf_op jit(solution)/shard_map/all_to_all | solution.py:368
  181.5 17.9 %all-to-all-start.4 = ((f32[128,8,128]{2,1,0:T(8,128)}), f32[128,8,128]{2,1,0:T(8,128)S(1)}, u32[]{:S(2)}, u32[]{:S(2)}) async-start(f32[128,8,128]{2,1,0:T(8,128)} %broadcast_in_dim.85), calls=%async_computation.4 | async-start | bytes 1048576 | tf_op jit(solution)/shard_map/all_to_all | solution.py:395

commit v3 on v2

--- a/solution.py
+++ b/solution.py
@@ -173,7 +173,7 @@
     )(*arrays)
 
 
-def first_sums_kernel(a0, a1, a2, a3, b0, b1, keep_a, go_a, keep_b, go_b1, go_b2, go_b3):
+def first_sums_kernel(a0, a1, a2, a3, b0, b1, c0, c1, keep_a, go_a, keep_b, go_b1, go_b2, go_b3):
     unit, wide = keep_a.shape
     for start in range(0, wide, 128):
         at = slice(start, start + 128)
@@ -182,8 +182,9 @@
             total = f32(a0[rows, at]) + f32(a1[rows, at]) + f32(a2[rows, at]) + f32(a3[rows, at])
             out[:, at] = total.astype(out.dtype)
         for n, out in enumerate((keep_b, go_b1, go_b2, go_b3)):
-            rows = slice(n * unit, (n + 1) * unit)
-            out[:, at] = (f32(b0[rows, at]) + f32(b1[rows, at])).astype(out.dtype)
+            rows = slice((n % 2) * unit, (n % 2 + 1) * unit)
+            own, came = (b0, c0) if n < 2 else (b1, c1)
+            out[:, at] = (f32(own[rows, at]) + f32(came[rows, at])).astype(out.dtype)
 
 
 def activate_kernel(keep_a, a1, keep_b, b1, b2, b3, out_a, out_b):
@@ -243,7 +244,8 @@
     )(order_a, order_b, *pieces, w_down)
 
 
-def qkv_kernel(mine_ref, other_ref, src_ref, dst_ref, w_ref, out, ordered):
+def qkv_kernel(mine_ref, other_ref, src_ref, dst_ref, w_ref, *refs):
+    outs, ordered = refs[:-1], refs[-1]
     half = mine_ref.shape[0]
     pick = jnp.where(dst_ref[...] == src_ref[...], 1.0, 0.0).astype(jnp.bfloat16)
     for start in range(0, mine_ref.shape[1], 512):
@@ -254,7 +256,7 @@
     wide = w_ref.shape[2]
     for part in range(w_ref.shape[0]):
         result = jnp.dot(ordered[...], w_ref[part], preferred_element_type=jnp.float32).astype(jnp.bfloat16)
-        out[:, part * wide : (part + 1) * wide] = result
+        spread(outs, result, part * wide)
 
 
 def slot_qkv(mine, other, key_src, key_dst, w_parts):
@@ -263,9 +265,9 @@
     parts, _, wide = w_parts.shape
     return pl.pallas_call(
         qkv_kernel,
-        out_shape=jax.ShapeDtypeStruct((rows, parts * wide), jnp.bfloat16),
+        out_shape=[jax.ShapeDtypeStruct((rows // 8, parts * wide), jnp.bfloat16)] * 8,
         in_specs=[VM] * 5,
-        out_specs=VM,
+        out_specs=[VM] * 8,
         scratch_shapes=[pltpu.VMEM((rows, width), jnp.bfloat16)],
         compiler_params=pltpu.CompilerParams(vmem_limit_bytes=12 * 1024 * 1024),
         cost_estimate=pl.CostEstimate(
@@ -326,21 +328,25 @@
     hit = row_of[:, None] == jnp.arange(total_rows, dtype=jnp.int32)[None, :]
     slot_of = jnp.sum(jnp.where(hit, row_slots[None, :], 0), axis=1)
     key_src = (((pos % per) // local_rows) * total_rows + slot_of)[None, :]
-    key_dst = ((pos % block) // owner_rows) * total_rows + pos // block * owner_rows + pos % owner_rows
+    moves = [(0, 0), (2, 1), (1, 1), (3, 1), (2, 0), (0, 1), (1, 0), (3, 0)]
+    target = jnp.zeros((rows,), jnp.int32)
+    for n, move in enumerate(moves):
+        target = jnp.where(pos // block == n, to(*move), target)
+    key_dst = ((pos % block) // owner_rows) * total_rows + target * owner_rows + pos % owner_rows
     key_dst = key_dst[:, None]
 
     own = states.reshape(per, width)
     gain = norm_gain[None, :]
     mine, other = gather_ty(own)
     *part_a, w_gate, w_up = gate_up(send_a, mine, gain, w_gate, w_up, 4, True)
-    part_b = gate_up(send_b, other, gain, w_gate, w_up, 2, False)
+    part_b = gate_up(send_b, other, gain, w_gate, w_up, 4, False)
     half_send = (unit, part_a[0].shape[1])
     came_a = [tx_move(part_a[dy], dy, 0) for dy in (2, 1, 3)]
-    came_b = tx_move(part_b[1], 0, 1)
+    came_b = [tx_move(part_b[n], 0, 1) for n in (2, 3)]
     keep_a, go_a, keep_b, *go_b = small_call(
         first_sums_kernel,
         [(half_send, jnp.float32), (half_send, jnp.bfloat16), (half_send, jnp.float32)] + [(half_send, jnp.bfloat16)] * 3,
-        part_a[0], *came_a, part_b[0], came_b,
+        part_a[0], *came_a, *part_b[:2], *came_b,
     )
     came_b = [tx_move(go_b[dy - 1], dy, 0) for dy in (2, 1, 3)]
     came_a = tx_move(go_a, 0, 1)
@@ -365,8 +371,10 @@
     mine, other = gather_ty(stream)
     w_parts = fetch(jnp.transpose(w_qkv, (1, 0, 2)), 3, mine)
     qkv = slot_qkv(mine, other, key_src, key_dst, w_parts)
-    received = lax.all_to_all(qkv.reshape(8, block, 3 * local_width), "tx", 0, 0)
-    triple = jnp.sum(f32(received), axis=0).astype(jnp.bfloat16)
+    triple = f32(qkv[0])
+    for piece, move in zip(qkv[1:], moves[1:]):
+        triple = triple + f32(tx_move(piece, *move))
+    triple = triple.astype(jnp.bfloat16)
     triple = triple.reshape(steps, owner_rows, 3, heads_here, HEAD_DIM)
     query, new_keys, new_vals = triple[:, :, 0], triple[:, :, 1], triple[:, :, 2]
     keys_h = cache_keys.reshape(owner_rows, history, heads_here, HEAD_DIM)

time: 201 us -> 202 us (level)
  starting transfers between devices: 42.1 us -> 52.2 us
  waiting for transfers between devices: 66 us -> 58 us
    all_to_all x1 -> x0, waiting for transfers between devices: 14.5 us -> none  [per_device(): lax.all_to_all(qkv.reshape(8, block, 3 * local_width), 'tx', 0, 0)]
    ppermute x16 -> x24, starting transfers between devices: 24.3 us -> 35.6 us  [tx_move(): return lax.ppermute(array, 'tx', pairs)]
    ppermute x16 -> x24, waiting for transfers between devices: 36.3 us -> 42.9 us  [tx_move(): return lax.ppermute(array, 'tx', pairs)]
    all_to_all x1 -> x0, starting transfers between devices: 6.38 us -> none  [per_device(): lax.all_to_all(qkv.reshape(8, block, 3 * local_width), 'tx', 0, 0)]
    all_to_all x1, starting transfers between devices: 4.2 us -> 8.6 us  [per_device(): lax.all_to_all(jnp.broadcast_to(packed[None], (128,) + packed.shape), ('t...]
  transfers between devices with their start and end apart: 21 -> 28, of which waited for: 13 -> 16; matrix products, arithmetic and copies ran while one was open for 1% -> 1% of each run, Pallas kernels for 6% -> 9%
where the time goes in v3:
time: 202 us
  waiting for transfers between devices  58 us (29%)
  blocking collectives  54.1 us (27%)
  starting transfers between devices  52.2 us (26%)
  Pallas kernels  26 us (13%)
  local copies, waits for them, and re-layouts  4.76 us (2%)
  matrix products  3.18 us (2%)
  other arithmetic  2.5 us (1%)
    all_to_all x3, blocking collectives, chip_exchange(): return lax.all_to_all(blocks, 'ty', 0, 0, axis_index_groups=groups)  54.1 us
    ppermute x24, waiting for transfers between devices, tx_move(): return lax.ppermute(array, 'tx', pairs)  42.9 us
    ppermute x24, starting transfers between devices, tx_move(): return lax.ppermute(array, 'tx', pairs)  35.6 us
    all_to_all x1, waiting for transfers between devices, per_device(): lax.all_to_all(jnp.broadcast_to(packed[None], (128,) + packed.shape), ('t...  12.9 us
    pallas_call x2, Pallas kernels, gate_up(): pl.pallas_call(load_gate_up_kernel if load else gate_up_kernel, out_shape...  12.6 us
    all_to_all x1, starting transfers between devices, per_device(): lax.all_to_all(jnp.broadcast_to(packed[None], (128,) + packed.shape), ('t...  8.6 us
    ppermute x3, starting transfers between devices, core_swap(): return lax.ppermute(array, 'ty', [(n, n ^ 1) for n in range(16)])  7.96 us
    pallas_call x2, Pallas kernels, fetch(): pl.pallas_call(fetch_kernel, out_shape=pltpu.VMEM(array.shape, array.dtyp...  4.92 us
  transfers between devices with their start and end apart: 28, of which 16 were waited for; matrix products, arithmetic and copies ran while one was open for 1% of the time, Pallas kernels for 9%

profile of v3, /device:TPU:1, one launch (start us, length us, event | category | flops | bytes accessed | tf_op | source)
XLA Modules:
  0.0 201.7 jit_solution(10814685229587146296)
XLA Ops:
  1.8 20.3 %all_to_all.20 = bf16[8,32,2048]{2,1,0:T(8,128)(2,1)S(1)} all-to-all(bf16[8,32,2048]{2,1,0:T(8,128)(2,1)S(1)} %broadcast_in_dim.101), channel_id=1, replica_groups={{0,2,4,6,8,10,12,14},{1,3,5,7,9,11,13,15},{16,18,20,22,24,26,28,30},{17..., dimensions={0} | all-to-all | bytes 2097152 | tf_op jit(solution)/shard_map/all_to_all | solution.py:27
  22.1 2.0 collective-permute-start.3
  24.9 8.0 %shard_map.122 = (bf16[64,3456]{1,0:T(8,128)(2,1)S(1)}, bf16[64,3456]{1,0:T(8,128)(2,1)S(1)}, bf16[64,3456]{1,0:T(8,128)(2,1)S(1)}, bf16[64,3456]{1,0:T(8,128)(2...) custom-call(s32[8]{0:T(128)S(1)} %stack.76.order, bf16[256,2048]{1,0:T(8,128)(2,1)S(1)} %bitcast.91, ...), custom_call_target="tpu_custom_call" | custom-call | flops 3489660928 | bytes 15335424 | tf_op jit(solution)/shard_map/pallas_call | solution.py:153
  32.9 3.0 %collective-permute-start = (bf16[64,3456]{1,0:T(8,128)(2,1)S(1)}, bf16[64,3456]{1,0:T(8,128)(2,1)S(1)}, u32[]{:S(2)}, u32[]{:S(2)}) collective-permute-start(bf16[64,3456]{1,0:T(8,128)(2,1)S(1)} %get-tuple-element.33), channel_id=1, source_target_pairs={{0,32},{16,48},{32,0},{48,16},{64,96},{80,112},{96,64},{112,80},{1... | collective-permute-start | bytes 1327112 | tf_op jit(solution)/shard_map/ppermute | solution.py:18
  36.3 2.3 %collective-permute-start.2 = (bf16[64,3456]{1,0:T(8,128)(2,1)S(1)}, bf16[64,3456]{1,0:T(8,128)(2,1)S(1)}, u32[]{:S(2)}, u32[]{:S(2)}) collective-permute-start(bf16[64,3456]{1,0:T(8,128)(2,1)S(1)} %get-tuple-element.35), channel_id=1, source_target_pairs={{0,48},{16,0},{32,16},{48,32},{64,112},{80,64},{96,80},{112,96},{1... | collective-permute-start | bytes 1327112 | tf_op jit(solution)/shard_map/ppermute | solution.py:18
  38.6 4.6 %shard_map.123 = (bf16[64,3456]{1,0:T(8,128)(2,1)S(1)}, bf16[64,3456]{1,0:T(8,128)(2,1)S(1)}, bf16[64,3456]{1,0:T(8,128)(2,1)S(1)}, bf16[64,3456]{1,0:T(8,128)(2,1)S(1)}) custom-call(s32[8]{0:T(128)S(1)} %stack.77.order, bf16[256,2048]{1,0:T(8,128)(2,1)S(1)} %collective-permute-done.3.x_ref, bf16[1,2048]{1,0:T(2,128)(2,1)S(1)} %broadcast_in_dim.102.gain_ref, ...), custom_call_target="tpu_custom_call" | custom-call | flops 3489660928 | bytes 15335424 | tf_op jit(solution)/shard_map/pallas_call | solution.py:153
  43.2 3.4 %collective-permute-start.4 = (bf16[64,3456]{1,0:T(8,128)(2,1)S(1)}, bf16[64,3456]{1,0:T(8,128)(2,1)S(1)}, u32[]{:S(2)}, u32[]{:S(2)}) collective-permute-start(bf16[64,3456]{1,0:T(8,128)(2,1)S(1)} %get-tuple-element.40), channel_id=1, source_target_pairs={{0,64},{16,80},{32,96},{48,112},{64,0},{80,16},{96,32},{112,48},{1... | collective-permute-start | bytes 1327112 | tf_op jit(solution)/shard_map/ppermute | solution.py:18
  46.7 9.4 %collective-permute-done.1.a2 = bf16[64,3456]{1,0:T(8,128)(2,1)S(1)} collective-permute-done((bf16[64,3456]{1,0:T(8,128)(2,1)S(1)}, bf16[64,3456]{1,0:T(8,128)(2,1)S(1)}, u32[]{:S(2)}, u32[]{:S(2)}) %collective-permute-start.1) | collective-permute-done | bytes 442400 | tf_op jit(solution)/shard_map/ppermute | solution.py:18
  56.3 9.5 %collective-permute-done.5.c1 = bf16[64,3456]{1,0:T(8,128)(2,1)S(1)} collective-permute-done((bf16[64,3456]{1,0:T(8,128)(2,1)S(1)}, bf16[64,3456]{1,0:T(8,128)(2,1)S(1)}, u32[]{:S(2)}, u32[]{:S(2)}) %collective-permute-start.5) | collective-permute-done | bytes 442400 | tf_op jit(solution)/shard_map/ppermute | solution.py:18
  66.2 2.7 %collective-permute-start.6 = (bf16[32,3456]{1,0:T(8,128)(2,1)S(1)}, bf16[32,3456]{1,0:T(8,128)(2,1)S(1)}, u32[]{:S(2)}, u32[]{:S(2)}) collective-permute-start(bf16[32,3456]{1,0:T(8,128)(2,1)S(1)} %get-tuple-element.43), channel_id=1, source_target_pairs={{0,64},{16,80},{32,96},{48,112},{64,0},{80,16},{96,32},{112,48},{1... | collective-permute-start | bytes 663560 | tf_op jit(solution)/shard_map/ppermute | solution.py:18
  73.3 2.0 %collective-permute-done.7.b1 = bf16[32,3456]{1,0:T(8,128)(2,1)S(1)} collective-permute-done((bf16[32,3456]{1,0:T(8,128)(2,1)S(1)}, bf16[32,3456]{1,0:T(8,128)(2,1)S(1)}, u32[]{:S(2)}, u32[]{:S(2)}) %collective-permute-start.7) | collective-permute-done | bytes 221216 | tf_op jit(solution)/shard_map/ppermute | solution.py:18
  75.3 6.6 %collective-permute-done.8.b2 = bf16[32,3456]{1,0:T(8,128)(2,1)S(1)} collective-permute-done((bf16[32,3456]{1,0:T(8,128)(2,1)S(1)}, bf16[32,3456]{1,0:T(8,128)(2,1)S(1)}, u32[]{:S(2)}, u32[]{:S(2)}) %collective-permute-start.8) | collective-permute-done | bytes 221216 | tf_op jit(solution)/shard_map/ppermute | solution.py:18
  85.3 2.1 %collective-permute-done.10.a1 = bf16[32,1664]{1,0:T(8,128)(2,1)S(1)} collective-permute-done((bf16[32,1664]{1,0:T(8,128)(2,1)S(1)}, bf16[32,1664]{1,0:T(8,128)(2,1)S(1)}, u32[]{:S(2)}, u32[]{:S(2)}) %collective-permute-start.10) | collective-permute-done | bytes 106528 | tf_op jit(solution)/shard_map/ppermute | solution.py:18
  89.9 2.7 %collective-permute-start.17 = (bf16[128,1664]{1,0:T(8,128)(2,1)S(1)}, bf16[128,1664]{1,0:T(8,128)(2,1)S(1)}, u32[]{:S(2)}, u32[]{:S(2)}) collective-permute-start(bf16[128,1664]{1,0:T(8,128)(2,1)S(1)} %get-tuple-element.51.refs_4_), channel_id=1, source_target_pairs={{0,64},{16,80},{32,96},{48,112},{64,0},{80,16},{96,32},{112,48},{1... | collective-permute-start | bytes 1277960 | tf_op jit(solution)/shard_map/ppermute | solution.py:18
  93.7 2.6 %collective-permute-start.15 = (bf16[64,1664]{1,0:T(8,128)(2,1)S(1)}, bf16[64,1664]{1,0:T(8,128)(2,1)S(1)}, u32[]{:S(2)}, u32[]{:S(2)}) collective-permute-start(bf16[64,1664]{1,0:T(8,128)(2,1)S(1)} %get-tuple-element.50.refs_0_), channel_id=1, source_target_pairs={{0,32},{16,48},{32,0},{48,16},{64,96},{80,112},{96,64},{112,80},{1... | collective-permute-start | bytes 638984 | tf_op jit(solution)/shard_map/ppermute | solution.py:18
  96.5 3.0 %shard_map.127.refs_6_ = bf16[1664,2048]{1,0:T(8,128)(2,1)S(1)} custom-call(bf16[1664,2048]{1,0:T(8,128)(2,1)} %source.1, bf16[64,1664]{1,0:T(8,128)(2,1)S(1)} %get-tuple-element.50.refs_0_), custom_call_target="tpu_custom_call" | custom-call | tf_op jit(solution)/shard_map/pallas_call | solution.py:58
  99.5 4.2 %collective-permute-done.15.refs_2_ = bf16[64,1664]{1,0:T(8,128)(2,1)S(1)} collective-permute-done((bf16[64,1664]{1,0:T(8,128)(2,1)S(1)}, bf16[64,1664]{1,0:T(8,128)(2,1)S(1)}, u32[]{:S(2)}, u32[]{:S(2)}) %collective-permute-start.15) | collective-permute-done | bytes 213024 | tf_op jit(solution)/shard_map/ppermute | solution.py:18
  103.8 4.6 %shard_map.128 = (bf16[256,2048]{1,0:T(8,128)(2,1)S(1)}, bf16[256,2048]{1,0:T(8,128)(2,1)S(1)}) custom-call(s32[8]{0:T(128)S(1)} %stack.72.order_a, s32[8]{0:T(128)S(1)} %stack.73.order_b, bf16[64,1664]{1,0:T(8,128)(2,1)S(1)} %get-tuple-element.50.refs_0_, bf16[64,1664]{1,0:T(8,128)(2,1)S(1)} %collective-permute-done.14.refs_1_, ...), custom_call_target="tpu_custom_call" | custom-call | tf_op jit(solution)/shard_map/pallas_call | solution.py:237
  108.4 3.3 %collective-permute-start.18 = (bf16[256,2048]{1,0:T(8,128)(2,1)S(1)}, bf16[256,2048]{1,0:T(8,128)(2,1)S(1)}, u32[]{:S(2)}, u32[]{:S(2)}) collective-permute-start(bf16[256,2048]{1,0:T(8,128)(2,1)S(1)} %get-tuple-element.53), channel_id=1, source_target_pairs={{0,1},{1,0},{2,3},{3,2},{4,5},{5,4},{6,7},{7,6},{8,9},{9,8},{10,11... | collective-permute-start | bytes 3145736 | tf_op jit(solution)/shard_map/ppermute | solution.py:22
  111.8 2.3 %collective-permute-done.18 = bf16[256,2048]{1,0:T(8,128)(2,1)S(1)} collective-permute-done((bf16[256,2048]{1,0:T(8,128)(2,1)S(1)}, bf16[256,2048]{1,0:T(8,128)(2,1)S(1)}, u32[]{:S(2)}, u32[]{:S(2)}) %collective-permute-start.18) | collective-permute-done | bytes 1048608 | tf_op jit(solution)/shard_map/ppermute | solution.py:22
  114.5 16.7 %all_to_all.21 = bf16[8,32,2048]{2,1,0:T(8,128)(2,1)S(1)} all-to-all(bf16[8,32,2048]{2,1,0:T(8,128)(2,1)S(1)} %bitcast.92), channel_id=1, replica_groups={{0,2,4,6,8,10,12,14},{1,3,5,7,9,11,13,15},{16,18,20,22,24,26,28,30},{17..., dimensions={0} | all-to-all | bytes 2097152 | tf_op jit(solution)/shard_map/all_to_all | solution.py:27
  131.4 17.1 %all_to_all.22 = bf16[8,32,2048]{2,1,0:T(8,128)(2,1)S(1)} all-to-all(bf16[8,32,2048]{2,1,0:T(8,128)(2,1)S(1)} %broadcast_in_dim.104), channel_id=1, replica_groups={{0,2,4,6,8,10,12,14},{1,3,5,7,9,11,13,15},{16,18,20,22,24,26,28,30},{17..., dimensions={0} | all-to-all | bytes 2097152 | tf_op jit(solution)/shard_map/all_to_all | solution.py:27
  148.5 2.6 %collective-permute-start.19 = (bf16[256,2048]{1,0:T(8,128)(2,1)S(1)}, bf16[256,2048]{1,0:T(8,128)(2,1)S(1)}, u32[]{:S(2)}, u32[]{:S(2)}) collective-permute-start(bf16[256,2048]{1,0:T(8,128)(2,1)S(1)} %bitcast.87), channel_id=1, source_target_pairs={{0,1},{1,0},{2,3},{3,2},{4,5},{5,4},{6,7},{7,6},{8,9},{9,8},{10,11... | collective-permute-start | bytes 3145736 | tf_op jit(solution)/shard_map/ppermute | solution.py:22
  151.6 1.9 shard_map.129.w_ref
  153.5 3.1 %shard_map.130 = (bf16[64,768]{1,0:T(8,128)(2,1)S(1)}, bf16[64,768]{1,0:T(8,128)(2,1)S(1)}, bf16[64,768]{1,0:T(8,128)(2,1)S(1)}, bf16[64,768]{1,0:T(8,128)(2,1)S...) custom-call(bf16[256,2048]{1,0:T(8,128)(2,1)S(1)} %bitcast.89, ...), custom_call_target="tpu_custom_call" | custom-call | flops 2684354560 | bytes 5242880 | tf_op jit(solution)/shard_map/pallas_call | solution.py:266
  156.5 2.0 %collective-permute-start.26 = (bf16[64,768]{1,0:T(8,128)(2,1)S(1)}, bf16[64,768]{1,0:T(8,128)(2,1)S(1)}, u32[]{:S(2)}, u32[]{:S(2)}) collective-permute-start(bf16[64,768]{1,0:T(8,128)(2,1)S(1)} %get-tuple-element.61), channel_id=1, source_target_pairs={{0,48},{16,0},{32,16},{48,32},{64,112},{80,64},{96,80},{112,96},{1... | collective-permute-start | bytes 294920 | tf_op jit(solution)/shard_map/ppermute | solution.py:18
  160.5 3.5 %collective-permute-start.22 = (bf16[64,768]{1,0:T(8,128)(2,1)S(1)}, bf16[64,768]{1,0:T(8,128)(2,1)S(1)}, u32[]{:S(2)}, u32[]{:S(2)}) collective-permute-start(bf16[64,768]{1,0:T(8,128)(2,1)S(1)} %get-tuple-element.57), channel_id=1, source_target_pairs={{0,112},{16,64},{32,80},{48,96},{64,48},{80,0},{96,16},{112,32},{1... | collective-permute-start | bytes 294920 | tf_op jit(solution)/shard_map/ppermute | solution.py:18
  164.6 3.6 %collective-permute-start.20 = (bf16[64,768]{1,0:T(8,128)(2,1)S(1)}, bf16[64,768]{1,0:T(8,128)(2,1)S(1)}, u32[]{:S(2)}, u32[]{:S(2)}) collective-permute-start(bf16[64,768]{1,0:T(8,128)(2,1)S(1)} %get-tuple-element.55), channel_id=1, source_target_pairs={{0,96},{16,112},{32,64},{48,80},{64,32},{80,48},{96,0},{112,16},{1... | collective-permute-start | bytes 294920 | tf_op jit(solution)/shard_map/ppermute | solution.py:18
  168.2 3.2 %collective-permute-done.21 = bf16[64,768]{1,0:T(8,128)(2,1)S(1)} collective-permute-done((bf16[64,768]{1,0:T(8,128)(2,1)S(1)}, bf16[64,768]{1,0:T(8,128)(2,1)S(1)}, u32[]{:S(2)}, u32[]{:S(2)}) %collective-permute-start.21) | collective-permute-done | bytes 98336 | tf_op jit(solution)/shard_map/ppermute | solution.py:18
  173.6 2.0 fusion.59
  178.4 8.6 %all-to-all-start.3 = ((f32[128,8,128]{2,1,0:T(8,128)}), f32[128,8,128]{2,1,0:T(8,128)S(1)}, u32[]{:S(2)}, u32[]{:S(2)}) async-start(f32[128,8,128]{2,1,0:T(8,128)} %broadcast_in_dim.118), calls=%async_computation.3 | async-start | bytes 1048576 | tf_op jit(solution)/shard_map/all_to_all | solution.py:403
  187.7 12.9 %all-to-all-done.3 = f32[128,8,128]{2,1,0:T(8,128)S(1)} async-done(((f32[128,8,128]{2,1,0:T(8,128)}), f32[128,8,128]{2,1,0:T(8,128)S(1)}, u32[]{:S(2)}, u32[]{:S(2)}) %all-to-all-start.3) | async-done | bytes 524320 | tf_op jit(solution)/shard_map/all_to_all | solution.py:403
  (95 shorter events, 25.0 us)
Async XLA Ops:
  0.6 175.9 %copy-start = (bf16[32,64,256]{2,1,0:T(8,128)(2,1)S(1)}, bf16[32,64,256]{2,1,0:T(8,128)(2,1)}, u32[]{:S(2)}) copy-start(bf16[32,64,256]{2,1,0:T(8,128)(2,1)} %param.19) | copy-start | bytes 3145732
  22.1 16.5 %collective-permute-start.3 = (bf16[256,2048]{1,0:T(8,128)(2,1)S(1)}, bf16[256,2048]{1,0:T(8,128)(2,1)S(1)}, u32[]{:S(2)}, u32[]{:S(2)}) collective-permute-start(bf16[256,2048]{1,0:T(8,128)(2,1)S(1)} %bitcast.90), channel_id=1, source_target_pairs={{0,1},{1,0},{2,3},{3,2},{4,5},{5,4},{6,7},{7,6},{8,9},{9,8},{10,11... | collective-permute-start | bytes 3145736 | tf_op jit(solution)/shard_map/ppermute | solution.py:22
  32.9 13.8 %collective-permute-start = (bf16[64,3456]{1,0:T(8,128)(2,1)S(1)}, bf16[64,3456]{1,0:T(8,128)(2,1)S(1)}, u32[]{:S(2)}, u32[]{:S(2)}) collective-permute-start(bf16[64,3456]{1,0:T(8,128)(2,1)S(1)} %get-tuple-element.33), channel_id=1, source_target_pairs={{0,32},{16,48},{32,0},{48,16},{64,96},{80,112},{96,64},{112,80},{1... | collective-permute-start | bytes 1327112 | tf_op jit(solution)/shard_map/ppermute | solution.py:18
  35.9 20.2 %collective-permute-start.1 = (bf16[64,3456]{1,0:T(8,128)(2,1)S(1)}, bf16[64,3456]{1,0:T(8,128)(2,1)S(1)}, u32[]{:S(2)}, u32[]{:S(2)}) collective-permute-start(bf16[64,3456]{1,0:T(8,128)(2,1)S(1)} %get-tuple-element.34), channel_id=1, source_target_pairs={{0,16},{16,32},{32,48},{48,0},{64,80},{80,96},{96,112},{112,64},{1... | collective-permute-start | bytes 1327112 | tf_op jit(solution)/shard_map/ppermute | solution.py:18
  36.3 19.9 %collective-permute-start.2 = (bf16[64,3456]{1,0:T(8,128)(2,1)S(1)}, bf16[64,3456]{1,0:T(8,128)(2,1)S(1)}, u32[]{:S(2)}, u32[]{:S(2)}) collective-permute-start(bf16[64,3456]{1,0:T(8,128)(2,1)S(1)} %get-tuple-element.35), channel_id=1, source_target_pairs={{0,48},{16,0},{32,16},{48,32},{64,112},{80,64},{96,80},{112,96},{1... | collective-permute-start | bytes 1327112 | tf_op jit(solution)/shard_map/ppermute | solution.py:18
  43.2 13.1 %collective-permute-start.4 = (bf16[64,3456]{1,0:T(8,128)(2,1)S(1)}, bf16[64,3456]{1,0:T(8,128)(2,1)S(1)}, u32[]{:S(2)}, u32[]{:S(2)}) collective-permute-start(bf16[64,3456]{1,0:T(8,128)(2,1)S(1)} %get-tuple-element.40), channel_id=1, source_target_pairs={{0,64},{16,80},{32,96},{48,112},{64,0},{80,16},{96,32},{112,48},{1... | collective-permute-start | bytes 1327112 | tf_op jit(solution)/shard_map/ppermute | solution.py:18
  46.6 19.2 %collective-permute-start.5 = (bf16[64,3456]{1,0:T(8,128)(2,1)S(1)}, bf16[64,3456]{1,0:T(8,128)(2,1)S(1)}, u32[]{:S(2)}, u32[]{:S(2)}) collective-permute-start(bf16[64,3456]{1,0:T(8,128)(2,1)S(1)} %get-tuple-element.41), channel_id=1, source_target_pairs={{0,64},{16,80},{32,96},{48,112},{64,0},{80,16},{96,32},{112,48},{1... | collective-permute-start | bytes 1327112 | tf_op jit(solution)/shard_map/ppermute | solution.py:18
  66.2 7.1 %collective-permute-start.6 = (bf16[32,3456]{1,0:T(8,128)(2,1)S(1)}, bf16[32,3456]{1,0:T(8,128)(2,1)S(1)}, u32[]{:S(2)}, u32[]{:S(2)}) collective-permute-start(bf16[32,3456]{1,0:T(8,128)(2,1)S(1)} %get-tuple-element.43), channel_id=1, source_target_pairs={{0,64},{16,80},{32,96},{48,112},{64,0},{80,16},{96,32},{112,48},{1... | collective-permute-start | bytes 663560 | tf_op jit(solution)/shard_map/ppermute | solution.py:18
  68.9 6.4 %collective-permute-start.7 = (bf16[32,3456]{1,0:T(8,128)(2,1)S(1)}, bf16[32,3456]{1,0:T(8,128)(2,1)S(1)}, u32[]{:S(2)}, u32[]{:S(2)}) collective-permute-start(bf16[32,3456]{1,0:T(8,128)(2,1)S(1)} %get-tuple-element.45), channel_id=1, source_target_pairs={{0,32},{16,48},{32,0},{48,16},{64,96},{80,112},{96,64},{112,80},{1... | collective-permute-start | bytes 663560 | tf_op jit(solution)/shard_map/ppermute | solution.py:18
  68.9 12.9 %collective-permute-start.8 = (bf16[32,3456]{1,0:T(8,128)(2,1)S(1)}, bf16[32,3456]{1,0:T(8,128)(2,1)S(1)}, u32[]{:S(2)}, u32[]{:S(2)}) collective-permute-start(bf16[32,3456]{1,0:T(8,128)(2,1)S(1)} %get-tuple-element.46), channel_id=1, source_target_pairs={{0,16},{16,32},{32,48},{48,0},{64,80},{80,96},{96,112},{112,64},{1... | collective-permute-start | bytes 663560 | tf_op jit(solution)/shard_map/ppermute | solution.py:18
  69.8 12.1 %collective-permute-start.9 = (bf16[32,3456]{1,0:T(8,128)(2,1)S(1)}, bf16[32,3456]{1,0:T(8,128)(2,1)S(1)}, u32[]{:S(2)}, u32[]{:S(2)}) collective-permute-start(bf16[32,3456]{1,0:T(8,128)(2,1)S(1)} %get-tuple-element.47), channel_id=1, source_target_pairs={{0,48},{16,0},{32,16},{48,32},{64,112},{80,64},{96,80},{112,96},{1... | collective-permute-start | bytes 663560 | tf_op jit(solution)/shard_map/ppermute | solution.py:18
  82.2 5.1 %collective-permute-start.10 = (bf16[32,1664]{1,0:T(8,128)(2,1)S(1)}, bf16[32,1664]{1,0:T(8,128)(2,1)S(1)}, u32[]{:S(2)}, u32[]{:S(2)}) collective-permute-start(bf16[32,1664]{1,0:T(8,128)(2,1)S(1)} %get-tuple-element.48.a0), channel_id=1, source_target_pairs={{0,64},{16,80},{32,96},{48,112},{64,0},{80,16},{96,32},{112,48},{1... | collective-permute-start | bytes 319496 | tf_op jit(solution)/shard_map/ppermute | solution.py:18
  82.6 6.5 %collective-permute-start.11 = (bf16[32,1664]{1,0:T(8,128)(2,1)S(1)}, bf16[32,1664]{1,0:T(8,128)(2,1)S(1)}, u32[]{:S(2)}, u32[]{:S(2)}) collective-permute-start(bf16[32,1664]{1,0:T(8,128)(2,1)S(1)} %get-tuple-element.49.b0), channel_id=1, source_target_pairs={{0,16},{16,32},{32,48},{48,0},{64,80},{80,96},{96,112},{112,64},{1... | collective-permute-start | bytes 319496 | tf_op jit(solution)/shard_map/ppermute | solution.py:18
  82.6 6.5 %collective-permute-start.12 = (bf16[32,1664]{1,0:T(8,128)(2,1)S(1)}, bf16[32,1664]{1,0:T(8,128)(2,1)S(1)}, u32[]{:S(2)}, u32[]{:S(2)}) collective-permute-start(bf16[32,1664]{1,0:T(8,128)(2,1)S(1)} %get-tuple-element.49.b0), channel_id=1, source_target_pairs={{0,32},{16,48},{32,0},{48,16},{64,96},{80,112},{96,64},{112,80},{1... | collective-permute-start | bytes 319496 | tf_op jit(solution)/shard_map/ppermute | solution.py:18
  84.0 5.9 %collective-permute-start.13 = (bf16[32,1664]{1,0:T(8,128)(2,1)S(1)}, bf16[32,1664]{1,0:T(8,128)(2,1)S(1)}, u32[]{:S(2)}, u32[]{:S(2)}) collective-permute-start(bf16[32,1664]{1,0:T(8,128)(2,1)S(1)} %get-tuple-element.49.b0), channel_id=1, source_target_pairs={{0,48},{16,0},{32,16},{48,32},{64,112},{80,64},{96,80},{112,96},{1... | collective-permute-start | bytes 319496 | tf_op jit(solution)/shard_map/ppermute | solution.py:18
  89.9 13.9 %collective-permute-start.17 = (bf16[128,1664]{1,0:T(8,128)(2,1)S(1)}, bf16[128,1664]{1,0:T(8,128)(2,1)S(1)}, u32[]{:S(2)}, u32[]{:S(2)}) collective-permute-start(bf16[128,1664]{1,0:T(8,128)(2,1)S(1)} %get-tuple-element.51.refs_4_), channel_id=1, source_target_pairs={{0,64},{16,80},{32,96},{48,112},{64,0},{80,16},{96,32},{112,48},{1... | collective-permute-start | bytes 1277960 | tf_op jit(solution)/shard_map/ppermute | solution.py:18
  92.6 6.9 %collective-permute-start.14 = (bf16[64,1664]{1,0:T(8,128)(2,1)S(1)}, bf16[64,1664]{1,0:T(8,128)(2,1)S(1)}, u32[]{:S(2)}, u32[]{:S(2)}) collective-permute-start(bf16[64,1664]{1,0:T(8,128)(2,1)S(1)} %get-tuple-element.50.refs_0_), channel_id=1, source_target_pairs={{0,16},{16,32},{32,48},{48,0},{64,80},{80,96},{96,112},{112,64},{1... | collective-permute-start | bytes 638984 | tf_op jit(solution)/shard_map/ppermute | solution.py:18
  93.7 10.0 %collective-permute-start.15 = (bf16[64,1664]{1,0:T(8,128)(2,1)S(1)}, bf16[64,1664]{1,0:T(8,128)(2,1)S(1)}, u32[]{:S(2)}, u32[]{:S(2)}) collective-permute-start(bf16[64,1664]{1,0:T(8,128)(2,1)S(1)} %get-tuple-element.50.refs_0_), channel_id=1, source_target_pairs={{0,32},{16,48},{32,0},{48,16},{64,96},{80,112},{96,64},{112,80},{1... | collective-permute-start | bytes 638984 | tf_op jit(solution)/shard_map/ppermute | solution.py:18
  96.3 7.5 %collective-permute-start.16 = (bf16[64,1664]{1,0:T(8,128)(2,1)S(1)}, bf16[64,1664]{1,0:T(8,128)(2,1)S(1)}, u32[]{:S(2)}, u32[]{:S(2)}) collective-permute-start(bf16[64,1664]{1,0:T(8,128)(2,1)S(1)} %get-tuple-element.50.refs_0_), channel_id=1, source_target_pairs={{0,48},{16,0},{32,16},{48,32},{64,112},{80,64},{96,80},{112,96},{1... | collective-permute-start | bytes 638984 | tf_op jit(solution)/shard_map/ppermute | solution.py:18
  99.5 31.8 %copy-start.1 = (bf16[2,16,2048]{2,1,0:T(8,128)(2,1)S(1)}, bf16[2,16,2048]{2,1,0:T(8,128)(2,1)}, u32[]{:S(2)}) copy-start(bf16[2,16,2048]{2,1,0:T(8,128)(2,1)} %param.11) | copy-start | bytes 393220
  108.4 42.9 %copy-start.3 = (s32[256]{0:T(256)S(1)}, s32[256]{0:T(256)}, u32[]{:S(2)}) copy-start(s32[256]{0:T(256)} %param.21) | copy-start | bytes 3076
  108.4 5.6 %collective-permute-start.18 = (bf16[256,2048]{1,0:T(8,128)(2,1)S(1)}, bf16[256,2048]{1,0:T(8,128)(2,1)S(1)}, u32[]{:S(2)}, u32[]{:S(2)}) collective-permute-start(bf16[256,2048]{1,0:T(8,128)(2,1)S(1)} %get-tuple-element.53), channel_id=1, source_target_pairs={{0,1},{1,0},{2,3},{3,2},{4,5},{5,4},{6,7},{7,6},{8,9},{9,8},{10,11... | collective-permute-start | bytes 3145736 | tf_op jit(solution)/shard_map/ppermute | solution.py:22
  148.5 4.9 %collective-permute-start.19 = (bf16[256,2048]{1,0:T(8,128)(2,1)S(1)}, bf16[256,2048]{1,0:T(8,128)(2,1)S(1)}, u32[]{:S(2)}, u32[]{:S(2)}) collective-permute-start(bf16[256,2048]{1,0:T(8,128)(2,1)S(1)} %bitcast.87), channel_id=1, source_target_pairs={{0,1},{1,0},{2,3},{3,2},{4,5},{5,4},{6,7},{7,6},{8,9},{9,8},{10,11... | collective-permute-start | bytes 3145736 | tf_op jit(solution)/shard_map/ppermute | solution.py:22
  153.5 23.9 %copy-start.2 = (bf16[256,14]{0,1:T(8,128)(2,1)S(1)}, bf16[256,14]{0,1:T(8,128)(2,1)}, u32[]{:S(2)}) copy-start(bf16[256,14]{0,1:T(8,128)(2,1)} %param.17) | copy-start | bytes 21508
  156.5 7.5 %collective-permute-start.26 = (bf16[64,768]{1,0:T(8,128)(2,1)S(1)}, bf16[64,768]{1,0:T(8,128)(2,1)S(1)}, u32[]{:S(2)}, u32[]{:S(2)}) collective-permute-start(bf16[64,768]{1,0:T(8,128)(2,1)S(1)} %get-tuple-element.61), channel_id=1, source_target_pairs={{0,48},{16,0},{32,16},{48,32},{64,112},{80,64},{96,80},{112,96},{1... | collective-permute-start | bytes 294920 | tf_op jit(solution)/shard_map/ppermute | solution.py:18
  158.6 6.0 %collective-permute-start.25 = (bf16[64,768]{1,0:T(8,128)(2,1)S(1)}, bf16[64,768]{1,0:T(8,128)(2,1)S(1)}, u32[]{:S(2)}, u32[]{:S(2)}) collective-permute-start(bf16[64,768]{1,0:T(8,128)(2,1)S(1)} %get-tuple-element.60), channel_id=1, source_target_pairs={{0,16},{16,32},{32,48},{48,0},{64,80},{80,96},{96,112},{112,64},{1... | collective-permute-start | bytes 294920 | tf_op jit(solution)/shard_map/ppermute | solution.py:18
  158.7 9.6 %collective-permute-start.24 = (bf16[64,768]{1,0:T(8,128)(2,1)S(1)}, bf16[64,768]{1,0:T(8,128)(2,1)S(1)}, u32[]{:S(2)}, u32[]{:S(2)}) collective-permute-start(bf16[64,768]{1,0:T(8,128)(2,1)S(1)} %get-tuple-element.59), channel_id=1, source_target_pairs={{0,64},{16,80},{32,96},{48,112},{64,0},{80,16},{96,32},{112,48},{1... | collective-permute-start | bytes 294920 | tf_op jit(solution)/shard_map/ppermute | solution.py:18
  159.3 9.0 %collective-permute-start.23 = (bf16[64,768]{1,0:T(8,128)(2,1)S(1)}, bf16[64,768]{1,0:T(8,128)(2,1)S(1)}, u32[]{:S(2)}, u32[]{:S(2)}) collective-permute-start(bf16[64,768]{1,0:T(8,128)(2,1)S(1)} %get-tuple-element.58), channel_id=1, source_target_pairs={{0,32},{16,48},{32,0},{48,16},{64,96},{80,112},{96,64},{112,80},{1... | collective-permute-start | bytes 294920 | tf_op jit(solution)/shard_map/ppermute | solution.py:18
  160.5 7.7 %collective-permute-start.22 = (bf16[64,768]{1,0:T(8,128)(2,1)S(1)}, bf16[64,768]{1,0:T(8,128)(2,1)S(1)}, u32[]{:S(2)}, u32[]{:S(2)}) collective-permute-start(bf16[64,768]{1,0:T(8,128)(2,1)S(1)} %get-tuple-element.57), channel_id=1, source_target_pairs={{0,112},{16,64},{32,80},{48,96},{64,48},{80,0},{96,16},{112,32},{1... | collective-permute-start | bytes 294920 | tf_op jit(solution)/shard_map/ppermute | solution.py:18
  164.0 7.4 %collective-permute-start.21 = (bf16[64,768]{1,0:T(8,128)(2,1)S(1)}, bf16[64,768]{1,0:T(8,128)(2,1)S(1)}, u32[]{:S(2)}, u32[]{:S(2)}) collective-permute-start(bf16[64,768]{1,0:T(8,128)(2,1)S(1)} %get-tuple-element.56), channel_id=1, source_target_pairs={{0,80},{16,96},{32,112},{48,64},{64,16},{80,32},{96,48},{112,0},{1... | collective-permute-start | bytes 294920 | tf_op jit(solution)/shard_map/ppermute | solution.py:18
  164.6 8.3 %collective-permute-start.20 = (bf16[64,768]{1,0:T(8,128)(2,1)S(1)}, bf16[64,768]{1,0:T(8,128)(2,1)S(1)}, u32[]{:S(2)}, u32[]{:S(2)}) collective-permute-start(bf16[64,768]{1,0:T(8,128)(2,1)S(1)} %get-tuple-element.55), channel_id=1, source_target_pairs={{0,96},{16,112},{32,64},{48,80},{64,32},{80,48},{96,0},{112,16},{1... | collective-permute-start | bytes 294920 | tf_op jit(solution)/shard_map/ppermute | solution.py:18
  178.4 22.1 %all-to-all-start.3 = ((f32[128,8,128]{2,1,0:T(8,128)}), f32[128,8,128]{2,1,0:T(8,128)S(1)}, u32[]{:S(2)}, u32[]{:S(2)}) async-start(f32[128,8,128]{2,1,0:T(8,128)} %broadcast_in_dim.118), calls=%async_computation.3 | async-start | bytes 1048576 | tf_op jit(solution)/shard_map/all_to_all | solution.py:403
  (1 other events, 7.0 us)

commit v4 on v3

--- a/solution.py
+++ b/solution.py
@@ -163,54 +163,63 @@
     )(order, x, gain, w_gate, w_up)
 
 
-def small_call(kernel, outs, *arrays):
+def small_call(kernel, outs, *arrays, after=(), weight=0):
+    def body(*refs):
+        kernel(*refs[: len(arrays)], *refs[len(arrays) + len(after) :])
+
     return pl.pallas_call(
-        kernel,
+        body,
         out_shape=[jax.ShapeDtypeStruct(shape, dtype) for shape, dtype in outs],
-        in_specs=[VM] * len(arrays),
+        in_specs=[VM] * len(arrays) + [ANY] * len(after),
         out_specs=[VM] * len(outs),
         compiler_params=pltpu.CompilerParams(vmem_limit_bytes=8 * 1024 * 1024),
-    )(*arrays)
-
-
-def first_sums_kernel(a0, a1, a2, a3, b0, b1, c0, c1, keep_a, go_a, keep_b, go_b1, go_b2, go_b3):
-    unit, wide = keep_a.shape
+        cost_estimate=pl.CostEstimate(flops=weight, transcendentals=0, bytes_accessed=0) if weight else None,
+    )(*arrays, *after)
+
+
+def line_sum_kernel(a0, a1, a2, a3, keep, go):
+    unit, wide = keep.shape
     for start in range(0, wide, 128):
         at = slice(start, start + 128)
-        for lo, out in ((0, keep_a), (unit, go_a)):
+        for lo, out in ((0, keep), (unit, go)):
             rows = slice(lo, lo + unit)
             total = f32(a0[rows, at]) + f32(a1[rows, at]) + f32(a2[rows, at]) + f32(a3[rows, at])
             out[:, at] = total.astype(out.dtype)
-        for n, out in enumerate((keep_b, go_b1, go_b2, go_b3)):
-            rows = slice((n % 2) * unit, (n % 2 + 1) * unit)
-            own, came = (b0, c0) if n < 2 else (b1, c1)
-            out[:, at] = (f32(own[rows, at]) + f32(came[rows, at])).astype(out.dtype)
-
-
-def activate_kernel(keep_a, a1, keep_b, b1, b2, b3, out_a, out_b):
-    hidden = out_a.shape[1]
-    for keep, others, out in ((keep_a, (a1,), out_a), (keep_b, (b1, b2, b3), out_b)):
-
-        def summed(start):
-            at = slice(start, start + 128)
-            value = keep[:, at]
-            for other in others:
-                value = value + f32(other[:, at])
-            return value
-
-        squares = jnp.sum(summed(2 * hidden), axis=1, keepdims=True)
-        scale = lax.rsqrt(squares / D + 1e-05) * UP
-        for start in range(0, hidden, 128):
-            gate = summed(start) * scale
-            up = summed(hidden + start) * scale
-            out[:, start : start + 128] = (gate / (1.0 + jnp.exp(-gate)) * up).astype(jnp.bfloat16)
-
-
-def stack_kernel(a0, a1, b0, b1, b2, b3, out_a, out_b):
-    unit = a0.shape[0]
-    for out, parts in ((out_a, (a0, a1)), (out_b, (b0, b1, b2, b3))):
-        for n, part in enumerate(parts):
-            out[n * unit : (n + 1) * unit, :] = part[...]
+
+
+def pair_sum_kernel(b0, b1, *outs):
+    unit, wide = outs[0].shape
+    for start in range(0, wide, 128):
+        at = slice(start, start + 128)
+        for n, out in enumerate(outs):
+            rows = slice(n * unit, (n + 1) * unit)
+            out[:, at] = (f32(b0[rows, at]) + f32(b1[rows, at])).astype(out.dtype)
+
+
+def activate_kernel(keep, *refs):
+    others, out = refs[:-1], refs[-1]
+    hidden = out.shape[1]
+
+    def summed(start):
+        at = slice(start, start + 128)
+        value = keep[:, at]
+        for other in others:
+            value = value + f32(other[:, at])
+        return value
+
+    squares = jnp.sum(summed(2 * hidden), axis=1, keepdims=True)
+    scale = lax.rsqrt(squares / D + 1e-05) * UP
+    for start in range(0, hidden, 128):
+        gate = summed(start) * scale
+        up = summed(hidden + start) * scale
+        out[:, start : start + 128] = (gate / (1.0 + jnp.exp(-gate)) * up).astype(jnp.bfloat16)
+
+
+def stack_kernel(*refs):
+    parts, out = refs[:-1], refs[-1]
+    unit = parts[0].shape[0]
+    for n, part in enumerate(parts):
+        out[n * unit : (n + 1) * unit, :] = part[...]
 
 
 def down_kernel(count, order_a, order_b, *refs):
@@ -339,26 +348,23 @@
     gain = norm_gain[None, :]
     mine, other = gather_ty(own)
     *part_a, w_gate, w_up = gate_up(send_a, mine, gain, w_gate, w_up, 4, True)
-    part_b = gate_up(send_b, other, gain, w_gate, w_up, 4, False)
+    part_b = gate_up(send_b, other, gain, w_gate, w_up, 2, False)
     half_send = (unit, part_a[0].shape[1])
     came_a = [tx_move(part_a[dy], dy, 0) for dy in (2, 1, 3)]
-    came_b = [tx_move(part_b[n], 0, 1) for n in (2, 3)]
-    keep_a, go_a, keep_b, *go_b = small_call(
-        first_sums_kernel,
-        [(half_send, jnp.float32), (half_send, jnp.bfloat16), (half_send, jnp.float32)] + [(half_send, jnp.bfloat16)] * 3,
-        part_a[0], *came_a, *part_b[:2], *came_b,
-    )
+    came_b = tx_move(part_b[1], 0, 1)
+    keep = (half_send, jnp.float32)
+    go = (half_send, jnp.bfloat16)
+    keep_a, go_a = small_call(line_sum_kernel, [keep, go], part_a[0], *came_a, weight=5000000000)
+    keep_b, *go_b = small_call(pair_sum_kernel, [keep, go, go, go], part_b[0], came_b, after=(go_a,))
     came_b = [tx_move(go_b[dy - 1], dy, 0) for dy in (2, 1, 3)]
     came_a = tx_move(go_a, 0, 1)
     half_hidden = ((unit, hidden_here), jnp.bfloat16)
-    hidden_a, hidden_b = small_call(activate_kernel, [half_hidden] * 2, keep_a, came_a, keep_b, *came_b)
-    came_b = [tx_move(hidden_b, dy, 0) for dy in (1, 2, 3)]
+    (hidden_a,) = small_call(activate_kernel, [half_hidden], keep_a, came_a)
     came_a = tx_move(hidden_a, 0, 1)
-    pair_a, line_b = small_call(
-        stack_kernel,
-        [((2 * unit, hidden_here), jnp.bfloat16), ((4 * unit, hidden_here), jnp.bfloat16)],
-        hidden_a, came_a, hidden_b, *came_b,
-    )
+    (pair_a,) = small_call(stack_kernel, [((2 * unit, hidden_here), jnp.bfloat16)], hidden_a, came_a)
+    (hidden_b,) = small_call(activate_kernel, [half_hidden], keep_b, *came_b, after=(pair_a,))
+    came_b = [tx_move(hidden_b, dy, 0) for dy in (2, 1, 3)]
+    (line_b,) = small_call(stack_kernel, [((4 * unit, hidden_here), jnp.bfloat16)], hidden_b, came_b[1], came_b[0], came_b[2])
     pieces_a = [pair_a] + [tx_move(pair_a, dy, 0) for dy in (1, 2, 3)]
     pieces_b = [line_b, tx_move(line_b, 0, 1)]
     w_down = fetch(w_down, 4, pair_a)

time: 202 us -> 198 us (0.980)
  waiting for transfers between devices: 58 us -> 51.3 us
  starting transfers between devices: 52.2 us -> 54.4 us
    ppermute x24 -> x23, waiting for transfers between devices: 42.9 us -> 36.2 us  [tx_move(): return lax.ppermute(array, 'tx', pairs)]
    ppermute x24 -> x23, starting transfers between devices: 35.6 us -> 37.1 us  [tx_move(): return lax.ppermute(array, 'tx', pairs)]
  transfers between devices with their start and end apart: 28 -> 27, of which waited for: 16 -> 14; matrix products, arithmetic and copies ran while one was open for 1% -> 1% of each run, Pallas kernels for 9% -> 9%
where the time goes in v4:
time: 198 us; the launch traced here: 197 us
  starting transfers between devices  54.4 us (27%)
  blocking collectives  54.1 us (27%)
  waiting for transfers between devices  51.3 us (26%)
  Pallas kernels  26 us (13%)
  local copies, waits for them, and re-layouts  4.76 us (2%)
  matrix products  3.17 us (2%)
  other arithmetic  2.5 us (1%)
    all_to_all x3, blocking collectives, chip_exchange(): return lax.all_to_all(blocks, 'ty', 0, 0, axis_index_groups=groups)  54.1 us
    ppermute x23, starting transfers between devices, tx_move(): return lax.ppermute(array, 'tx', pairs)  37.1 us
    ppermute x23, waiting for transfers between devices, tx_move(): return lax.ppermute(array, 'tx', pairs)  36.2 us
    all_to_all x1, waiting for transfers between devices, per_device(): lax.all_to_all(jnp.broadcast_to(packed[None], (128,) + packed.shape), ('t...  12.9 us
    pallas_call x2, Pallas kernels, gate_up(): pl.pallas_call(load_gate_up_kernel if load else gate_up_kernel, out_shape...  12.6 us
    ppermute x3, starting transfers between devices, core_swap(): return lax.ppermute(array, 'ty', [(n, n ^ 1) for n in range(16)])  8.91 us
    all_to_all x1, starting transfers between devices, per_device(): lax.all_to_all(jnp.broadcast_to(packed[None], (128,) + packed.shape), ('t...  8.31 us
    pallas_call x2, Pallas kernels, fetch(): pl.pallas_call(fetch_kernel, out_shape=pltpu.VMEM(array.shape, array.dtyp...  4.92 us
  transfers between devices with their start and end apart: 27, of which 14 were waited for; matrix products, arithmetic and copies ran while one was open for 1% of the time, Pallas kernels for 9%

profile of v4, /device:TPU:1, one launch (start us, length us, event | category | flops | bytes accessed | tf_op | source)
XLA Modules:
  0.0 197.2 jit_solution(2917014879450320063)
XLA Ops:
  1.8 20.3 %all_to_all.20 = bf16[8,32,2048]{2,1,0:T(8,128)(2,1)S(1)} all-to-all(bf16[8,32,2048]{2,1,0:T(8,128)(2,1)S(1)} %broadcast_in_dim.101), channel_id=1, replica_groups={{0,2,4,6,8,10,12,14},{1,3,5,7,9,11,13,15},{16,18,20,22,24,26,28,30},{17..., dimensions={0} | all-to-all | bytes 2097152 | tf_op jit(solution)/shard_map/all_to_all | solution.py:27
  22.1 2.0 %collective-permute-start.8 = (bf16[256,2048]{1,0:T(8,128)(2,1)S(1)}, bf16[256,2048]{1,0:T(8,128)(2,1)S(1)}, u32[]{:S(2)}, u32[]{:S(2)}) collective-permute-start(bf16[256,2048]{1,0:T(8,128)(2,1)S(1)} %bitcast.90), channel_id=1, source_target_pairs={{0,1},{1,0},{2,3},{3,2},{4,5},{5,4},{6,7},{7,6},{8,9},{9,8},{10,11... | collective-permute-start | bytes 3145736 | tf_op jit(solution)/shard_map/ppermute | solution.py:22
  24.9 8.0 %shard_map.122 = (bf16[64,3456]{1,0:T(8,128)(2,1)S(1)}, bf16[64,3456]{1,0:T(8,128)(2,1)S(1)}, bf16[64,3456]{1,0:T(8,128)(2,1)S(1)}, bf16[64,3456]{1,0:T(8,128)(2...) custom-call(s32[8]{0:T(128)S(1)} %stack.76.order, bf16[256,2048]{1,0:T(8,128)(2,1)S(1)} %bitcast.91, ...), custom_call_target="tpu_custom_call" | custom-call | flops 3489660928 | bytes 15335424 | tf_op jit(solution)/shard_map/pallas_call | solution.py:153
  32.9 3.0 %collective-permute-start = (bf16[64,3456]{1,0:T(8,128)(2,1)S(1)}, bf16[64,3456]{1,0:T(8,128)(2,1)S(1)}, u32[]{:S(2)}, u32[]{:S(2)}) collective-permute-start(bf16[64,3456]{1,0:T(8,128)(2,1)S(1)} %get-tuple-element.27), channel_id=1, source_target_pairs={{0,32},{16,48},{32,0},{48,16},{64,96},{80,112},{96,64},{112,80},{1... | collective-permute-start | bytes 1327112 | tf_op jit(solution)/shard_map/ppermute | solution.py:18
  36.3 2.3 %collective-permute-start.2 = (bf16[64,3456]{1,0:T(8,128)(2,1)S(1)}, bf16[64,3456]{1,0:T(8,128)(2,1)S(1)}, u32[]{:S(2)}, u32[]{:S(2)}) collective-permute-start(bf16[64,3456]{1,0:T(8,128)(2,1)S(1)} %get-tuple-element.29), channel_id=1, source_target_pairs={{0,48},{16,0},{32,16},{48,32},{64,112},{80,64},{96,80},{112,96},{1... | collective-permute-start | bytes 1327112 | tf_op jit(solution)/shard_map/ppermute | solution.py:18
  38.6 4.6 %shard_map.126 = (bf16[128,3456]{1,0:T(8,128)(2,1)S(1)}, bf16[128,3456]{1,0:T(8,128)(2,1)S(1)}) custom-call(s32[8]{0:T(128)S(1)} %stack.77.order, bf16[256,2048]{1,0:T(8,128)(2,1)S(1)} %collective-permute-done.8.x_ref, bf16[1,2048]{1,0:T(2,128)(2,1)S(1)} %broadcast_in_dim.102.gain_ref, bf16[2048,1664]{1,0:T(8,128)(2,1)S(1)} %get-tuple-element.32.wg_ref, ...), custom_call_target="tpu_custom_call" | custom-call | flops 3489660928 | bytes 15335424 | tf_op jit(solution)/shard_map/pallas_call | solution.py:153
  43.2 3.4 %collective-permute-start.9 = (bf16[128,3456]{1,0:T(8,128)(2,1)S(1)}, bf16[128,3456]{1,0:T(8,128)(2,1)S(1)}, u32[]{:S(2)}, u32[]{:S(2)}) collective-permute-start(bf16[128,3456]{1,0:T(8,128)(2,1)S(1)} %get-tuple-element.35), channel_id=1, source_target_pairs={{0,64},{16,80},{32,96},{48,112},{64,0},{80,16},{96,32},{112,48},{1... | collective-permute-start | bytes 2654216 | tf_op jit(solution)/shard_map/ppermute | solution.py:18
  46.6 9.5 %collective-permute-done.1.refs_2_ = bf16[64,3456]{1,0:T(8,128)(2,1)S(1)} collective-permute-done((bf16[64,3456]{1,0:T(8,128)(2,1)S(1)}, bf16[64,3456]{1,0:T(8,128)(2,1)S(1)}, u32[]{:S(2)}, u32[]{:S(2)}) %collective-permute-start.1) | collective-permute-done | bytes 442400 | tf_op jit(solution)/shard_map/ppermute | solution.py:18
  56.4 3.4 %collective-permute-start.3 = (bf16[32,3456]{1,0:T(8,128)(2,1)S(1)}, bf16[32,3456]{1,0:T(8,128)(2,1)S(1)}, u32[]{:S(2)}, u32[]{:S(2)}) collective-permute-start(bf16[32,3456]{1,0:T(8,128)(2,1)S(1)} %get-tuple-element.31.refs_2_), channel_id=1, source_target_pairs={{0,64},{16,80},{32,96},{48,112},{64,0},{80,16},{96,32},{112,48},{1... | collective-permute-start | bytes 663560 | tf_op jit(solution)/shard_map/ppermute | solution.py:18
  59.8 6.0 %collective-permute-done.9.refs_1_ = bf16[128,3456]{1,0:T(8,128)(2,1)S(1)} collective-permute-done((bf16[128,3456]{1,0:T(8,128)(2,1)S(1)}, bf16[128,3456]{1,0:T(8,128)(2,1)S(1)}, u32[]{:S(2)}, u32[]{:S(2)}) %collective-permute-start.9) | collective-permute-done | bytes 884768 | tf_op jit(solution)/shard_map/ppermute | solution.py:18
  70.7 2.7 %collective-permute-start.4 = (bf16[32,1664]{1,0:T(8,128)(2,1)S(1)}, bf16[32,1664]{1,0:T(8,128)(2,1)S(1)}, u32[]{:S(2)}, u32[]{:S(2)}) collective-permute-start(bf16[32,1664]{1,0:T(8,128)(2,1)S(1)} %shard_map.124.refs_0_), channel_id=1, source_target_pairs={{0,64},{16,80},{32,96},{48,112},{64,0},{80,16},{96,32},{112,48},{1... | collective-permute-start | bytes 319496 | tf_op jit(solution)/shard_map/ppermute | solution.py:18
  73.4 2.7 %collective-permute-done.4.refs_1_ = bf16[32,1664]{1,0:T(8,128)(2,1)S(1)} collective-permute-done((bf16[32,1664]{1,0:T(8,128)(2,1)S(1)}, bf16[32,1664]{1,0:T(8,128)(2,1)S(1)}, u32[]{:S(2)}, u32[]{:S(2)}) %collective-permute-start.4) | collective-permute-done | bytes 106528 | tf_op jit(solution)/shard_map/ppermute | solution.py:18
  76.2 2.8 %collective-permute-done.11.refs_2_ = bf16[32,3456]{1,0:T(8,128)(2,1)S(1)} collective-permute-done((bf16[32,3456]{1,0:T(8,128)(2,1)S(1)}, bf16[32,3456]{1,0:T(8,128)(2,1)S(1)}, u32[]{:S(2)}, u32[]{:S(2)}) %collective-permute-start.11) | collective-permute-done | bytes 221216 | tf_op jit(solution)/shard_map/ppermute | solution.py:18
  81.9 3.7 %collective-permute-done.13.refs_1_ = bf16[32,1664]{1,0:T(8,128)(2,1)S(1)} collective-permute-done((bf16[32,1664]{1,0:T(8,128)(2,1)S(1)}, bf16[32,1664]{1,0:T(8,128)(2,1)S(1)}, u32[]{:S(2)}, u32[]{:S(2)}) %collective-permute-start.13) | collective-permute-done | bytes 106528 | tf_op jit(solution)/shard_map/ppermute | solution.py:18
  88.2 2.9 %collective-permute-start.6 = (bf16[64,1664]{1,0:T(8,128)(2,1)S(1)}, bf16[64,1664]{1,0:T(8,128)(2,1)S(1)}, u32[]{:S(2)}, u32[]{:S(2)}) collective-permute-start(bf16[64,1664]{1,0:T(8,128)(2,1)S(1)} %shard_map.125.refs_4_.refs_0_), channel_id=1, source_target_pairs={{0,32},{16,48},{32,0},{48,16},{64,96},{80,112},{96,64},{112,80},{1... | collective-permute-start | bytes 638984 | tf_op jit(solution)/shard_map/ppermute | solution.py:18
  91.3 3.0 %shard_map.130.refs_6_ = bf16[1664,2048]{1,0:T(8,128)(2,1)S(1)} custom-call(bf16[1664,2048]{1,0:T(8,128)(2,1)} %source.1, bf16[64,1664]{1,0:T(8,128)(2,1)S(1)} %shard_map.125.refs_4_.refs_0_), custom_call_target="tpu_custom_call" | custom-call | tf_op jit(solution)/shard_map/pallas_call | solution.py:58
  94.4 3.0 %collective-permute-done.6.refs_2_ = bf16[64,1664]{1,0:T(8,128)(2,1)S(1)} collective-permute-done((bf16[64,1664]{1,0:T(8,128)(2,1)S(1)}, bf16[64,1664]{1,0:T(8,128)(2,1)S(1)}, u32[]{:S(2)}, u32[]{:S(2)}) %collective-permute-start.6) | collective-permute-done | bytes 213024 | tf_op jit(solution)/shard_map/ppermute | solution.py:18
  98.1 4.6 %shard_map.131 = (bf16[256,2048]{1,0:T(8,128)(2,1)S(1)}, bf16[256,2048]{1,0:T(8,128)(2,1)S(1)}) custom-call(s32[8]{0:T(128)S(1)} %stack.72.order_a, s32[8]{0:T(128)S(1)} %stack.73.order_b, bf16[64,1664]{1,0:T(8,128)(2,1)S(1)} %shard_map.125.refs_4_.refs_0_, bf16[64,1664]{1,0:T(8,128)(2,1)S(1)} %collective-permute-done.5.refs_1_, ...), custom_call_target="tpu_custom_call" | custom-call | tf_op jit(solution)/shard_map/pallas_call | solution.py:246
  102.7 4.3 %collective-permute-start.17 = (bf16[256,2048]{1,0:T(8,128)(2,1)S(1)}, bf16[256,2048]{1,0:T(8,128)(2,1)S(1)}, u32[]{:S(2)}, u32[]{:S(2)}) collective-permute-start(bf16[256,2048]{1,0:T(8,128)(2,1)S(1)} %get-tuple-element.41), channel_id=1, source_target_pairs={{0,1},{1,0},{2,3},{3,2},{4,5},{5,4},{6,7},{7,6},{8,9},{9,8},{10,11... | collective-permute-start | bytes 3145736 | tf_op jit(solution)/shard_map/ppermute | solution.py:22
  107.0 2.3 %collective-permute-done.17 = bf16[256,2048]{1,0:T(8,128)(2,1)S(1)} collective-permute-done((bf16[256,2048]{1,0:T(8,128)(2,1)S(1)}, bf16[256,2048]{1,0:T(8,128)(2,1)S(1)}, u32[]{:S(2)}, u32[]{:S(2)}) %collective-permute-start.17) | collective-permute-done | bytes 1048608 | tf_op jit(solution)/shard_map/ppermute | solution.py:22
  109.7 16.7 %all_to_all.21 = bf16[8,32,2048]{2,1,0:T(8,128)(2,1)S(1)} all-to-all(bf16[8,32,2048]{2,1,0:T(8,128)(2,1)S(1)} %bitcast.92), channel_id=1, replica_groups={{0,2,4,6,8,10,12,14},{1,3,5,7,9,11,13,15},{16,18,20,22,24,26,28,30},{17..., dimensions={0} | all-to-all | bytes 2097152 | tf_op jit(solution)/shard_map/all_to_all | solution.py:27
  126.7 17.1 %all_to_all.22 = bf16[8,32,2048]{2,1,0:T(8,128)(2,1)S(1)} all-to-all(bf16[8,32,2048]{2,1,0:T(8,128)(2,1)S(1)} %broadcast_in_dim.104), channel_id=1, replica_groups={{0,2,4,6,8,10,12,14},{1,3,5,7,9,11,13,15},{16,18,20,22,24,26,28,30},{17..., dimensions={0} | all-to-all | bytes 2097152 | tf_op jit(solution)/shard_map/all_to_all | solution.py:27
  143.7 2.6 %collective-permute-start.18 = (bf16[256,2048]{1,0:T(8,128)(2,1)S(1)}, bf16[256,2048]{1,0:T(8,128)(2,1)S(1)}, u32[]{:S(2)}, u32[]{:S(2)}) collective-permute-start(bf16[256,2048]{1,0:T(8,128)(2,1)S(1)} %bitcast.87), channel_id=1, source_target_pairs={{0,1},{1,0},{2,3},{3,2},{4,5},{5,4},{6,7},{7,6},{8,9},{9,8},{10,11... | collective-permute-start | bytes 3145736 | tf_op jit(solution)/shard_map/ppermute | solution.py:22
  148.7 3.1 %shard_map.133 = (bf16[64,768]{1,0:T(8,128)(2,1)S(1)}, bf16[64,768]{1,0:T(8,128)(2,1)S(1)}, bf16[64,768]{1,0:T(8,128)(2,1)S(1)}, bf16[64,768]{1,0:T(8,128)(2,1)S...) custom-call(bf16[256,2048]{1,0:T(8,128)(2,1)S(1)} %bitcast.89, ...), custom_call_target="tpu_custom_call" | custom-call | flops 2684354560 | bytes 5242880 | tf_op jit(solution)/shard_map/pallas_call | solution.py:275
  151.8 2.4 %collective-permute-start.25 = (bf16[64,768]{1,0:T(8,128)(2,1)S(1)}, bf16[64,768]{1,0:T(8,128)(2,1)S(1)}, u32[]{:S(2)}, u32[]{:S(2)}) collective-permute-start(bf16[64,768]{1,0:T(8,128)(2,1)S(1)} %get-tuple-element.49), channel_id=1, source_target_pairs={{0,48},{16,0},{32,16},{48,32},{64,112},{80,64},{96,80},{112,96},{1... | collective-permute-start | bytes 294920 | tf_op jit(solution)/shard_map/ppermute | solution.py:18
  157.4 2.2 %collective-permute-start.21 = (bf16[64,768]{1,0:T(8,128)(2,1)S(1)}, bf16[64,768]{1,0:T(8,128)(2,1)S(1)}, u32[]{:S(2)}, u32[]{:S(2)}) collective-permute-start(bf16[64,768]{1,0:T(8,128)(2,1)S(1)} %get-tuple-element.45), channel_id=1, source_target_pairs={{0,112},{16,64},{32,80},{48,96},{64,48},{80,0},{96,16},{112,32},{1... | collective-permute-start | bytes 294920 | tf_op jit(solution)/shard_map/ppermute | solution.py:18
  161.2 2.5 %collective-permute-start.19 = (bf16[64,768]{1,0:T(8,128)(2,1)S(1)}, bf16[64,768]{1,0:T(8,128)(2,1)S(1)}, u32[]{:S(2)}, u32[]{:S(2)}) collective-permute-start(bf16[64,768]{1,0:T(8,128)(2,1)S(1)} %get-tuple-element.43), channel_id=1, source_target_pairs={{0,96},{16,112},{32,64},{48,80},{64,32},{80,48},{96,0},{112,16},{1... | collective-permute-start | bytes 294920 | tf_op jit(solution)/shard_map/ppermute | solution.py:18
  163.8 2.9 %collective-permute-done.20 = bf16[64,768]{1,0:T(8,128)(2,1)S(1)} collective-permute-done((bf16[64,768]{1,0:T(8,128)(2,1)S(1)}, bf16[64,768]{1,0:T(8,128)(2,1)S(1)}, u32[]{:S(2)}, u32[]{:S(2)}) %collective-permute-start.20) | collective-permute-done | bytes 98336 | tf_op jit(solution)/shard_map/ppermute | solution.py:18
  166.7 2.1 %collective-permute-done.19 = bf16[64,768]{1,0:T(8,128)(2,1)S(1)} collective-permute-done((bf16[64,768]{1,0:T(8,128)(2,1)S(1)}, bf16[64,768]{1,0:T(8,128)(2,1)S(1)}, u32[]{:S(2)}, u32[]{:S(2)}) %collective-permute-start.19) | collective-permute-done | bytes 98336 | tf_op jit(solution)/shard_map/ppermute | solution.py:18
  169.5 2.0 %fusion.59 = (f32[2,32,2]{0,2,1:T(2,128)S(1)}, f32[2,32,2,64]{3,0,2,1:T(2,128)S(1)}) fusion(bf16[2,32,1,2,128]{4,3,2,1,0:T(2,128)(2,1)S(1)} %get-tuple-element.64, pred[32,64]{1,0:T(8,128)(4,1)S(1)} %iota_compare_fusion.2, bf16[32,64,256]{2,1,0:T(8,128)(2,1)} %param.18), kind=kOutput, calls=%fused_computation.111 | convolution fusion | flops 2121600 | bytes 1116672 | tf_op jit(solution)/shard_map/tshd,slhd->tshl/dot_general | solution.py:388
  174.2 8.3 %all-to-all-start.3 = ((f32[128,8,128]{2,1,0:T(8,128)}), f32[128,8,128]{2,1,0:T(8,128)S(1)}, u32[]{:S(2)}, u32[]{:S(2)}) async-start(f32[128,8,128]{2,1,0:T(8,128)} %broadcast_in_dim.118), calls=%async_computation.3 | async-start | bytes 1048576 | tf_op jit(solution)/shard_map/all_to_all | solution.py:409
  183.2 12.9 %all-to-all-done.3 = f32[128,8,128]{2,1,0:T(8,128)S(1)} async-done(((f32[128,8,128]{2,1,0:T(8,128)}), f32[128,8,128]{2,1,0:T(8,128)S(1)}, u32[]{:S(2)}, u32[]{:S(2)}) %all-to-all-start.3) | async-done | bytes 524320 | tf_op jit(solution)/shard_map/all_to_all | solution.py:409
  (96 shorter events, 27.2 us)
Async XLA Ops:
  0.6 171.8 %copy-start = (bf16[32,64,256]{2,1,0:T(8,128)(2,1)S(1)}, bf16[32,64,256]{2,1,0:T(8,128)(2,1)}, u32[]{:S(2)}) copy-start(bf16[32,64,256]{2,1,0:T(8,128)(2,1)} %param.19) | copy-start | bytes 3145732
  22.1 16.5 %collective-permute-start.8 = (bf16[256,2048]{1,0:T(8,128)(2,1)S(1)}, bf16[256,2048]{1,0:T(8,128)(2,1)S(1)}, u32[]{:S(2)}, u32[]{:S(2)}) collective-permute-start(bf16[256,2048]{1,0:T(8,128)(2,1)S(1)} %bitcast.90), channel_id=1, source_target_pairs={{0,1},{1,0},{2,3},{3,2},{4,5},{5,4},{6,7},{7,6},{8,9},{9,8},{10,11... | collective-permute-start | bytes 3145736 | tf_op jit(solution)/shard_map/ppermute | solution.py:22
  32.9 13.7 %collective-permute-start = (bf16[64,3456]{1,0:T(8,128)(2,1)S(1)}, bf16[64,3456]{1,0:T(8,128)(2,1)S(1)}, u32[]{:S(2)}, u32[]{:S(2)}) collective-permute-start(bf16[64,3456]{1,0:T(8,128)(2,1)S(1)} %get-tuple-element.27), channel_id=1, source_target_pairs={{0,32},{16,48},{32,0},{48,16},{64,96},{80,112},{96,64},{112,80},{1... | collective-permute-start | bytes 1327112 | tf_op jit(solution)/shard_map/ppermute | solution.py:18
  35.9 20.2 %collective-permute-start.1 = (bf16[64,3456]{1,0:T(8,128)(2,1)S(1)}, bf16[64,3456]{1,0:T(8,128)(2,1)S(1)}, u32[]{:S(2)}, u32[]{:S(2)}) collective-permute-start(bf16[64,3456]{1,0:T(8,128)(2,1)S(1)} %get-tuple-element.28), channel_id=1, source_target_pairs={{0,16},{16,32},{32,48},{48,0},{64,80},{80,96},{96,112},{112,64},{1... | collective-permute-start | bytes 1327112 | tf_op jit(solution)/shard_map/ppermute | solution.py:18
  36.3 19.9 %collective-permute-start.2 = (bf16[64,3456]{1,0:T(8,128)(2,1)S(1)}, bf16[64,3456]{1,0:T(8,128)(2,1)S(1)}, u32[]{:S(2)}, u32[]{:S(2)}) collective-permute-start(bf16[64,3456]{1,0:T(8,128)(2,1)S(1)} %get-tuple-element.29), channel_id=1, source_target_pairs={{0,48},{16,0},{32,16},{48,32},{64,112},{80,64},{96,80},{112,96},{1... | collective-permute-start | bytes 1327112 | tf_op jit(solution)/shard_map/ppermute | solution.py:18
  43.2 22.6 %collective-permute-start.9 = (bf16[128,3456]{1,0:T(8,128)(2,1)S(1)}, bf16[128,3456]{1,0:T(8,128)(2,1)S(1)}, u32[]{:S(2)}, u32[]{:S(2)}) collective-permute-start(bf16[128,3456]{1,0:T(8,128)(2,1)S(1)} %get-tuple-element.35), channel_id=1, source_target_pairs={{0,64},{16,80},{32,96},{48,112},{64,0},{80,16},{96,32},{112,48},{1... | collective-permute-start | bytes 2654216 | tf_op jit(solution)/shard_map/ppermute | solution.py:18
  56.4 14.1 %collective-permute-start.3 = (bf16[32,3456]{1,0:T(8,128)(2,1)S(1)}, bf16[32,3456]{1,0:T(8,128)(2,1)S(1)}, u32[]{:S(2)}, u32[]{:S(2)}) collective-permute-start(bf16[32,3456]{1,0:T(8,128)(2,1)S(1)} %get-tuple-element.31.refs_2_), channel_id=1, source_target_pairs={{0,64},{16,80},{32,96},{48,112},{64,0},{80,16},{96,32},{112,48},{1... | collective-permute-start | bytes 663560 | tf_op jit(solution)/shard_map/ppermute | solution.py:18
  66.0 10.2 %collective-permute-start.10 = (bf16[32,3456]{1,0:T(8,128)(2,1)S(1)}, bf16[32,3456]{1,0:T(8,128)(2,1)S(1)}, u32[]{:S(2)}, u32[]{:S(2)}) collective-permute-start(bf16[32,3456]{1,0:T(8,128)(2,1)S(1)} %get-tuple-element.37), channel_id=1, source_target_pairs={{0,32},{16,48},{32,0},{48,16},{64,96},{80,112},{96,64},{112,80},{1... | collective-permute-start | bytes 663560 | tf_op jit(solution)/shard_map/ppermute | solution.py:18
  66.1 12.9 %collective-permute-start.11 = (bf16[32,3456]{1,0:T(8,128)(2,1)S(1)}, bf16[32,3456]{1,0:T(8,128)(2,1)S(1)}, u32[]{:S(2)}, u32[]{:S(2)}) collective-permute-start(bf16[32,3456]{1,0:T(8,128)(2,1)S(1)} %get-tuple-element.38), channel_id=1, source_target_pairs={{0,16},{16,32},{32,48},{48,0},{64,80},{80,96},{96,112},{112,64},{1... | collective-permute-start | bytes 663560 | tf_op jit(solution)/shard_map/ppermute | solution.py:18
  67.0 12.0 %collective-permute-start.12 = (bf16[32,3456]{1,0:T(8,128)(2,1)S(1)}, bf16[32,3456]{1,0:T(8,128)(2,1)S(1)}, u32[]{:S(2)}, u32[]{:S(2)}) collective-permute-start(bf16[32,3456]{1,0:T(8,128)(2,1)S(1)} %get-tuple-element.39), channel_id=1, source_target_pairs={{0,48},{16,0},{32,16},{48,32},{64,112},{80,64},{96,80},{112,96},{1... | collective-permute-start | bytes 663560 | tf_op jit(solution)/shard_map/ppermute | solution.py:18
  70.7 5.4 %collective-permute-start.4 = (bf16[32,1664]{1,0:T(8,128)(2,1)S(1)}, bf16[32,1664]{1,0:T(8,128)(2,1)S(1)}, u32[]{:S(2)}, u32[]{:S(2)}) collective-permute-start(bf16[32,1664]{1,0:T(8,128)(2,1)S(1)} %shard_map.124.refs_0_), channel_id=1, source_target_pairs={{0,64},{16,80},{32,96},{48,112},{64,0},{80,16},{96,32},{112,48},{1... | collective-permute-start | bytes 319496 | tf_op jit(solution)/shard_map/ppermute | solution.py:18
  79.1 6.4 %collective-permute-start.13 = (bf16[32,1664]{1,0:T(8,128)(2,1)S(1)}, bf16[32,1664]{1,0:T(8,128)(2,1)S(1)}, u32[]{:S(2)}, u32[]{:S(2)}) collective-permute-start(bf16[32,1664]{1,0:T(8,128)(2,1)S(1)} %shard_map.128.refs_0_), channel_id=1, source_target_pairs={{0,16},{16,32},{32,48},{48,0},{64,80},{80,96},{96,112},{112,64},{1... | collective-permute-start | bytes 319496 | tf_op jit(solution)/shard_map/ppermute | solution.py:18
  79.2 6.3 %collective-permute-start.14 = (bf16[32,1664]{1,0:T(8,128)(2,1)S(1)}, bf16[32,1664]{1,0:T(8,128)(2,1)S(1)}, u32[]{:S(2)}, u32[]{:S(2)}) collective-permute-start(bf16[32,1664]{1,0:T(8,128)(2,1)S(1)} %shard_map.128.refs_0_), channel_id=1, source_target_pairs={{0,32},{16,48},{32,0},{48,16},{64,96},{80,112},{96,64},{112,80},{1... | collective-permute-start | bytes 319496 | tf_op jit(solution)/shard_map/ppermute | solution.py:18
  80.0 6.6 %collective-permute-start.15 = (bf16[32,1664]{1,0:T(8,128)(2,1)S(1)}, bf16[32,1664]{1,0:T(8,128)(2,1)S(1)}, u32[]{:S(2)}, u32[]{:S(2)}) collective-permute-start(bf16[32,1664]{1,0:T(8,128)(2,1)S(1)} %shard_map.128.refs_0_), channel_id=1, source_target_pairs={{0,48},{16,0},{32,16},{48,32},{64,112},{80,64},{96,80},{112,96},{1... | collective-permute-start | bytes 319496 | tf_op jit(solution)/shard_map/ppermute | solution.py:18
  86.6 11.5 %collective-permute-start.16 = (bf16[128,1664]{1,0:T(8,128)(2,1)S(1)}, bf16[128,1664]{1,0:T(8,128)(2,1)S(1)}, u32[]{:S(2)}, u32[]{:S(2)}) collective-permute-start(bf16[128,1664]{1,0:T(8,128)(2,1)S(1)} %shard_map.129.refs_4_), channel_id=1, source_target_pairs={{0,64},{16,80},{32,96},{48,112},{64,0},{80,16},{96,32},{112,48},{1... | collective-permute-start | bytes 1277960 | tf_op jit(solution)/shard_map/ppermute | solution.py:18
  88.2 6.2 %collective-permute-start.5 = (bf16[64,1664]{1,0:T(8,128)(2,1)S(1)}, bf16[64,1664]{1,0:T(8,128)(2,1)S(1)}, u32[]{:S(2)}, u32[]{:S(2)}) collective-permute-start(bf16[64,1664]{1,0:T(8,128)(2,1)S(1)} %shard_map.125.refs_4_.refs_0_), channel_id=1, source_target_pairs={{0,16},{16,32},{32,48},{48,0},{64,80},{80,96},{96,112},{112,64},{1... | collective-permute-start | bytes 638984 | tf_op jit(solution)/shard_map/ppermute | solution.py:18
  88.2 9.2 %collective-permute-start.6 = (bf16[64,1664]{1,0:T(8,128)(2,1)S(1)}, bf16[64,1664]{1,0:T(8,128)(2,1)S(1)}, u32[]{:S(2)}, u32[]{:S(2)}) collective-permute-start(bf16[64,1664]{1,0:T(8,128)(2,1)S(1)} %shard_map.125.refs_4_.refs_0_), channel_id=1, source_target_pairs={{0,32},{16,48},{32,0},{48,16},{64,96},{80,112},{96,64},{112,80},{1... | collective-permute-start | bytes 638984 | tf_op jit(solution)/shard_map/ppermute | solution.py:18
  91.1 7.0 %collective-permute-start.7 = (bf16[64,1664]{1,0:T(8,128)(2,1)S(1)}, bf16[64,1664]{1,0:T(8,128)(2,1)S(1)}, u32[]{:S(2)}, u32[]{:S(2)}) collective-permute-start(bf16[64,1664]{1,0:T(8,128)(2,1)S(1)} %shard_map.125.refs_4_.refs_0_), channel_id=1, source_target_pairs={{0,48},{16,0},{32,16},{48,32},{64,112},{80,64},{96,80},{112,96},{1... | collective-permute-start | bytes 638984 | tf_op jit(solution)/shard_map/ppermute | solution.py:18
  94.3 32.2 %copy-start.1 = (bf16[2,16,2048]{2,1,0:T(8,128)(2,1)S(1)}, bf16[2,16,2048]{2,1,0:T(8,128)(2,1)}, u32[]{:S(2)}) copy-start(bf16[2,16,2048]{2,1,0:T(8,128)(2,1)} %param.11) | copy-start | bytes 393220
  102.7 43.8 %copy-start.3 = (s32[256]{0:T(256)S(1)}, s32[256]{0:T(256)}, u32[]{:S(2)}) copy-start(s32[256]{0:T(256)} %param.21) | copy-start | bytes 3076
  102.7 6.6 %collective-permute-start.17 = (bf16[256,2048]{1,0:T(8,128)(2,1)S(1)}, bf16[256,2048]{1,0:T(8,128)(2,1)S(1)}, u32[]{:S(2)}, u32[]{:S(2)}) collective-permute-start(bf16[256,2048]{1,0:T(8,128)(2,1)S(1)} %get-tuple-element.41), channel_id=1, source_target_pairs={{0,1},{1,0},{2,3},{3,2},{4,5},{5,4},{6,7},{7,6},{8,9},{9,8},{10,11... | collective-permute-start | bytes 3145736 | tf_op jit(solution)/shard_map/ppermute | solution.py:22
  143.7 4.9 %collective-permute-start.18 = (bf16[256,2048]{1,0:T(8,128)(2,1)S(1)}, bf16[256,2048]{1,0:T(8,128)(2,1)S(1)}, u32[]{:S(2)}, u32[]{:S(2)}) collective-permute-start(bf16[256,2048]{1,0:T(8,128)(2,1)S(1)} %bitcast.87), channel_id=1, source_target_pairs={{0,1},{1,0},{2,3},{3,2},{4,5},{5,4},{6,7},{7,6},{8,9},{9,8},{10,11... | collective-permute-start | bytes 3145736 | tf_op jit(solution)/shard_map/ppermute | solution.py:22
  146.7 7.4 %copy-start.4 = (s32[32]{0:T(128)S(1)}, s32[32]{0:T(128)}, u32[]{:S(2)}) copy-start(s32[32]{0:T(128)} %param.20) | copy-start | bytes 388
  148.7 24.5 %copy-start.2 = (bf16[256,14]{0,1:T(8,128)(2,1)S(1)}, bf16[256,14]{0,1:T(8,128)(2,1)}, u32[]{:S(2)}) copy-start(bf16[256,14]{0,1:T(8,128)(2,1)} %param.17) | copy-start | bytes 21508
  151.8 7.8 %collective-permute-start.25 = (bf16[64,768]{1,0:T(8,128)(2,1)S(1)}, bf16[64,768]{1,0:T(8,128)(2,1)S(1)}, u32[]{:S(2)}, u32[]{:S(2)}) collective-permute-start(bf16[64,768]{1,0:T(8,128)(2,1)S(1)} %get-tuple-element.49), channel_id=1, source_target_pairs={{0,48},{16,0},{32,16},{48,32},{64,112},{80,64},{96,80},{112,96},{1... | collective-permute-start | bytes 294920 | tf_op jit(solution)/shard_map/ppermute | solution.py:18
  154.1 7.1 %collective-permute-start.24 = (bf16[64,768]{1,0:T(8,128)(2,1)S(1)}, bf16[64,768]{1,0:T(8,128)(2,1)S(1)}, u32[]{:S(2)}, u32[]{:S(2)}) collective-permute-start(bf16[64,768]{1,0:T(8,128)(2,1)S(1)} %get-tuple-element.48), channel_id=1, source_target_pairs={{0,16},{16,32},{32,48},{48,0},{64,80},{80,96},{96,112},{112,64},{1... | collective-permute-start | bytes 294920 | tf_op jit(solution)/shard_map/ppermute | solution.py:18
  154.2 9.6 %collective-permute-start.23 = (bf16[64,768]{1,0:T(8,128)(2,1)S(1)}, bf16[64,768]{1,0:T(8,128)(2,1)S(1)}, u32[]{:S(2)}, u32[]{:S(2)}) collective-permute-start(bf16[64,768]{1,0:T(8,128)(2,1)S(1)} %get-tuple-element.47), channel_id=1, source_target_pairs={{0,64},{16,80},{32,96},{48,112},{64,0},{80,16},{96,32},{112,48},{1... | collective-permute-start | bytes 294920 | tf_op jit(solution)/shard_map/ppermute | solution.py:18
  156.1 7.6 %collective-permute-start.22 = (bf16[64,768]{1,0:T(8,128)(2,1)S(1)}, bf16[64,768]{1,0:T(8,128)(2,1)S(1)}, u32[]{:S(2)}, u32[]{:S(2)}) collective-permute-start(bf16[64,768]{1,0:T(8,128)(2,1)S(1)} %get-tuple-element.46), channel_id=1, source_target_pairs={{0,32},{16,48},{32,0},{48,16},{64,96},{80,112},{96,64},{112,80},{1... | collective-permute-start | bytes 294920 | tf_op jit(solution)/shard_map/ppermute | solution.py:18
  157.4 6.4 %collective-permute-start.21 = (bf16[64,768]{1,0:T(8,128)(2,1)S(1)}, bf16[64,768]{1,0:T(8,128)(2,1)S(1)}, u32[]{:S(2)}, u32[]{:S(2)}) collective-permute-start(bf16[64,768]{1,0:T(8,128)(2,1)S(1)} %get-tuple-element.45), channel_id=1, source_target_pairs={{0,112},{16,64},{32,80},{48,96},{64,48},{80,0},{96,16},{112,32},{1... | collective-permute-start | bytes 294920 | tf_op jit(solution)/shard_map/ppermute | solution.py:18
  159.6 7.1 %collective-permute-start.20 = (bf16[64,768]{1,0:T(8,128)(2,1)S(1)}, bf16[64,768]{1,0:T(8,128)(2,1)S(1)}, u32[]{:S(2)}, u32[]{:S(2)}) collective-permute-start(bf16[64,768]{1,0:T(8,128)(2,1)S(1)} %get-tuple-element.44), channel_id=1, source_target_pairs={{0,80},{16,96},{32,112},{48,64},{64,16},{80,32},{96,48},{112,0},{1... | collective-permute-start | bytes 294920 | tf_op jit(solution)/shard_map/ppermute | solution.py:18
  161.2 7.5 %collective-permute-start.19 = (bf16[64,768]{1,0:T(8,128)(2,1)S(1)}, bf16[64,768]{1,0:T(8,128)(2,1)S(1)}, u32[]{:S(2)}, u32[]{:S(2)}) collective-permute-start(bf16[64,768]{1,0:T(8,128)(2,1)S(1)} %get-tuple-element.43), channel_id=1, source_target_pairs={{0,96},{16,112},{32,64},{48,80},{64,32},{80,48},{96,0},{112,16},{1... | collective-permute-start | bytes 294920 | tf_op jit(solution)/shard_map/ppermute | solution.py:18
  174.2 21.8 %all-to-all-start.3 = ((f32[128,8,128]{2,1,0:T(8,128)}), f32[128,8,128]{2,1,0:T(8,128)S(1)}, u32[]{:S(2)}, u32[]{:S(2)}) async-start(f32[128,8,128]{2,1,0:T(8,128)} %broadcast_in_dim.118), calls=%async_computation.3 | async-start | bytes 1048576 | tf_op jit(solution)/shard_map/all_to_all | solution.py:409

commit v5 on v4

--- a/solution.py
+++ b/solution.py
@@ -39,6 +39,7 @@
 
 VM = pl.BlockSpec(memory_space=pltpu.VMEM)
 ANY = pl.BlockSpec(memory_space=pl.ANY)
+SMEM = pl.BlockSpec(memory_space=pltpu.SMEM)
 
 
 def fetch_kernel(source, *refs):
@@ -89,74 +90,60 @@
         out[:, start : start + result.shape[1]] = result[n * rows : (n + 1) * rows]
 
 
-def project(scaled, w_ref, outs, base):
-    hidden = w_ref.shape[1]
-    for start in range(0, hidden, 256):
-        stop = min(start + 256, hidden)
-        result = jnp.dot(scaled[...], w_ref[:, start:stop], preferred_element_type=jnp.float32)
-        spread(outs, result.astype(jnp.bfloat16), base + start)
-
-
 def load_gate_up_kernel(order, x_ref, gain_ref, wg_hbm, wu_hbm, *refs):
-    outs, wg_ref, wu_ref, scaled, half_sum, sems = refs[:-5], *refs[-5:]
+    outs, scaled, half_sum, wg_ref, wu_ref, sems = refs[:-5], *refs[-5:]
     width, hidden = wg_ref.shape
-    part = width // 4
-    copies = [
-        pltpu.make_async_copy(source.at[pl.ds(m * part, part)], target.at[pl.ds(m * part, part)], sems.at[4 * n + m])
-        for n, (source, target) in enumerate(((wg_hbm, wg_ref), (wu_hbm, wu_ref)))
-        for m in range(4)
-    ]
-    for copy in copies[:4]:
+    half, part = width // 2, width // 4
+    groups = []
+    for n, (source, target) in enumerate(((wg_hbm, wg_ref), (wu_hbm, wu_ref))):
+        for m in range(2):
+            rows = [pl.ds(m * half + k * part, part) for k in range(2)]
+            groups.append(
+                [
+                    pltpu.make_async_copy(source.at[row], target.at[row], sems.at[4 * n + 2 * m + k])
+                    for k, row in enumerate(rows)
+                ]
+            )
+    for copy in groups[0] + groups[1]:
         copy.start()
     scale_rows(order, x_ref, gain_ref, hidden, outs, scaled)
-    for copy in copies[:2]:
-        copy.wait()
-    for copy in copies[4:]:
-        copy.start()
-    for start in range(0, hidden, 256):
-        stop = min(start + 256, hidden)
-        half_sum[:, start:stop] = jnp.dot(
-            scaled[:, : 2 * part], wg_ref[: 2 * part, start:stop], preferred_element_type=jnp.float32
-        )
-    for copy in copies[2:4]:
-        copy.wait()
-    for start in range(0, hidden, 256):
-        stop = min(start + 256, hidden)
-        result = half_sum[:, start:stop] + jnp.dot(
-            scaled[:, 2 * part :], wg_ref[2 * part :, start:stop], preferred_element_type=jnp.float32
-        )
-        spread(outs, result.astype(jnp.bfloat16), start)
-    for copy in copies[4:]:
-        copy.wait()
-    project(scaled, wu_ref, outs, hidden)
-
-
-def gate_up_kernel(order, x_ref, gain_ref, wg_ref, wu_ref, *refs):
-    outs, scaled = refs[:-1], refs[-1]
-    hidden = wg_ref.shape[1]
-    scale_rows(order, x_ref, gain_ref, hidden, outs, scaled)
-    project(scaled, wg_ref, outs, 0)
-    project(scaled, wu_ref, outs, hidden)
-
-
-def gate_up(order, x, gain, w_gate, w_up, blocks, load):
+    for n, w_ref in enumerate((wg_ref, wu_ref)):
+        for m in range(2):
+            for copy in groups[2 * n + m]:
+                copy.wait()
+            if n == 0:
+                for copy in groups[2 + m]:
+                    copy.start()
+            k = slice(m * half, (m + 1) * half)
+            for start in range(0, hidden, 256):
+                at = slice(start, min(start + 256, hidden))
+                result = jnp.dot(scaled[:, k], w_ref[k, at], preferred_element_type=jnp.float32)
+                if m == 0:
+                    half_sum[:, at] = result
+                else:
+                    spread(outs, (half_sum[:, at] + result).astype(jnp.bfloat16), n * hidden + start)
+
+
+def gate_up(order, x, gain, w_gate, w_up, blocks):
     rows, width = x.shape
     hidden = w_gate.shape[1]
-    out = jax.ShapeDtypeStruct((rows // blocks, 2 * hidden + 128), jnp.bfloat16)
-    scratch = [pltpu.VMEM((rows, width), jnp.bfloat16)]
-    held = []
-    if load:
-        scratch += [pltpu.VMEM((rows, hidden), jnp.float32), pltpu.SemaphoreType.DMA((8,))]
-        held = [pltpu.VMEM(w_gate.shape, w_gate.dtype)] * 2
-        w_gate = pltpu.with_memory_space_constraint(w_gate, pltpu.HBM)
-        w_up = pltpu.with_memory_space_constraint(w_up, pltpu.HBM)
-    return pl.pallas_call(
-        load_gate_up_kernel if load else gate_up_kernel,
-        out_shape=[out] * blocks + held,
-        in_specs=[pl.BlockSpec(memory_space=pltpu.SMEM)] + [VM] * 2 + [ANY if load else VM] * 2,
-        out_specs=[VM] * (blocks + len(held)),
-        scratch_shapes=scratch,
-        compiler_params=pltpu.CompilerParams(vmem_limit_bytes=12 * 1024 * 1024),
+    space = pltpu.HBM if blocks == 2 else pltpu.VMEM
+    out = space((rows // blocks, 2 * hidden + 128), jnp.bfloat16)
+    w_gate = pltpu.with_memory_space_constraint(w_gate, pltpu.HBM)
+    w_up = pltpu.with_memory_space_constraint(w_up, pltpu.HBM)
+    return pl.pallas_call(
+        load_gate_up_kernel,
+        out_shape=[out] * blocks,
+        in_specs=[SMEM] + [VM] * 2 + [ANY] * 2,
+        out_specs=[VM] * blocks,
+        scratch_shapes=[
+            pltpu.VMEM((rows, width), jnp.bfloat16),
+            pltpu.VMEM((rows, hidden), jnp.float32),
+            pltpu.VMEM(w_gate.shape, w_gate.dtype),
+            pltpu.VMEM(w_up.shape, w_up.dtype),
+            pltpu.SemaphoreType.DMA((8,)),
+        ],
+        compiler_params=pltpu.CompilerParams(vmem_limit_bytes=24 * 1024 * 1024),
         cost_estimate=pl.CostEstimate(
             flops=4 * rows * width * hidden, transcendentals=0, bytes_accessed=4 * width * hidden + 4 * rows * hidden
         ),
@@ -222,16 +209,35 @@
         out[n * unit : (n + 1) * unit, :] = part[...]
 
 
-def down_kernel(count, order_a, order_b, *refs):
+def put_blocks(order, pieces, target, base, unit):
+    per = pieces[0].shape[0] // unit
+    for n in range(8):
+        start = pl.multiple_of(order[n] * unit, unit)
+        at = (n % per) * unit
+        target[pl.ds(base + start, unit), :] = pieces[n // per][at : at + unit, :]
+
+
+def place_kernel(order, *refs):
+    put_blocks(order, refs[:-1], refs[-1], 0, refs[-1].shape[0] // 8)
+
+
+def place(order, pieces, weight):
+    rows = sum(piece.shape[0] for piece in pieces)
+    return pl.pallas_call(
+        place_kernel,
+        out_shape=jax.ShapeDtypeStruct((rows, pieces[0].shape[1]), pieces[0].dtype),
+        in_specs=[SMEM] + [VM] * len(pieces),
+        out_specs=VM,
+        compiler_params=pltpu.CompilerParams(vmem_limit_bytes=4 * 1024 * 1024),
+        cost_estimate=pl.CostEstimate(flops=weight, transcendentals=0, bytes_accessed=0),
+    )(order, *pieces)
+
+
+def down_kernel(order_b, placed, *refs):
     pieces, w_ref, out_a, out_b, hidden = refs[:-4], *refs[-4:]
     half = hidden.shape[0] // 2
-    unit = half // 8
-    for base, order, group in ((0, order_a, pieces[:count]), (half, order_b, pieces[count:])):
-        per = group[0].shape[0] // unit
-        for n in range(8):
-            start = pl.multiple_of(order[n] * unit, unit)
-            at = (n % per) * unit
-            hidden[pl.ds(base + start, unit), :] = group[n // per][at : at + unit, :]
+    hidden[:half, :] = placed[...]
+    put_blocks(order_b, pieces, hidden, half, half // 8)
     for start in range(0, w_ref.shape[1], 256):
         result = jnp.dot(hidden[...], w_ref[:, start : start + 256], preferred_element_type=jnp.float32)
         result = result.astype(jnp.bfloat16)
@@ -239,18 +245,17 @@
         out_b[:, start : start + 256] = result[half:]
 
 
-def down(order_a, order_b, pieces_a, pieces_b, w_down):
-    rows = sum(piece.shape[0] for piece in pieces_a)
+def down(order_b, placed, pieces_b, w_down):
+    rows = placed.shape[0]
     inner, width = w_down.shape
-    pieces = [*pieces_a, *pieces_b]
-    return pl.pallas_call(
-        functools.partial(down_kernel, len(pieces_a)),
+    return pl.pallas_call(
+        down_kernel,
         out_shape=[jax.ShapeDtypeStruct((rows, width), jnp.bfloat16)] * 2,
-        in_specs=[pl.BlockSpec(memory_space=pltpu.SMEM)] * 2 + [VM] * (len(pieces) + 1),
+        in_specs=[SMEM] + [VM] * (len(pieces_b) + 2),
         out_specs=[VM] * 2,
         scratch_shapes=[pltpu.VMEM((2 * rows, inner), jnp.bfloat16)],
         compiler_params=pltpu.CompilerParams(vmem_limit_bytes=10 * 1024 * 1024),
-    )(order_a, order_b, *pieces, w_down)
+    )(order_b, placed, *pieces_b, w_down)
 
 
 def qkv_kernel(mine_ref, other_ref, src_ref, dst_ref, w_ref, *refs):
@@ -347,29 +352,32 @@
     own = states.reshape(per, width)
     gain = norm_gain[None, :]
     mine, other = gather_ty(own)
-    *part_a, w_gate, w_up = gate_up(send_a, mine, gain, w_gate, w_up, 4, True)
-    part_b = gate_up(send_b, other, gain, w_gate, w_up, 2, False)
+    part_b = gate_up(send_b, mine, gain, w_gate, w_up, 2)
+    part_a = gate_up(send_a, other, gain, w_gate, w_up, 4)
     half_send = (unit, part_a[0].shape[1])
-    came_a = [tx_move(part_a[dy], dy, 0) for dy in (2, 1, 3)]
-    came_b = tx_move(part_b[1], 0, 1)
     keep = (half_send, jnp.float32)
     go = (half_send, jnp.bfloat16)
-    keep_a, go_a = small_call(line_sum_kernel, [keep, go], part_a[0], *came_a, weight=5000000000)
-    keep_b, *go_b = small_call(pair_sum_kernel, [keep, go, go, go], part_b[0], came_b, after=(go_a,))
+    half_hidden = ((unit, hidden_here), jnp.bfloat16)
+    came_b = tx_move(part_b[1], 0, 1)
+    came_a = [tx_move(part_a[dy], dy, 0) for dy in (2, 1, 3)]
+    keep_b, *go_b = small_call(pair_sum_kernel, [keep, go, go, go], part_b[0], came_b)
     came_b = [tx_move(go_b[dy - 1], dy, 0) for dy in (2, 1, 3)]
+    keep_a, go_a = small_call(line_sum_kernel, [keep, go], part_a[0], *came_a, after=(go_b[0],))
     came_a = tx_move(go_a, 0, 1)
-    half_hidden = ((unit, hidden_here), jnp.bfloat16)
-    (hidden_a,) = small_call(activate_kernel, [half_hidden], keep_a, came_a)
+    (hidden_b,) = small_call(activate_kernel, [half_hidden], keep_b, *came_b, after=(go_a,))
+    came_b = [tx_move(hidden_b, dy, 0) for dy in (2, 1, 3)]
+    (hidden_a,) = small_call(activate_kernel, [half_hidden], keep_a, came_a, after=(hidden_b,))
     came_a = tx_move(hidden_a, 0, 1)
     (pair_a,) = small_call(stack_kernel, [((2 * unit, hidden_here), jnp.bfloat16)], hidden_a, came_a)
-    (hidden_b,) = small_call(activate_kernel, [half_hidden], keep_b, *came_b, after=(pair_a,))
-    came_b = [tx_move(hidden_b, dy, 0) for dy in (2, 1, 3)]
-    (line_b,) = small_call(stack_kernel, [((4 * unit, hidden_here), jnp.bfloat16)], hidden_b, came_b[1], came_b[0], came_b[2])
+    (line_b,) = small_call(
+        stack_kernel, [((4 * unit, hidden_here), jnp.bfloat16)], hidden_b, came_b[1], came_b[0], came_b[2], after=(pair_a,)
+    )
     pieces_a = [pair_a] + [tx_move(pair_a, dy, 0) for dy in (1, 2, 3)]
     pieces_b = [line_b, tx_move(line_b, 0, 1)]
     w_down = fetch(w_down, 4, pair_a)
-    mixed_a, mixed_b = down(from_a, from_b, pieces_a, pieces_b, w_down)
-    chip = (f32(mixed_a) + f32(core_swap(mixed_b))).astype(jnp.bfloat16)
+    placed = place(from_a, pieces_a, 2500000000)
+    mixed_a, mixed_b = down(from_b, placed, pieces_b, w_down)
+    chip = (f32(mixed_b) + f32(core_swap(mixed_a))).astype(jnp.bfloat16)
     parts = chip_exchange(chip.reshape(8, per, width))
     stream = (f32(own) + jnp.sum(f32(parts), axis=0)).astype(jnp.bfloat16)
     stream_out = stream.reshape(steps, local_rows, width)

time: 198 us -> 194 us (0.980)
  waiting for transfers between devices: 51.3 us -> 43.2 us
  Pallas kernels: 26 us -> 30.7 us
    ppermute x23, waiting for transfers between devices: 36.2 us -> 28 us  [tx_move(): return lax.ppermute(array, 'tx', pairs)]
    pallas_call x3 -> x4, Pallas kernels: 17.2 us -> 20.6 us  [the longest x2 15.4 us: gate_up(): pl.pallas_call(load_gate_up_kernel, out_shape=[out] * blocks, in_specs=[S...]
  transfers between devices with their start and end apart: 27 -> 27, of which waited for: 14 -> 12; matrix products, arithmetic and copies ran while one was open for 1% -> 1% of each run, Pallas kernels for 9% -> 12%
where the time goes in v5:
time: 194 us
  starting transfers between devices  55.2 us (28%)
  blocking collectives  54.1 us (28%)
  waiting for transfers between devices  43.2 us (22%)
  Pallas kernels  30.7 us (16%)
  local copies, waits for them, and re-layouts  4.08 us (2%)
  matrix products  3.15 us (2%)
  other arithmetic  2.52 us (1%)
    all_to_all x3, blocking collectives, chip_exchange(): return lax.all_to_all(blocks, 'ty', 0, 0, axis_index_groups=groups)  54.1 us
    ppermute x23, starting transfers between devices, tx_move(): return lax.ppermute(array, 'tx', pairs)  38.1 us
    ppermute x23, waiting for transfers between devices, tx_move(): return lax.ppermute(array, 'tx', pairs)  28 us
    pallas_call x2, Pallas kernels, gate_up(): pl.pallas_call(load_gate_up_kernel, out_shape=[out] * blocks, in_specs=[S...  15.4 us
    all_to_all x1, waiting for transfers between devices, per_device(): lax.all_to_all(jnp.broadcast_to(packed[None], (128,) + packed.shape), ('t...  12.9 us
    all_to_all x1, starting transfers between devices, per_device(): lax.all_to_all(jnp.broadcast_to(packed[None], (128,) + packed.shape), ('t...  9.09 us
    ppermute x3, starting transfers between devices, core_swap(): return lax.ppermute(array, 'ty', [(n, n ^ 1) for n in range(16)])  7.97 us
    pallas_call x2, Pallas kernels, fetch(): pl.pallas_call(fetch_kernel, out_shape=pltpu.VMEM(array.shape, array.dtyp...  4.92 us
  transfers between devices with their start and end apart: 27, of which 12 were waited for; matrix products, arithmetic and copies ran while one was open for 1% of the time, Pallas kernels for 12%

profile of v5, /device:TPU:1, one launch (start us, length us, event | category | flops | bytes accessed | tf_op | source)
XLA Modules:
  0.0 193.9 jit_solution(5770553782576095050)
XLA Ops:
  1.8 20.3 %all_to_all.20 = bf16[8,32,2048]{2,1,0:T(8,128)(2,1)S(1)} all-to-all(bf16[8,32,2048]{2,1,0:T(8,128)(2,1)S(1)} %broadcast_in_dim.101), channel_id=1, replica_groups={{0,2,4,6,8,10,12,14},{1,3,5,7,9,11,13,15},{16,18,20,22,24,26,28,30},{17..., dimensions={0} | all-to-all | bytes 2097152 | tf_op jit(solution)/shard_map/all_to_all | solution.py:27
  22.1 2.0 %collective-permute-start = (bf16[256,2048]{1,0:T(8,128)(2,1)S(1)}, bf16[256,2048]{1,0:T(8,128)(2,1)S(1)}, u32[]{:S(2)}, u32[]{:S(2)}) collective-permute-start(bf16[256,2048]{1,0:T(8,128)(2,1)S(1)} %bitcast.90), channel_id=1, source_target_pairs={{0,1},{1,0},{2,3},{3,2},{4,5},{5,4},{6,7},{7,6},{8,9},{9,8},{10,11... | collective-permute-start | bytes 3145736 | tf_op jit(solution)/shard_map/ppermute | solution.py:22
  24.2 8.3 %shard_map.123 = (bf16[128,3456]{1,0:T(8,128)(2,1)}, bf16[128,3456]{1,0:T(8,128)(2,1)}) custom-call(s32[8]{0:T(128)S(1)} %stack.77.order, bf16[256,2048]{1,0:T(8,128)(2,1)S(1)} %bitcast.91, bf16[1,2048]{1,0:T(2,128)(2,1)S(1)} %broadcast_in_dim.102.gain_ref, bf16[2048,1664]{1,0:T(8,128)(2,1)} %wg_hbm.3, bf16[2048,1664]{1,0:T(8,128)(2,1)} %wu_hbm.3), custom_call_target="tpu_custom_call" | custom-call | flops 3489660928 | bytes 15335424 | tf_op jit(solution)/shard_map/pallas_call | solution.py:134
  32.5 3.4 %collective-permute-start.4 = (bf16[128,3456]{1,0:T(8,128)(2,1)}, bf16[128,3456]{1,0:T(8,128)(2,1)}, u32[]{:S(2)}, u32[]{:S(2)}) collective-permute-start(bf16[128,3456]{1,0:T(8,128)(2,1)} %get-tuple-element.29), channel_id=1, source_target_pairs={{0,64},{16,80},{32,96},{48,112},{64,0},{80,16},{96,32},{112,48},{1... | collective-permute-start | bytes 2654216 | tf_op jit(solution)/shard_map/ppermute | solution.py:18
  35.9 7.2 %shard_map.122 = (bf16[64,3456]{1,0:T(8,128)(2,1)S(1)}, bf16[64,3456]{1,0:T(8,128)(2,1)S(1)}, bf16[64,3456]{1,0:T(8,128)(2,1)S(1)}, bf16[64,3456]{1,0:T(8,128)(2,1)S(1)}) custom-call(s32[8]{0:T(128)S(1)} %stack.76.order, bf16[256,2048]{1,0:T(8,128)(2,1)S(1)} %collective-permute-done.x_ref, bf16[1,2048]{1,0:T(2,128)(2,1)S(1)} %broadcast_in_dim.102.gain_ref, ...), custom_call_target="tpu_custom_call" | custom-call | flops 3489660928 | bytes 15335424 | tf_op jit(solution)/shard_map/pallas_call | solution.py:134
  43.1 3.0 %collective-permute-start.1 = (bf16[64,3456]{1,0:T(8,128)(2,1)S(1)}, bf16[64,3456]{1,0:T(8,128)(2,1)S(1)}, u32[]{:S(2)}, u32[]{:S(2)}) collective-permute-start(bf16[64,3456]{1,0:T(8,128)(2,1)S(1)} %get-tuple-element.25), channel_id=1, source_target_pairs={{0,32},{16,48},{32,0},{48,16},{64,96},{80,112},{96,64},{112,80},{1... | collective-permute-start | bytes 1327112 | tf_op jit(solution)/shard_map/ppermute | solution.py:18
  46.5 2.3 %collective-permute-start.3 = (bf16[64,3456]{1,0:T(8,128)(2,1)S(1)}, bf16[64,3456]{1,0:T(8,128)(2,1)S(1)}, u32[]{:S(2)}, u32[]{:S(2)}) collective-permute-start(bf16[64,3456]{1,0:T(8,128)(2,1)S(1)} %get-tuple-element.27), channel_id=1, source_target_pairs={{0,48},{16,0},{32,16},{48,32},{64,112},{80,64},{96,80},{112,96},{1... | collective-permute-start | bytes 1327112 | tf_op jit(solution)/shard_map/ppermute | solution.py:18
  48.8 7.4 %collective-permute-done.4.refs_1_ = bf16[128,3456]{1,0:T(8,128)(2,1)} collective-permute-done((bf16[128,3456]{1,0:T(8,128)(2,1)}, bf16[128,3456]{1,0:T(8,128)(2,1)}, u32[]{:S(2)}, u32[]{:S(2)}) %collective-permute-start.4) | collective-permute-done | bytes 884768 | tf_op jit(solution)/shard_map/ppermute | solution.py:18
  57.6 3.0 %collective-permute-start.6 = (bf16[32,3456]{1,0:T(8,128)(2,1)S(1)}, bf16[32,3456]{1,0:T(8,128)(2,1)S(1)}, u32[]{:S(2)}, u32[]{:S(2)}) collective-permute-start(bf16[32,3456]{1,0:T(8,128)(2,1)S(1)} %get-tuple-element.34), channel_id=1, source_target_pairs={{0,32},{16,48},{32,0},{48,16},{64,96},{80,112},{96,64},{112,80},{1... | collective-permute-start | bytes 663560 | tf_op jit(solution)/shard_map/ppermute | solution.py:18
  61.0 2.3 %collective-permute-start.8 = (bf16[32,3456]{1,0:T(8,128)(2,1)S(1)}, bf16[32,3456]{1,0:T(8,128)(2,1)S(1)}, u32[]{:S(2)}, u32[]{:S(2)}) collective-permute-start(bf16[32,3456]{1,0:T(8,128)(2,1)S(1)} %get-tuple-element.35), channel_id=1, source_target_pairs={{0,48},{16,0},{32,16},{48,32},{64,112},{80,64},{96,80},{112,96},{1... | collective-permute-start | bytes 663560 | tf_op jit(solution)/shard_map/ppermute | solution.py:18
  63.2 3.6 %collective-permute-done.2.refs_2_ = bf16[64,3456]{1,0:T(8,128)(2,1)S(1)} collective-permute-done((bf16[64,3456]{1,0:T(8,128)(2,1)S(1)}, bf16[64,3456]{1,0:T(8,128)(2,1)S(1)}, u32[]{:S(2)}, u32[]{:S(2)}) %collective-permute-start.2) | collective-permute-done | bytes 442400 | tf_op jit(solution)/shard_map/ppermute | solution.py:18
  67.2 3.3 %collective-permute-done.6.refs_1_ = bf16[32,3456]{1,0:T(8,128)(2,1)S(1)} collective-permute-done((bf16[32,3456]{1,0:T(8,128)(2,1)S(1)}, bf16[32,3456]{1,0:T(8,128)(2,1)S(1)}, u32[]{:S(2)}, u32[]{:S(2)}) %collective-permute-start.6) | collective-permute-done | bytes 221216 | tf_op jit(solution)/shard_map/ppermute | solution.py:18
  70.5 5.3 %collective-permute-done.7.refs_2_ = bf16[32,3456]{1,0:T(8,128)(2,1)S(1)} collective-permute-done((bf16[32,3456]{1,0:T(8,128)(2,1)S(1)}, bf16[32,3456]{1,0:T(8,128)(2,1)S(1)}, u32[]{:S(2)}, u32[]{:S(2)}) %collective-permute-start.7) | collective-permute-done | bytes 221216 | tf_op jit(solution)/shard_map/ppermute | solution.py:18
  77.8 2.6 %collective-permute-start.14 = (bf16[32,1664]{1,0:T(8,128)(2,1)S(1)}, bf16[32,1664]{1,0:T(8,128)(2,1)S(1)}, u32[]{:S(2)}, u32[]{:S(2)}) collective-permute-start(bf16[32,1664]{1,0:T(8,128)(2,1)S(1)} %shard_map.126.refs_2_.refs_0_), channel_id=1, source_target_pairs={{0,32},{16,48},{32,0},{48,16},{64,96},{80,112},{96,64},{112,80},{1... | collective-permute-start | bytes 319496 | tf_op jit(solution)/shard_map/ppermute | solution.py:18
  82.7 3.0 %collective-permute-start.11 = (bf16[64,1664]{1,0:T(8,128)(2,1)S(1)}, bf16[64,1664]{1,0:T(8,128)(2,1)S(1)}, u32[]{:S(2)}, u32[]{:S(2)}) collective-permute-start(bf16[64,1664]{1,0:T(8,128)(2,1)S(1)} %shard_map.128.refs_0_.refs_4_), channel_id=1, source_target_pairs={{0,32},{16,48},{32,0},{48,16},{64,96},{80,112},{96,64},{112,80},{1... | collective-permute-start | bytes 638984 | tf_op jit(solution)/shard_map/ppermute | solution.py:18
  85.8 2.4 %collective-permute-start.16 = (bf16[128,1664]{1,0:T(8,128)(2,1)S(1)}, bf16[128,1664]{1,0:T(8,128)(2,1)S(1)}, u32[]{:S(2)}, u32[]{:S(2)}) collective-permute-start(bf16[128,1664]{1,0:T(8,128)(2,1)S(1)} %shard_map.130.refs_0_), channel_id=1, source_target_pairs={{0,64},{16,80},{32,96},{48,112},{64,0},{80,16},{96,32},{112,48},{1... | collective-permute-start | bytes 1277960 | tf_op jit(solution)/shard_map/ppermute | solution.py:18
  88.4 3.0 %shard_map.131.refs_2_ = bf16[1664,2048]{1,0:T(8,128)(2,1)S(1)} custom-call(bf16[1664,2048]{1,0:T(8,128)(2,1)} %source.1, bf16[64,1664]{1,0:T(8,128)(2,1)S(1)} %shard_map.128.refs_0_.refs_4_), custom_call_target="tpu_custom_call" | custom-call | tf_op jit(solution)/shard_map/pallas_call | solution.py:59
  91.4 2.7 %collective-permute-done.11.refs_2_ = bf16[64,1664]{1,0:T(8,128)(2,1)S(1)} collective-permute-done((bf16[64,1664]{1,0:T(8,128)(2,1)S(1)}, bf16[64,1664]{1,0:T(8,128)(2,1)S(1)}, u32[]{:S(2)}, u32[]{:S(2)}) %collective-permute-start.11) | collective-permute-done | bytes 213024 | tf_op jit(solution)/shard_map/ppermute | solution.py:18
  96.3 4.6 %shard_map.132 = (bf16[256,2048]{1,0:T(8,128)(2,1)S(1)}, bf16[256,2048]{1,0:T(8,128)(2,1)S(1)}) custom-call(s32[8]{0:T(128)S(1)} %stack.72.order_b, bf16[256,1664]{1,0:T(8,128)(2,1)S(1)} %shard_map.129.placed, bf16[128,1664]{1,0:T(8,128)(2,1)S(1)} %shard_map.130.refs_0_, bf16[128,1664]{1,0:T(8,128)(2,1)S(1)} %collective-permute-done.16.refs_1_, ...), custom_call_target="tpu_custom_call" | custom-call | tf_op jit(solution)/shard_map/pallas_call | solution.py:251
  100.9 3.3 %collective-permute-start.17 = (bf16[256,2048]{1,0:T(8,128)(2,1)S(1)}, bf16[256,2048]{1,0:T(8,128)(2,1)S(1)}, u32[]{:S(2)}, u32[]{:S(2)}) collective-permute-start(bf16[256,2048]{1,0:T(8,128)(2,1)S(1)} %get-tuple-element.37), channel_id=1, source_target_pairs={{0,1},{1,0},{2,3},{3,2},{4,5},{5,4},{6,7},{7,6},{8,9},{9,8},{10,11... | collective-permute-start | bytes 3145736 | tf_op jit(solution)/shard_map/ppermute | solution.py:22
  104.3 2.3 %collective-permute-done.17 = bf16[256,2048]{1,0:T(8,128)(2,1)S(1)} collective-permute-done((bf16[256,2048]{1,0:T(8,128)(2,1)S(1)}, bf16[256,2048]{1,0:T(8,128)(2,1)S(1)}, u32[]{:S(2)}, u32[]{:S(2)}) %collective-permute-start.17) | collective-permute-done | bytes 1048608 | tf_op jit(solution)/shard_map/ppermute | solution.py:22
  106.9 16.7 %all_to_all.21 = bf16[8,32,2048]{2,1,0:T(8,128)(2,1)S(1)} all-to-all(bf16[8,32,2048]{2,1,0:T(8,128)(2,1)S(1)} %bitcast.92), channel_id=1, replica_groups={{0,2,4,6,8,10,12,14},{1,3,5,7,9,11,13,15},{16,18,20,22,24,26,28,30},{17..., dimensions={0} | all-to-all | bytes 2097152 | tf_op jit(solution)/shard_map/all_to_all | solution.py:27
  123.9 17.1 %all_to_all.22 = bf16[8,32,2048]{2,1,0:T(8,128)(2,1)S(1)} all-to-all(bf16[8,32,2048]{2,1,0:T(8,128)(2,1)S(1)} %broadcast_in_dim.104), channel_id=1, replica_groups={{0,2,4,6,8,10,12,14},{1,3,5,7,9,11,13,15},{16,18,20,22,24,26,28,30},{17..., dimensions={0} | all-to-all | bytes 2097152 | tf_op jit(solution)/shard_map/all_to_all | solution.py:27
  141.0 2.6 %collective-permute-start.18 = (bf16[256,2048]{1,0:T(8,128)(2,1)S(1)}, bf16[256,2048]{1,0:T(8,128)(2,1)S(1)}, u32[]{:S(2)}, u32[]{:S(2)}) collective-permute-start(bf16[256,2048]{1,0:T(8,128)(2,1)S(1)} %bitcast.87), channel_id=1, source_target_pairs={{0,1},{1,0},{2,3},{3,2},{4,5},{5,4},{6,7},{7,6},{8,9},{9,8},{10,11... | collective-permute-start | bytes 3145736 | tf_op jit(solution)/shard_map/ppermute | solution.py:22
  144.0 1.9 shard_map.133.w_ref
  146.0 3.1 %shard_map.134 = (bf16[64,768]{1,0:T(8,128)(2,1)S(1)}, bf16[64,768]{1,0:T(8,128)(2,1)S(1)}, bf16[64,768]{1,0:T(8,128)(2,1)S(1)}, bf16[64,768]{1,0:T(8,128)(2,1)S...) custom-call(bf16[256,2048]{1,0:T(8,128)(2,1)S(1)} %bitcast.89, ...), custom_call_target="tpu_custom_call" | custom-call | flops 2684354560 | bytes 5242880 | tf_op jit(solution)/shard_map/pallas_call | solution.py:280
  149.0 2.7 %collective-permute-start.19 = (bf16[64,768]{1,0:T(8,128)(2,1)S(1)}, bf16[64,768]{1,0:T(8,128)(2,1)S(1)}, u32[]{:S(2)}, u32[]{:S(2)}) collective-permute-start(bf16[64,768]{1,0:T(8,128)(2,1)S(1)} %get-tuple-element.39), channel_id=1, source_target_pairs={{0,96},{16,112},{32,64},{48,80},{64,32},{80,48},{96,0},{112,16},{1... | collective-permute-start | bytes 294920 | tf_op jit(solution)/shard_map/ppermute | solution.py:18
  151.7 1.9 collective-permute-start.20
  153.7 3.2 %collective-permute-start.21 = (bf16[64,768]{1,0:T(8,128)(2,1)S(1)}, bf16[64,768]{1,0:T(8,128)(2,1)S(1)}, u32[]{:S(2)}, u32[]{:S(2)}) collective-permute-start(bf16[64,768]{1,0:T(8,128)(2,1)S(1)} %get-tuple-element.41), channel_id=1, source_target_pairs={{0,112},{16,64},{32,80},{48,96},{64,48},{80,0},{96,16},{112,32},{1... | collective-permute-start | bytes 294920 | tf_op jit(solution)/shard_map/ppermute | solution.py:18
  165.4 2.0 %fusion.59 = (f32[2,32,2]{0,2,1:T(2,128)S(1)}, f32[2,32,2,64]{3,0,2,1:T(2,128)S(1)}) fusion(bf16[2,32,1,2,128]{4,3,2,1,0:T(2,128)(2,1)S(1)} %get-tuple-element.60, pred[32,64]{1,0:T(8,128)(4,1)S(1)} %iota_compare_fusion.2, bf16[32,64,256]{2,1,0:T(8,128)(2,1)} %param.18), kind=kOutput, calls=%fused_computation.111 | convolution fusion | flops 2121600 | bytes 1116672 | tf_op jit(solution)/shard_map/tshd,slhd->tshl/dot_general | solution.py:396
  170.1 9.1 %all-to-all-start.3 = ((f32[128,8,128]{2,1,0:T(8,128)}), f32[128,8,128]{2,1,0:T(8,128)S(1)}, u32[]{:S(2)}, u32[]{:S(2)}) async-start(f32[128,8,128]{2,1,0:T(8,128)} %broadcast_in_dim.118), calls=%async_computation.3 | async-start | bytes 1048576 | tf_op jit(solution)/shard_map/all_to_all | solution.py:417
  179.9 12.9 %all-to-all-done.3 = f32[128,8,128]{2,1,0:T(8,128)S(1)} async-done(((f32[128,8,128]{2,1,0:T(8,128)}), f32[128,8,128]{2,1,0:T(8,128)S(1)}, u32[]{:S(2)}, u32[]{:S(2)}) %all-to-all-start.3) | async-done | bytes 524320 | tf_op jit(solution)/shard_map/all_to_all | solution.py:417
  (101 shorter events, 24.6 us)
Async XLA Ops:
  0.6 167.5 %copy-start = (bf16[32,64,256]{2,1,0:T(8,128)(2,1)S(1)}, bf16[32,64,256]{2,1,0:T(8,128)(2,1)}, u32[]{:S(2)}) copy-start(bf16[32,64,256]{2,1,0:T(8,128)(2,1)} %param.19) | copy-start | bytes 3145732
  0.6 23.4 %copy-start.4 = (bf16[2048]{0:T(1024)(128)(2,1)S(1)}, bf16[2048]{0:T(1024)(128)(2,1)}, u32[]{:S(2)}) copy-start(bf16[2048]{0:T(1024)(128)(2,1)} %param.12) | copy-start | bytes 12292
  22.1 13.9 %collective-permute-start = (bf16[256,2048]{1,0:T(8,128)(2,1)S(1)}, bf16[256,2048]{1,0:T(8,128)(2,1)S(1)}, u32[]{:S(2)}, u32[]{:S(2)}) collective-permute-start(bf16[256,2048]{1,0:T(8,128)(2,1)S(1)} %bitcast.90), channel_id=1, source_target_pairs={{0,1},{1,0},{2,3},{3,2},{4,5},{5,4},{6,7},{7,6},{8,9},{9,8},{10,11... | collective-permute-start | bytes 3145736 | tf_op jit(solution)/shard_map/ppermute | solution.py:22
  32.5 23.7 %collective-permute-start.4 = (bf16[128,3456]{1,0:T(8,128)(2,1)}, bf16[128,3456]{1,0:T(8,128)(2,1)}, u32[]{:S(2)}, u32[]{:S(2)}) collective-permute-start(bf16[128,3456]{1,0:T(8,128)(2,1)} %get-tuple-element.29), channel_id=1, source_target_pairs={{0,64},{16,80},{32,96},{48,112},{64,0},{80,16},{96,32},{112,48},{1... | collective-permute-start | bytes 2654216 | tf_op jit(solution)/shard_map/ppermute | solution.py:18
  35.9 20.3 %copy-start.1 = (bf16[128,3456]{1,0:T(8,128)(2,1)S(1)}, bf16[128,3456]{1,0:T(8,128)(2,1)}, u32[]{:S(2)}) copy-start(bf16[128,3456]{1,0:T(8,128)(2,1)} %get-tuple-element.28.refs_0_) | copy-start | bytes 2654212
  43.1 17.8 %collective-permute-start.1 = (bf16[64,3456]{1,0:T(8,128)(2,1)S(1)}, bf16[64,3456]{1,0:T(8,128)(2,1)S(1)}, u32[]{:S(2)}, u32[]{:S(2)}) collective-permute-start(bf16[64,3456]{1,0:T(8,128)(2,1)S(1)} %get-tuple-element.25), channel_id=1, source_target_pairs={{0,32},{16,48},{32,0},{48,16},{64,96},{80,112},{96,64},{112,80},{1... | collective-permute-start | bytes 1327112 | tf_op jit(solution)/shard_map/ppermute | solution.py:18
  46.1 20.7 %collective-permute-start.2 = (bf16[64,3456]{1,0:T(8,128)(2,1)S(1)}, bf16[64,3456]{1,0:T(8,128)(2,1)S(1)}, u32[]{:S(2)}, u32[]{:S(2)}) collective-permute-start(bf16[64,3456]{1,0:T(8,128)(2,1)S(1)} %get-tuple-element.26), channel_id=1, source_target_pairs={{0,16},{16,32},{32,48},{48,0},{64,80},{80,96},{96,112},{112,64},{1... | collective-permute-start | bytes 1327112 | tf_op jit(solution)/shard_map/ppermute | solution.py:18
  46.5 20.3 %collective-permute-start.3 = (bf16[64,3456]{1,0:T(8,128)(2,1)S(1)}, bf16[64,3456]{1,0:T(8,128)(2,1)S(1)}, u32[]{:S(2)}, u32[]{:S(2)}) collective-permute-start(bf16[64,3456]{1,0:T(8,128)(2,1)S(1)} %get-tuple-element.27), channel_id=1, source_target_pairs={{0,48},{16,0},{32,16},{48,32},{64,112},{80,64},{96,80},{112,96},{1... | collective-permute-start | bytes 1327112 | tf_op jit(solution)/shard_map/ppermute | solution.py:18
  57.6 12.9 %collective-permute-start.6 = (bf16[32,3456]{1,0:T(8,128)(2,1)S(1)}, bf16[32,3456]{1,0:T(8,128)(2,1)S(1)}, u32[]{:S(2)}, u32[]{:S(2)}) collective-permute-start(bf16[32,3456]{1,0:T(8,128)(2,1)S(1)} %get-tuple-element.34), channel_id=1, source_target_pairs={{0,32},{16,48},{32,0},{48,16},{64,96},{80,112},{96,64},{112,80},{1... | collective-permute-start | bytes 663560 | tf_op jit(solution)/shard_map/ppermute | solution.py:18
  60.6 15.2 %collective-permute-start.7 = (bf16[32,3456]{1,0:T(8,128)(2,1)S(1)}, bf16[32,3456]{1,0:T(8,128)(2,1)S(1)}, u32[]{:S(2)}, u32[]{:S(2)}) collective-permute-start(bf16[32,3456]{1,0:T(8,128)(2,1)S(1)} %get-tuple-element.30.refs_4_), channel_id=1, source_target_pairs={{0,16},{16,32},{32,48},{48,0},{64,80},{80,96},{96,112},{112,64},{1... | collective-permute-start | bytes 663560 | tf_op jit(solution)/shard_map/ppermute | solution.py:18
  61.0 14.8 %collective-permute-start.8 = (bf16[32,3456]{1,0:T(8,128)(2,1)S(1)}, bf16[32,3456]{1,0:T(8,128)(2,1)S(1)}, u32[]{:S(2)}, u32[]{:S(2)}) collective-permute-start(bf16[32,3456]{1,0:T(8,128)(2,1)S(1)} %get-tuple-element.35), channel_id=1, source_target_pairs={{0,48},{16,0},{32,16},{48,32},{64,112},{80,64},{96,80},{112,96},{1... | collective-permute-start | bytes 663560 | tf_op jit(solution)/shard_map/ppermute | solution.py:18
  67.1 8.9 %collective-permute-start.5 = (bf16[32,3456]{1,0:T(8,128)(2,1)S(1)}, bf16[32,3456]{1,0:T(8,128)(2,1)S(1)}, u32[]{:S(2)}, u32[]{:S(2)}) collective-permute-start(bf16[32,3456]{1,0:T(8,128)(2,1)S(1)} %get-tuple-element.32.refs_4_), channel_id=1, source_target_pairs={{0,64},{16,80},{32,96},{48,112},{64,0},{80,16},{96,32},{112,48},{1... | collective-permute-start | bytes 663560 | tf_op jit(solution)/shard_map/ppermute | solution.py:18
  76.2 5.1 %collective-permute-start.9 = (bf16[32,1664]{1,0:T(8,128)(2,1)S(1)}, bf16[32,1664]{1,0:T(8,128)(2,1)S(1)}, u32[]{:S(2)}, u32[]{:S(2)}) collective-permute-start(bf16[32,1664]{1,0:T(8,128)(2,1)S(1)} %shard_map.127.refs_0_), channel_id=1, source_target_pairs={{0,64},{16,80},{32,96},{48,112},{64,0},{80,16},{96,32},{112,48},{1... | collective-permute-start | bytes 319496 | tf_op jit(solution)/shard_map/ppermute | solution.py:18
  76.4 9.3 %collective-permute-start.13 = (bf16[32,1664]{1,0:T(8,128)(2,1)S(1)}, bf16[32,1664]{1,0:T(8,128)(2,1)S(1)}, u32[]{:S(2)}, u32[]{:S(2)}) collective-permute-start(bf16[32,1664]{1,0:T(8,128)(2,1)S(1)} %shard_map.126.refs_2_.refs_0_), channel_id=1, source_target_pairs={{0,16},{16,32},{32,48},{48,0},{64,80},{80,96},{96,112},{112,64},{1... | collective-permute-start | bytes 319496 | tf_op jit(solution)/shard_map/ppermute | solution.py:18
  77.8 7.9 %collective-permute-start.14 = (bf16[32,1664]{1,0:T(8,128)(2,1)S(1)}, bf16[32,1664]{1,0:T(8,128)(2,1)S(1)}, u32[]{:S(2)}, u32[]{:S(2)}) collective-permute-start(bf16[32,1664]{1,0:T(8,128)(2,1)S(1)} %shard_map.126.refs_2_.refs_0_), channel_id=1, source_target_pairs={{0,32},{16,48},{32,0},{48,16},{64,96},{80,112},{96,64},{112,80},{1... | collective-permute-start | bytes 319496 | tf_op jit(solution)/shard_map/ppermute | solution.py:18
  80.4 5.3 %collective-permute-start.15 = (bf16[32,1664]{1,0:T(8,128)(2,1)S(1)}, bf16[32,1664]{1,0:T(8,128)(2,1)S(1)}, u32[]{:S(2)}, u32[]{:S(2)}) collective-permute-start(bf16[32,1664]{1,0:T(8,128)(2,1)S(1)} %shard_map.126.refs_2_.refs_0_), channel_id=1, source_target_pairs={{0,48},{16,0},{32,16},{48,32},{64,112},{80,64},{96,80},{112,96},{1... | collective-permute-start | bytes 319496 | tf_op jit(solution)/shard_map/ppermute | solution.py:18
  81.3 10.1 %collective-permute-start.10 = (bf16[64,1664]{1,0:T(8,128)(2,1)S(1)}, bf16[64,1664]{1,0:T(8,128)(2,1)S(1)}, u32[]{:S(2)}, u32[]{:S(2)}) collective-permute-start(bf16[64,1664]{1,0:T(8,128)(2,1)S(1)} %shard_map.128.refs_0_.refs_4_), channel_id=1, source_target_pairs={{0,16},{16,32},{32,48},{48,0},{64,80},{80,96},{96,112},{112,64},{1... | collective-permute-start | bytes 638984 | tf_op jit(solution)/shard_map/ppermute | solution.py:18
  82.7 11.5 %collective-permute-start.11 = (bf16[64,1664]{1,0:T(8,128)(2,1)S(1)}, bf16[64,1664]{1,0:T(8,128)(2,1)S(1)}, u32[]{:S(2)}, u32[]{:S(2)}) collective-permute-start(bf16[64,1664]{1,0:T(8,128)(2,1)S(1)} %shard_map.128.refs_0_.refs_4_), channel_id=1, source_target_pairs={{0,32},{16,48},{32,0},{48,16},{64,96},{80,112},{96,64},{112,80},{1... | collective-permute-start | bytes 638984 | tf_op jit(solution)/shard_map/ppermute | solution.py:18
  85.7 8.4 %collective-permute-start.12 = (bf16[64,1664]{1,0:T(8,128)(2,1)S(1)}, bf16[64,1664]{1,0:T(8,128)(2,1)S(1)}, u32[]{:S(2)}, u32[]{:S(2)}) collective-permute-start(bf16[64,1664]{1,0:T(8,128)(2,1)S(1)} %shard_map.128.refs_0_.refs_4_), channel_id=1, source_target_pairs={{0,48},{16,0},{32,16},{48,32},{64,112},{80,64},{96,80},{112,96},{1... | collective-permute-start | bytes 638984 | tf_op jit(solution)/shard_map/ppermute | solution.py:18
  85.8 10.6 %collective-permute-start.16 = (bf16[128,1664]{1,0:T(8,128)(2,1)S(1)}, bf16[128,1664]{1,0:T(8,128)(2,1)S(1)}, u32[]{:S(2)}, u32[]{:S(2)}) collective-permute-start(bf16[128,1664]{1,0:T(8,128)(2,1)S(1)} %shard_map.130.refs_0_), channel_id=1, source_target_pairs={{0,64},{16,80},{32,96},{48,112},{64,0},{80,16},{96,32},{112,48},{1... | collective-permute-start | bytes 1277960 | tf_op jit(solution)/shard_map/ppermute | solution.py:18
  100.9 5.6 %collective-permute-start.17 = (bf16[256,2048]{1,0:T(8,128)(2,1)S(1)}, bf16[256,2048]{1,0:T(8,128)(2,1)S(1)}, u32[]{:S(2)}, u32[]{:S(2)}) collective-permute-start(bf16[256,2048]{1,0:T(8,128)(2,1)S(1)} %get-tuple-element.37), channel_id=1, source_target_pairs={{0,1},{1,0},{2,3},{3,2},{4,5},{5,4},{6,7},{7,6},{8,9},{9,8},{10,11... | collective-permute-start | bytes 3145736 | tf_op jit(solution)/shard_map/ppermute | solution.py:22
  106.5 17.2 %copy-start.2 = (bf16[2,16,2048]{2,1,0:T(8,128)(2,1)S(1)}, bf16[2,16,2048]{2,1,0:T(8,128)(2,1)}, u32[]{:S(2)}) copy-start(bf16[2,16,2048]{2,1,0:T(8,128)(2,1)} %param.11) | copy-start | bytes 393220
  123.6 20.2 %copy-start.5 = (s32[256]{0:T(256)S(1)}, s32[256]{0:T(256)}, u32[]{:S(2)}) copy-start(s32[256]{0:T(256)} %param.21) | copy-start | bytes 3076
  141.0 4.9 %collective-permute-start.18 = (bf16[256,2048]{1,0:T(8,128)(2,1)S(1)}, bf16[256,2048]{1,0:T(8,128)(2,1)S(1)}, u32[]{:S(2)}, u32[]{:S(2)}) collective-permute-start(bf16[256,2048]{1,0:T(8,128)(2,1)S(1)} %bitcast.87), channel_id=1, source_target_pairs={{0,1},{1,0},{2,3},{3,2},{4,5},{5,4},{6,7},{7,6},{8,9},{9,8},{10,11... | collective-permute-start | bytes 3145736 | tf_op jit(solution)/shard_map/ppermute | solution.py:22
  149.0 9.7 %collective-permute-start.19 = (bf16[64,768]{1,0:T(8,128)(2,1)S(1)}, bf16[64,768]{1,0:T(8,128)(2,1)S(1)}, u32[]{:S(2)}, u32[]{:S(2)}) collective-permute-start(bf16[64,768]{1,0:T(8,128)(2,1)S(1)} %get-tuple-element.39), channel_id=1, source_target_pairs={{0,96},{16,112},{32,64},{48,80},{64,32},{80,48},{96,0},{112,16},{1... | collective-permute-start | bytes 294920 | tf_op jit(solution)/shard_map/ppermute | solution.py:18
  151.7 8.5 %collective-permute-start.20 = (bf16[64,768]{1,0:T(8,128)(2,1)S(1)}, bf16[64,768]{1,0:T(8,128)(2,1)S(1)}, u32[]{:S(2)}, u32[]{:S(2)}) collective-permute-start(bf16[64,768]{1,0:T(8,128)(2,1)S(1)} %get-tuple-element.40), channel_id=1, source_target_pairs={{0,80},{16,96},{32,112},{48,64},{64,16},{80,32},{96,48},{112,0},{1... | collective-permute-start | bytes 294920 | tf_op jit(solution)/shard_map/ppermute | solution.py:18
  153.7 7.7 %collective-permute-start.21 = (bf16[64,768]{1,0:T(8,128)(2,1)S(1)}, bf16[64,768]{1,0:T(8,128)(2,1)S(1)}, u32[]{:S(2)}, u32[]{:S(2)}) collective-permute-start(bf16[64,768]{1,0:T(8,128)(2,1)S(1)} %get-tuple-element.41), channel_id=1, source_target_pairs={{0,112},{16,64},{32,80},{48,96},{64,48},{80,0},{96,16},{112,32},{1... | collective-permute-start | bytes 294920 | tf_op jit(solution)/shard_map/ppermute | solution.py:18
  156.8 5.3 %collective-permute-start.22 = (bf16[64,768]{1,0:T(8,128)(2,1)S(1)}, bf16[64,768]{1,0:T(8,128)(2,1)S(1)}, u32[]{:S(2)}, u32[]{:S(2)}) collective-permute-start(bf16[64,768]{1,0:T(8,128)(2,1)S(1)} %get-tuple-element.42), channel_id=1, source_target_pairs={{0,32},{16,48},{32,0},{48,16},{64,96},{80,112},{96,64},{112,80},{1... | collective-permute-start | bytes 294920 | tf_op jit(solution)/shard_map/ppermute | solution.py:18
  158.4 5.3 %collective-permute-start.23 = (bf16[64,768]{1,0:T(8,128)(2,1)S(1)}, bf16[64,768]{1,0:T(8,128)(2,1)S(1)}, u32[]{:S(2)}, u32[]{:S(2)}) collective-permute-start(bf16[64,768]{1,0:T(8,128)(2,1)S(1)} %get-tuple-element.43), channel_id=1, source_target_pairs={{0,64},{16,80},{32,96},{48,112},{64,0},{80,16},{96,32},{112,48},{1... | collective-permute-start | bytes 294920 | tf_op jit(solution)/shard_map/ppermute | solution.py:18
  158.7 5.9 %collective-permute-start.24 = (bf16[64,768]{1,0:T(8,128)(2,1)S(1)}, bf16[64,768]{1,0:T(8,128)(2,1)S(1)}, u32[]{:S(2)}, u32[]{:S(2)}) collective-permute-start(bf16[64,768]{1,0:T(8,128)(2,1)S(1)} %get-tuple-element.44), channel_id=1, source_target_pairs={{0,16},{16,32},{32,48},{48,0},{64,80},{80,96},{96,112},{112,64},{1... | collective-permute-start | bytes 294920 | tf_op jit(solution)/shard_map/ppermute | solution.py:18
  160.2 4.5 %collective-permute-start.25 = (bf16[64,768]{1,0:T(8,128)(2,1)S(1)}, bf16[64,768]{1,0:T(8,128)(2,1)S(1)}, u32[]{:S(2)}, u32[]{:S(2)}) collective-permute-start(bf16[64,768]{1,0:T(8,128)(2,1)S(1)} %get-tuple-element.45), channel_id=1, source_target_pairs={{0,48},{16,0},{32,16},{48,32},{64,112},{80,64},{96,80},{112,96},{1... | collective-permute-start | bytes 294920 | tf_op jit(solution)/shard_map/ppermute | solution.py:18
  170.1 22.6 %all-to-all-start.3 = ((f32[128,8,128]{2,1,0:T(8,128)}), f32[128,8,128]{2,1,0:T(8,128)S(1)}, u32[]{:S(2)}, u32[]{:S(2)}) async-start(f32[128,8,128]{2,1,0:T(8,128)} %broadcast_in_dim.118), calls=%async_computation.3 | async-start | bytes 1048576 | tf_op jit(solution)/shard_map/all_to_all | solution.py:417
  (2 other events, 11.3 us)

commit v6 on v5

--- a/solution.py
+++ b/solution.py
@@ -66,31 +66,39 @@
     )(pltpu.with_memory_space_constraint(array, pltpu.HBM), *after)
 
 
-def scale_rows(order, x_ref, gain_ref, hidden, outs, scaled):
-    rows = outs[0].shape[0]
-    unit = x_ref.shape[0] // 8
+def blocks_of(outs):
+    found, at = [], 0
+    for out in outs:
+        found.append((out, at, out.shape[0]))
+        at += out.shape[0]
+    return found
+
+
+def scale_rows(orders, x_ref, gain_ref, hidden, outs, scaled):
+    unit = x_ref.shape[0] // 16
     gain = gain_ref[...].astype(jnp.float32) * DOWN
     lane = lax.broadcasted_iota(jnp.int32, (unit, 128), 1)
-    for n in range(8):
-        start = pl.multiple_of(order[n] * unit, unit)
+    for n in range(16):
+        start = pl.multiple_of(orders[n // 8][n % 8] * (2 * unit) + (n // 8) * unit, unit)
         values = x_ref[pl.ds(start, unit), :].astype(jnp.float32)
-        scaled[n * unit : (n + 1) * unit, :] = (values * gain).astype(jnp.bfloat16)
+        to = n * unit
+        scaled[to : to + unit, :] = (values * gain).astype(jnp.bfloat16)
         squares = jnp.sum(values * values, axis=1, keepdims=True)
         first = squares.astype(jnp.bfloat16).astype(jnp.float32)
         second = (squares - first).astype(jnp.bfloat16).astype(jnp.float32)
         third = squares - first - second
         columns = jnp.where(lane == 0, first, jnp.where(lane == 1, second, jnp.where(lane == 2, third, 0.0)))
-        at = (n * unit) % rows
-        outs[n * unit // rows][at : at + unit, 2 * hidden :] = columns.astype(jnp.bfloat16)
+        for out, at, rows in blocks_of(outs):
+            if at <= to < at + rows:
+                out[to - at : to - at + unit, 2 * hidden :] = columns.astype(jnp.bfloat16)
 
 
 def spread(outs, result, start):
-    rows = outs[0].shape[0]
-    for n, out in enumerate(outs):
-        out[:, start : start + result.shape[1]] = result[n * rows : (n + 1) * rows]
-
-
-def load_gate_up_kernel(order, x_ref, gain_ref, wg_hbm, wu_hbm, *refs):
+    for out, at, rows in blocks_of(outs):
+        out[:, start : start + result.shape[1]] = result[at : at + rows]
+
+
+def load_gate_up_kernel(order_z, order_y, x_ref, gain_ref, wg_hbm, wu_hbm, *refs):
     outs, scaled, half_sum, wg_ref, wu_ref, sems = refs[:-5], *refs[-5:]
     width, hidden = wg_ref.shape
     half, part = width // 2, width // 4
@@ -106,7 +114,7 @@
             )
     for copy in groups[0] + groups[1]:
         copy.start()
-    scale_rows(order, x_ref, gain_ref, hidden, outs, scaled)
+    scale_rows((order_z, order_y), x_ref, gain_ref, hidden, outs, scaled)
     for n, w_ref in enumerate((wg_ref, wu_ref)):
         for m in range(2):
             for copy in groups[2 * n + m]:
@@ -124,18 +132,19 @@
                     spread(outs, (half_sum[:, at] + result).astype(jnp.bfloat16), n * hidden + start)
 
 
-def gate_up(order, x, gain, w_gate, w_up, blocks):
+def gate_up(order_z, order_y, x, gain, w_gate, w_up):
     rows, width = x.shape
     hidden = w_gate.shape[1]
-    space = pltpu.HBM if blocks == 2 else pltpu.VMEM
-    out = space((rows // blocks, 2 * hidden + 128), jnp.bfloat16)
+    wide = 2 * hidden + 128
+    outs = [jax.ShapeDtypeStruct((rows // 4, wide), jnp.bfloat16)] * 2
+    outs += [jax.ShapeDtypeStruct((rows // 8, wide), jnp.bfloat16)] * 4
     w_gate = pltpu.with_memory_space_constraint(w_gate, pltpu.HBM)
     w_up = pltpu.with_memory_space_constraint(w_up, pltpu.HBM)
     return pl.pallas_call(
         load_gate_up_kernel,
-        out_shape=[out] * blocks,
-        in_specs=[SMEM] + [VM] * 2 + [ANY] * 2,
-        out_specs=[VM] * blocks,
+        out_shape=outs,
+        in_specs=[SMEM] * 2 + [VM] * 2 + [ANY] * 2,
+        out_specs=[VM] * 6,
         scratch_shapes=[
             pltpu.VMEM((rows, width), jnp.bfloat16),
             pltpu.VMEM((rows, hidden), jnp.float32),
@@ -147,7 +156,7 @@
         cost_estimate=pl.CostEstimate(
             flops=4 * rows * width * hidden, transcendentals=0, bytes_accessed=4 * width * hidden + 4 * rows * hidden
         ),
-    )(order, x, gain, w_gate, w_up)
+    )(order_z, order_y, x, gain, w_gate, w_up)
 
 
 def small_call(kernel, outs, *arrays, after=(), weight=0):
@@ -164,23 +173,30 @@
     )(*arrays, *after)
 
 
-def line_sum_kernel(a0, a1, a2, a3, keep, go):
-    unit, wide = keep.shape
-    for start in range(0, wide, 128):
+def early_sum_kernel(a0, a1, a2, a3, out):
+    for start in range(0, out.shape[1], 128):
         at = slice(start, start + 128)
+        out[:, at] = f32(a0[:, at]) + f32(a1[:, at]) + f32(a2[:, at]) + f32(a3[:, at])
+
+
+def line_sum_kernel(early, a0, a1, a2, a3, keep, go):
+    unit = keep.shape[0] // 2
+    for start in range(0, keep.shape[1], 128):
+        at = slice(start, start + 128)
+        late = f32(a0[:, at]) + f32(a1[:, at]) + f32(a2[:, at]) + f32(a3[:, at])
         for lo, out in ((0, keep), (unit, go)):
-            rows = slice(lo, lo + unit)
-            total = f32(a0[rows, at]) + f32(a1[rows, at]) + f32(a2[rows, at]) + f32(a3[rows, at])
-            out[:, at] = total.astype(out.dtype)
-
-
-def pair_sum_kernel(b0, b1, *outs):
-    unit, wide = outs[0].shape
-    for start in range(0, wide, 128):
+            out[:unit, at] = early[lo : lo + unit, at].astype(out.dtype)
+            out[unit:, at] = late[lo : lo + unit].astype(out.dtype)
+
+
+def pair_sum_kernel(b0, b1, c0, c1, *outs):
+    unit = outs[0].shape[0] // 2
+    for start in range(0, outs[0].shape[1], 128):
         at = slice(start, start + 128)
         for n, out in enumerate(outs):
             rows = slice(n * unit, (n + 1) * unit)
-            out[:, at] = (f32(b0[rows, at]) + f32(b1[rows, at])).astype(out.dtype)
+            out[:unit, at] = (f32(b0[rows, at]) + f32(b1[rows, at])).astype(out.dtype)
+            out[unit:, at] = (f32(c0[rows, at]) + f32(c1[rows, at])).astype(out.dtype)
 
 
 def activate_kernel(keep, *refs):
@@ -234,15 +250,23 @@
 
 
 def down_kernel(order_b, placed, *refs):
-    pieces, w_ref, out_a, out_b, hidden = refs[:-4], *refs[-4:]
+    pieces, w_ref, out_mine, out_other, hidden = refs[:-4], *refs[-4:]
     half = hidden.shape[0] // 2
-    hidden[:half, :] = placed[...]
-    put_blocks(order_b, pieces, hidden, half, half // 8)
+    unit = half // 16
+    per = pieces[0].shape[0] // (2 * unit)
+    for n in range(8):
+        start = pl.multiple_of(order_b[n] * (2 * unit), 2 * unit)
+        at = (n % per) * 2 * unit
+        for group in range(2):
+            piece = pieces[n // per][at + group * unit : at + (group + 1) * unit, :]
+            hidden[pl.ds(group * half + start, unit), :] = piece
+            to = group * half + (2 * n + 1) * unit
+            hidden[to : to + unit, :] = placed[(2 * n + group) * unit : (2 * n + group + 1) * unit, :]
     for start in range(0, w_ref.shape[1], 256):
         result = jnp.dot(hidden[...], w_ref[:, start : start + 256], preferred_element_type=jnp.float32)
         result = result.astype(jnp.bfloat16)
-        out_a[:, start : start + 256] = result[:half]
-        out_b[:, start : start + 256] = result[half:]
+        out_mine[:, start : start + 256] = result[:half]
+        out_other[:, start : start + 256] = result[half:]
 
 
 def down(order_b, placed, pieces_b, w_down):
@@ -352,17 +376,20 @@
     own = states.reshape(per, width)
     gain = norm_gain[None, :]
     mine, other = gather_ty(own)
-    part_b = gate_up(send_b, mine, gain, w_gate, w_up, 2)
-    part_a = gate_up(send_a, other, gain, w_gate, w_up, 4)
-    half_send = (unit, part_a[0].shape[1])
+    parts = gate_up(send_b, send_a, mine, gain, w_gate, w_up)
+    more = gate_up(send_b, send_a, other, gain, w_gate, w_up)
+    half_send = (unit, parts[0].shape[1])
     keep = (half_send, jnp.float32)
     go = (half_send, jnp.bfloat16)
     half_hidden = ((unit, hidden_here), jnp.bfloat16)
-    came_b = tx_move(part_b[1], 0, 1)
-    came_a = [tx_move(part_a[dy], dy, 0) for dy in (2, 1, 3)]
-    keep_b, *go_b = small_call(pair_sum_kernel, [keep, go, go, go], part_b[0], came_b)
+    both_b, both_a = [], []
+    for group in (parts, more):
+        both_b += [group[0], tx_move(group[1], 0, 1)]
+        both_a += [group[2]] + [tx_move(group[2 + dy], dy, 0) for dy in (2, 1, 3)]
+    (early,) = small_call(early_sum_kernel, [keep], *both_a[:4], weight=5000000000)
+    keep_b, *go_b = small_call(pair_sum_kernel, [keep, go, go, go], *both_b, after=(early,))
     came_b = [tx_move(go_b[dy - 1], dy, 0) for dy in (2, 1, 3)]
-    keep_a, go_a = small_call(line_sum_kernel, [keep, go], part_a[0], *came_a, after=(go_b[0],))
+    keep_a, go_a = small_call(line_sum_kernel, [keep, go], early, *both_a[4:], after=(go_b[0],))
     came_a = tx_move(go_a, 0, 1)
     (hidden_b,) = small_call(activate_kernel, [half_hidden], keep_b, *came_b, after=(go_a,))
     came_b = [tx_move(hidden_b, dy, 0) for dy in (2, 1, 3)]
@@ -376,7 +403,7 @@
     pieces_b = [line_b, tx_move(line_b, 0, 1)]
     w_down = fetch(w_down, 4, pair_a)
     placed = place(from_a, pieces_a, 2500000000)
-    mixed_a, mixed_b = down(from_b, placed, pieces_b, w_down)
+    mixed_b, mixed_a = down(from_b, placed, pieces_b, w_down)
     chip = (f32(mixed_b) + f32(core_swap(mixed_a))).astype(jnp.bfloat16)
     parts = chip_exchange(chip.reshape(8, per, width))
     stream = (f32(own) + jnp.sum(f32(parts), axis=0)).astype(jnp.bfloat16)

time: 194 us -> 191 us (0.985)
  Pallas kernels: 30.7 us -> 28.5 us
    ppermute x23 -> x27, starting transfers between devices: 38.1 us -> 40.1 us  [tx_move(): return lax.ppermute(array, 'tx', pairs)]
    ppermute x23 -> x27, waiting for transfers between devices: 28 us -> 26.2 us  [tx_move(): return lax.ppermute(array, 'tx', pairs)]
  transfers between devices with their start and end apart: 27 -> 31, of which waited for: 12 -> 10; matrix products, arithmetic and copies ran while one was open for 1% -> 1% of each run, Pallas kernels for 12% -> 11%
where the time goes in v6:
time: 191 us
  starting transfers between devices  56.3 us (29%)
  blocking collectives  54.1 us (28%)
  waiting for transfers between devices  41.3 us (22%)
  Pallas kernels  28.5 us (15%)
  local copies, waits for them, and re-layouts  4.07 us (2%)
  matrix products  3.16 us (2%)
  other arithmetic  2.52 us (1%)
    all_to_all x3, blocking collectives, chip_exchange(): return lax.all_to_all(blocks, 'ty', 0, 0, axis_index_groups=groups)  54.1 us
    ppermute x27, starting transfers between devices, tx_move(): return lax.ppermute(array, 'tx', pairs)  40.1 us
    ppermute x27, waiting for transfers between devices, tx_move(): return lax.ppermute(array, 'tx', pairs)  26.2 us
    pallas_call x2, Pallas kernels, gate_up(): pl.pallas_call(load_gate_up_kernel, out_shape=outs, in_specs=[SMEM] * 2 +...  14.4 us
    all_to_all x1, waiting for transfers between devices, per_device(): lax.all_to_all(jnp.broadcast_to(packed[None], (128,) + packed.shape), ('t...  12.9 us
    ppermute x3, starting transfers between devices, core_swap(): return lax.ppermute(array, 'ty', [(n, n ^ 1) for n in range(16)])  8.35 us
    all_to_all x1, starting transfers between devices, per_device(): lax.all_to_all(jnp.broadcast_to(packed[None], (128,) + packed.shape), ('t...  7.78 us
    pallas_call x2, Pallas kernels, fetch(): pl.pallas_call(fetch_kernel, out_shape=pltpu.VMEM(array.shape, array.dtyp...  4.92 us
  transfers between devices with their start and end apart: 31, of which 10 were waited for; matrix products, arithmetic and copies ran while one was open for 1% of the time, Pallas kernels for 11%

profile of v6, /device:TPU:1, one launch (start us, length us, event | category | flops | bytes accessed | tf_op | source)
XLA Modules:
  0.0 191.0 jit_solution(13810983873467208171)
XLA Ops:
  1.8 20.3 %all_to_all.20 = bf16[8,32,2048]{2,1,0:T(8,128)(2,1)S(1)} all-to-all(bf16[8,32,2048]{2,1,0:T(8,128)(2,1)S(1)} %broadcast_in_dim.101), channel_id=1, replica_groups={{0,2,4,6,8,10,12,14},{1,3,5,7,9,11,13,15},{16,18,20,22,24,26,28,30},{17..., dimensions={0} | all-to-all | bytes 2097152 | tf_op jit(solution)/shard_map/all_to_all | solution.py:27
  22.1 2.0 %collective-permute-start.3 = (bf16[256,2048]{1,0:T(8,128)(2,1)S(1)}, bf16[256,2048]{1,0:T(8,128)(2,1)S(1)}, u32[]{:S(2)}, u32[]{:S(2)}) collective-permute-start(bf16[256,2048]{1,0:T(8,128)(2,1)S(1)} %bitcast.87), channel_id=1, source_target_pairs={{0,1},{1,0},{2,3},{3,2},{4,5},{5,4},{6,7},{7,6},{8,9},{9,8},{10,11... | collective-permute-start | bytes 3145736 | tf_op jit(solution)/shard_map/ppermute | solution.py:22
  24.3 7.2 %shard_map.122 = (bf16[64,3456]{1,0:T(8,128)(2,1)S(1)}, bf16[64,3456]{1,0:T(8,128)(2,1)S(1)}, bf16[32,3456]{1,0:T(8,128)(2,1)S(1)}, bf16[32,3456]{1,0:T(8,128)(2...) custom-call(s32[8]{0:T(128)S(1)} %stack.76.order_z, s32[8]{0:T(128)S(1)} %stack.77.order_y, ...), custom_call_target="tpu_custom_call" | custom-call | flops 3489660928 | bytes 15335424 | tf_op jit(solution)/shard_map/pallas_call | solution.py:143
  31.5 3.0 %collective-permute-start = (bf16[32,3456]{1,0:T(8,128)(2,1)S(1)}, bf16[32,3456]{1,0:T(8,128)(2,1)S(1)}, u32[]{:S(2)}, u32[]{:S(2)}) collective-permute-start(bf16[32,3456]{1,0:T(8,128)(2,1)S(1)} %get-tuple-element.31), channel_id=1, source_target_pairs={{0,32},{16,48},{32,0},{48,16},{64,96},{80,112},{96,64},{112,80},{1... | collective-permute-start | bytes 663560 | tf_op jit(solution)/shard_map/ppermute | solution.py:18
  34.9 2.3 %collective-permute-start.2 = (bf16[32,3456]{1,0:T(8,128)(2,1)S(1)}, bf16[32,3456]{1,0:T(8,128)(2,1)S(1)}, u32[]{:S(2)}, u32[]{:S(2)}) collective-permute-start(bf16[32,3456]{1,0:T(8,128)(2,1)S(1)} %get-tuple-element.33), channel_id=1, source_target_pairs={{0,48},{16,0},{32,16},{48,32},{64,112},{80,64},{96,80},{112,96},{1... | collective-permute-start | bytes 663560 | tf_op jit(solution)/shard_map/ppermute | solution.py:18
  37.2 3.3 %collective-permute-start.7 = (bf16[64,3456]{1,0:T(8,128)(2,1)S(1)}, bf16[64,3456]{1,0:T(8,128)(2,1)S(1)}, u32[]{:S(2)}, u32[]{:S(2)}) collective-permute-start(bf16[64,3456]{1,0:T(8,128)(2,1)S(1)} %get-tuple-element.39), channel_id=1, source_target_pairs={{0,64},{16,80},{32,96},{48,112},{64,0},{80,16},{96,32},{112,48},{1... | collective-permute-start | bytes 1327112 | tf_op jit(solution)/shard_map/ppermute | solution.py:18
  40.5 7.2 %shard_map.124 = (bf16[64,3456]{1,0:T(8,128)(2,1)S(1)}, bf16[64,3456]{1,0:T(8,128)(2,1)S(1)}, bf16[32,3456]{1,0:T(8,128)(2,1)S(1)}, bf16[32,3456]{1,0:T(8,128)(2...) custom-call(s32[8]{0:T(128)S(1)} %stack.76.order_z, s32[8]{0:T(128)S(1)} %stack.77.order_y, ...), custom_call_target="tpu_custom_call" | custom-call | flops 3489660928 | bytes 15335424 | tf_op jit(solution)/shard_map/pallas_call | solution.py:143
  48.5 2.2 %collective-permute-start.6 = (bf16[32,3456]{1,0:T(8,128)(2,1)S(1)}, bf16[32,3456]{1,0:T(8,128)(2,1)S(1)}, u32[]{:S(2)}, u32[]{:S(2)}) collective-permute-start(bf16[32,3456]{1,0:T(8,128)(2,1)S(1)} %get-tuple-element.37), channel_id=1, source_target_pairs={{0,48},{16,0},{32,16},{48,32},{64,112},{80,64},{96,80},{112,96},{1... | collective-permute-start | bytes 663560 | tf_op jit(solution)/shard_map/ppermute | solution.py:18
  50.8 9.0 %collective-permute-done.8.refs_3_ = bf16[64,3456]{1,0:T(8,128)(2,1)S(1)} collective-permute-done((bf16[64,3456]{1,0:T(8,128)(2,1)S(1)}, bf16[64,3456]{1,0:T(8,128)(2,1)S(1)}, u32[]{:S(2)}, u32[]{:S(2)}) %collective-permute-start.8) | collective-permute-done | bytes 442400 | tf_op jit(solution)/shard_map/ppermute | solution.py:18
  61.1 1.8 collective-permute-start.12
  63.1 2.6 %collective-permute-start.9 = (bf16[32,3456]{1,0:T(8,128)(2,1)S(1)}, bf16[32,3456]{1,0:T(8,128)(2,1)S(1)}, u32[]{:S(2)}, u32[]{:S(2)}) collective-permute-start(bf16[32,3456]{1,0:T(8,128)(2,1)S(1)} %get-tuple-element.44.refs_4_), channel_id=1, source_target_pairs={{0,64},{16,80},{32,96},{48,112},{64,0},{80,16},{96,32},{112,48},{1... | collective-permute-start | bytes 663560 | tf_op jit(solution)/shard_map/ppermute | solution.py:18
  66.5 6.8 %collective-permute-done.11.refs_2_ = bf16[32,3456]{1,0:T(8,128)(2,1)S(1)} collective-permute-done((bf16[32,3456]{1,0:T(8,128)(2,1)S(1)}, bf16[32,3456]{1,0:T(8,128)(2,1)S(1)}, u32[]{:S(2)}, u32[]{:S(2)}) %collective-permute-start.11) | collective-permute-done | bytes 221216 | tf_op jit(solution)/shard_map/ppermute | solution.py:18
  73.7 2.6 %collective-permute-start.13 = (bf16[32,1664]{1,0:T(8,128)(2,1)S(1)}, bf16[32,1664]{1,0:T(8,128)(2,1)S(1)}, u32[]{:S(2)}, u32[]{:S(2)}) collective-permute-start(bf16[32,1664]{1,0:T(8,128)(2,1)S(1)} %shard_map.128.refs_0_), channel_id=1, source_target_pairs={{0,64},{16,80},{32,96},{48,112},{64,0},{80,16},{96,32},{112,48},{1... | collective-permute-start | bytes 319496 | tf_op jit(solution)/shard_map/ppermute | solution.py:18
  77.3 1.6 collective-permute-start.19
  79.6 1.9 collective-permute-start.15
  84.4 3.0 %shard_map.132.refs_2_ = bf16[1664,2048]{1,0:T(8,128)(2,1)S(1)} custom-call(bf16[1664,2048]{1,0:T(8,128)(2,1)} %source.1, bf16[64,1664]{1,0:T(8,128)(2,1)S(1)} %shard_map.129.refs_0_.refs_4_), custom_call_target="tpu_custom_call" | custom-call | tf_op jit(solution)/shard_map/pallas_call | solution.py:59
  87.4 5.8 %collective-permute-done.14.refs_1_ = bf16[64,1664]{1,0:T(8,128)(2,1)S(1)} collective-permute-done((bf16[64,1664]{1,0:T(8,128)(2,1)S(1)}, bf16[64,1664]{1,0:T(8,128)(2,1)S(1)}, u32[]{:S(2)}, u32[]{:S(2)}) %collective-permute-start.14) | collective-permute-done | bytes 213024 | tf_op jit(solution)/shard_map/ppermute | solution.py:18
  93.8 4.6 %shard_map.133 = (bf16[256,2048]{1,0:T(8,128)(2,1)S(1)}, bf16[256,2048]{1,0:T(8,128)(2,1)S(1)}) custom-call(s32[8]{0:T(128)S(1)} %stack.72.order_b, bf16[256,1664]{1,0:T(8,128)(2,1)S(1)} %shard_map.130.placed, bf16[128,1664]{1,0:T(8,128)(2,1)S(1)} %shard_map.131.refs_0_, bf16[128,1664]{1,0:T(8,128)(2,1)S(1)} %collective-permute-done.20.refs_1_, ...), custom_call_target="tpu_custom_call" | custom-call | tf_op jit(solution)/shard_map/pallas_call | solution.py:275
  98.4 3.7 %collective-permute-start.21 = (bf16[256,2048]{1,0:T(8,128)(2,1)S(1)}, bf16[256,2048]{1,0:T(8,128)(2,1)S(1)}, u32[]{:S(2)}, u32[]{:S(2)}) collective-permute-start(bf16[256,2048]{1,0:T(8,128)(2,1)S(1)} %get-tuple-element.49), channel_id=1, source_target_pairs={{0,1},{1,0},{2,3},{3,2},{4,5},{5,4},{6,7},{7,6},{8,9},{9,8},{10,11... | collective-permute-start | bytes 3145736 | tf_op jit(solution)/shard_map/ppermute | solution.py:22
  102.2 2.3 %collective-permute-done.21 = bf16[256,2048]{1,0:T(8,128)(2,1)S(1)} collective-permute-done((bf16[256,2048]{1,0:T(8,128)(2,1)S(1)}, bf16[256,2048]{1,0:T(8,128)(2,1)S(1)}, u32[]{:S(2)}, u32[]{:S(2)}) %collective-permute-start.21) | collective-permute-done | bytes 1048608 | tf_op jit(solution)/shard_map/ppermute | solution.py:22
  104.8 16.7 %all_to_all.21 = bf16[8,32,2048]{2,1,0:T(8,128)(2,1)S(1)} all-to-all(bf16[8,32,2048]{2,1,0:T(8,128)(2,1)S(1)} %bitcast.92), channel_id=1, replica_groups={{0,2,4,6,8,10,12,14},{1,3,5,7,9,11,13,15},{16,18,20,22,24,26,28,30},{17..., dimensions={0} | all-to-all | bytes 2097152 | tf_op jit(solution)/shard_map/all_to_all | solution.py:27
  121.8 17.1 %all_to_all.22 = bf16[8,32,2048]{2,1,0:T(8,128)(2,1)S(1)} all-to-all(bf16[8,32,2048]{2,1,0:T(8,128)(2,1)S(1)} %broadcast_in_dim.104), channel_id=1, replica_groups={{0,2,4,6,8,10,12,14},{1,3,5,7,9,11,13,15},{16,18,20,22,24,26,28,30},{17..., dimensions={0} | all-to-all | bytes 2097152 | tf_op jit(solution)/shard_map/all_to_all | solution.py:27
  138.9 2.6 %collective-permute-start.22 = (bf16[256,2048]{1,0:T(8,128)(2,1)S(1)}, bf16[256,2048]{1,0:T(8,128)(2,1)S(1)}, u32[]{:S(2)}, u32[]{:S(2)}) collective-permute-start(bf16[256,2048]{1,0:T(8,128)(2,1)S(1)} %bitcast.89), channel_id=1, source_target_pairs={{0,1},{1,0},{2,3},{3,2},{4,5},{5,4},{6,7},{7,6},{8,9},{9,8},{10,11... | collective-permute-start | bytes 3145736 | tf_op jit(solution)/shard_map/ppermute | solution.py:22
  141.9 1.9 shard_map.134.w_ref
  143.9 3.1 %shard_map.135 = (bf16[64,768]{1,0:T(8,128)(2,1)S(1)}, bf16[64,768]{1,0:T(8,128)(2,1)S(1)}, bf16[64,768]{1,0:T(8,128)(2,1)S(1)}, bf16[64,768]{1,0:T(8,128)(2,1)S...) custom-call(bf16[256,2048]{1,0:T(8,128)(2,1)S(1)} %bitcast.91, ...), custom_call_target="tpu_custom_call" | custom-call | flops 2684354560 | bytes 5242880 | tf_op jit(solution)/shard_map/pallas_call | solution.py:304
  146.9 3.0 %collective-permute-start.23 = (bf16[64,768]{1,0:T(8,128)(2,1)S(1)}, bf16[64,768]{1,0:T(8,128)(2,1)S(1)}, u32[]{:S(2)}, u32[]{:S(2)}) collective-permute-start(bf16[64,768]{1,0:T(8,128)(2,1)S(1)} %get-tuple-element.51), channel_id=1, source_target_pairs={{0,96},{16,112},{32,64},{48,80},{64,32},{80,48},{96,0},{112,16},{1... | collective-permute-start | bytes 294920 | tf_op jit(solution)/shard_map/ppermute | solution.py:18
  149.9 4.0 %collective-permute-start.24 = (bf16[64,768]{1,0:T(8,128)(2,1)S(1)}, bf16[64,768]{1,0:T(8,128)(2,1)S(1)}, u32[]{:S(2)}, u32[]{:S(2)}) collective-permute-start(bf16[64,768]{1,0:T(8,128)(2,1)S(1)} %get-tuple-element.52), channel_id=1, source_target_pairs={{0,80},{16,96},{32,112},{48,64},{64,16},{80,32},{96,48},{112,0},{1... | collective-permute-start | bytes 294920 | tf_op jit(solution)/shard_map/ppermute | solution.py:18
  156.6 2.0 %collective-permute-start.28 = (bf16[64,768]{1,0:T(8,128)(2,1)S(1)}, bf16[64,768]{1,0:T(8,128)(2,1)S(1)}, u32[]{:S(2)}, u32[]{:S(2)}) collective-permute-start(bf16[64,768]{1,0:T(8,128)(2,1)S(1)} %get-tuple-element.56), channel_id=1, source_target_pairs={{0,16},{16,32},{32,48},{48,0},{64,80},{80,96},{96,112},{112,64},{1... | collective-permute-start | bytes 294920 | tf_op jit(solution)/shard_map/ppermute | solution.py:18
  158.6 2.2 %collective-permute-start.29 = (bf16[64,768]{1,0:T(8,128)(2,1)S(1)}, bf16[64,768]{1,0:T(8,128)(2,1)S(1)}, u32[]{:S(2)}, u32[]{:S(2)}) collective-permute-start(bf16[64,768]{1,0:T(8,128)(2,1)S(1)} %get-tuple-element.57), channel_id=1, source_target_pairs={{0,48},{16,0},{32,16},{48,32},{64,112},{80,64},{96,80},{112,96},{1... | collective-permute-start | bytes 294920 | tf_op jit(solution)/shard_map/ppermute | solution.py:18
  163.8 2.0 %fusion.59 = (f32[2,32,2]{0,2,1:T(2,128)S(1)}, f32[2,32,2,64]{3,0,2,1:T(2,128)S(1)}) fusion(bf16[2,32,1,2,128]{4,3,2,1,0:T(2,128)(2,1)S(1)} %get-tuple-element.72, pred[32,64]{1,0:T(8,128)(4,1)S(1)} %iota_compare_fusion.2, bf16[32,64,256]{2,1,0:T(8,128)(2,1)} %param.18), kind=kOutput, calls=%fused_computation.111 | convolution fusion | flops 2121600 | bytes 1116672 | tf_op jit(solution)/shard_map/tshd,slhd->tshl/dot_general | solution.py:423
  168.5 7.8 %all-to-all-start.3 = ((f32[128,8,128]{2,1,0:T(8,128)}), f32[128,8,128]{2,1,0:T(8,128)S(1)}, u32[]{:S(2)}, u32[]{:S(2)}) async-start(f32[128,8,128]{2,1,0:T(8,128)} %broadcast_in_dim.118), calls=%async_computation.3 | async-start | bytes 1048576 | tf_op jit(solution)/shard_map/all_to_all | solution.py:444
  177.0 12.9 %all-to-all-done.3 = f32[128,8,128]{2,1,0:T(8,128)S(1)} async-done(((f32[128,8,128]{2,1,0:T(8,128)}), f32[128,8,128]{2,1,0:T(8,128)S(1)}, u32[]{:S(2)}, u32[]{:S(2)}) %all-to-all-start.3) | async-done | bytes 524320 | tf_op jit(solution)/shard_map/all_to_all | solution.py:444
  (108 shorter events, 21.6 us)
Async XLA Ops:
  0.6 165.9 %copy-start = (bf16[32,64,256]{2,1,0:T(8,128)(2,1)S(1)}, bf16[32,64,256]{2,1,0:T(8,128)(2,1)}, u32[]{:S(2)}) copy-start(bf16[32,64,256]{2,1,0:T(8,128)(2,1)} %param.19) | copy-start | bytes 3145732
  22.1 18.4 %collective-permute-start.3 = (bf16[256,2048]{1,0:T(8,128)(2,1)S(1)}, bf16[256,2048]{1,0:T(8,128)(2,1)S(1)}, u32[]{:S(2)}, u32[]{:S(2)}) collective-permute-start(bf16[256,2048]{1,0:T(8,128)(2,1)S(1)} %bitcast.87), channel_id=1, source_target_pairs={{0,1},{1,0},{2,3},{3,2},{4,5},{5,4},{6,7},{7,6},{8,9},{9,8},{10,11... | collective-permute-start | bytes 3145736 | tf_op jit(solution)/shard_map/ppermute | solution.py:22
  31.5 16.3 %collective-permute-start = (bf16[32,3456]{1,0:T(8,128)(2,1)S(1)}, bf16[32,3456]{1,0:T(8,128)(2,1)S(1)}, u32[]{:S(2)}, u32[]{:S(2)}) collective-permute-start(bf16[32,3456]{1,0:T(8,128)(2,1)S(1)} %get-tuple-element.31), channel_id=1, source_target_pairs={{0,32},{16,48},{32,0},{48,16},{64,96},{80,112},{96,64},{112,80},{1... | collective-permute-start | bytes 663560 | tf_op jit(solution)/shard_map/ppermute | solution.py:18
  34.5 13.4 %collective-permute-start.1 = (bf16[32,3456]{1,0:T(8,128)(2,1)S(1)}, bf16[32,3456]{1,0:T(8,128)(2,1)S(1)}, u32[]{:S(2)}, u32[]{:S(2)}) collective-permute-start(bf16[32,3456]{1,0:T(8,128)(2,1)S(1)} %get-tuple-element.32), channel_id=1, source_target_pairs={{0,16},{16,32},{32,48},{48,0},{64,80},{80,96},{96,112},{112,64},{1... | collective-permute-start | bytes 663560 | tf_op jit(solution)/shard_map/ppermute | solution.py:18
  34.9 13.6 %collective-permute-start.2 = (bf16[32,3456]{1,0:T(8,128)(2,1)S(1)}, bf16[32,3456]{1,0:T(8,128)(2,1)S(1)}, u32[]{:S(2)}, u32[]{:S(2)}) collective-permute-start(bf16[32,3456]{1,0:T(8,128)(2,1)S(1)} %get-tuple-element.33), channel_id=1, source_target_pairs={{0,48},{16,0},{32,16},{48,32},{64,112},{80,64},{96,80},{112,96},{1... | collective-permute-start | bytes 663560 | tf_op jit(solution)/shard_map/ppermute | solution.py:18
  37.2 13.6 %collective-permute-start.7 = (bf16[64,3456]{1,0:T(8,128)(2,1)S(1)}, bf16[64,3456]{1,0:T(8,128)(2,1)S(1)}, u32[]{:S(2)}, u32[]{:S(2)}) collective-permute-start(bf16[64,3456]{1,0:T(8,128)(2,1)S(1)} %get-tuple-element.39), channel_id=1, source_target_pairs={{0,64},{16,80},{32,96},{48,112},{64,0},{80,16},{96,32},{112,48},{1... | collective-permute-start | bytes 1327112 | tf_op jit(solution)/shard_map/ppermute | solution.py:18
  47.7 12.1 %collective-permute-start.8 = (bf16[64,3456]{1,0:T(8,128)(2,1)S(1)}, bf16[64,3456]{1,0:T(8,128)(2,1)S(1)}, u32[]{:S(2)}, u32[]{:S(2)}) collective-permute-start(bf16[64,3456]{1,0:T(8,128)(2,1)S(1)} %get-tuple-element.41), channel_id=1, source_target_pairs={{0,64},{16,80},{32,96},{48,112},{64,0},{80,16},{96,32},{112,48},{1... | collective-permute-start | bytes 1327112 | tf_op jit(solution)/shard_map/ppermute | solution.py:18
  47.8 13.3 %collective-permute-start.4 = (bf16[32,3456]{1,0:T(8,128)(2,1)S(1)}, bf16[32,3456]{1,0:T(8,128)(2,1)S(1)}, u32[]{:S(2)}, u32[]{:S(2)}) collective-permute-start(bf16[32,3456]{1,0:T(8,128)(2,1)S(1)} %get-tuple-element.35), channel_id=1, source_target_pairs={{0,32},{16,48},{32,0},{48,16},{64,96},{80,112},{96,64},{112,80},{1... | collective-permute-start | bytes 663560 | tf_op jit(solution)/shard_map/ppermute | solution.py:18
  47.9 15.0 %collective-permute-start.5 = (bf16[32,3456]{1,0:T(8,128)(2,1)S(1)}, bf16[32,3456]{1,0:T(8,128)(2,1)S(1)}, u32[]{:S(2)}, u32[]{:S(2)}) collective-permute-start(bf16[32,3456]{1,0:T(8,128)(2,1)S(1)} %get-tuple-element.36), channel_id=1, source_target_pairs={{0,16},{16,32},{32,48},{48,0},{64,80},{80,96},{96,112},{112,64},{1... | collective-permute-start | bytes 663560 | tf_op jit(solution)/shard_map/ppermute | solution.py:18
  48.5 14.4 %collective-permute-start.6 = (bf16[32,3456]{1,0:T(8,128)(2,1)S(1)}, bf16[32,3456]{1,0:T(8,128)(2,1)S(1)}, u32[]{:S(2)}, u32[]{:S(2)}) collective-permute-start(bf16[32,3456]{1,0:T(8,128)(2,1)S(1)} %get-tuple-element.37), channel_id=1, source_target_pairs={{0,48},{16,0},{32,16},{48,32},{64,112},{80,64},{96,80},{112,96},{1... | collective-permute-start | bytes 663560 | tf_op jit(solution)/shard_map/ppermute | solution.py:18
  60.1 6.5 %collective-permute-start.10 = (bf16[32,3456]{1,0:T(8,128)(2,1)S(1)}, bf16[32,3456]{1,0:T(8,128)(2,1)S(1)}, u32[]{:S(2)}, u32[]{:S(2)}) collective-permute-start(bf16[32,3456]{1,0:T(8,128)(2,1)S(1)} %get-tuple-element.46), channel_id=1, source_target_pairs={{0,32},{16,48},{32,0},{48,16},{64,96},{80,112},{96,64},{112,80},{1... | collective-permute-start | bytes 663560 | tf_op jit(solution)/shard_map/ppermute | solution.py:18
  60.2 13.2 %collective-permute-start.11 = (bf16[32,3456]{1,0:T(8,128)(2,1)S(1)}, bf16[32,3456]{1,0:T(8,128)(2,1)S(1)}, u32[]{:S(2)}, u32[]{:S(2)}) collective-permute-start(bf16[32,3456]{1,0:T(8,128)(2,1)S(1)} %get-tuple-element.42.refs_5_), channel_id=1, source_target_pairs={{0,16},{16,32},{32,48},{48,0},{64,80},{80,96},{96,112},{112,64},{1... | collective-permute-start | bytes 663560 | tf_op jit(solution)/shard_map/ppermute | solution.py:18
  61.1 12.3 %collective-permute-start.12 = (bf16[32,3456]{1,0:T(8,128)(2,1)S(1)}, bf16[32,3456]{1,0:T(8,128)(2,1)S(1)}, u32[]{:S(2)}, u32[]{:S(2)}) collective-permute-start(bf16[32,3456]{1,0:T(8,128)(2,1)S(1)} %get-tuple-element.47), channel_id=1, source_target_pairs={{0,48},{16,0},{32,16},{48,32},{64,112},{80,64},{96,80},{112,96},{1... | collective-permute-start | bytes 663560 | tf_op jit(solution)/shard_map/ppermute | solution.py:18
  63.1 10.5 %collective-permute-start.9 = (bf16[32,3456]{1,0:T(8,128)(2,1)S(1)}, bf16[32,3456]{1,0:T(8,128)(2,1)S(1)}, u32[]{:S(2)}, u32[]{:S(2)}) collective-permute-start(bf16[32,3456]{1,0:T(8,128)(2,1)S(1)} %get-tuple-element.44.refs_4_), channel_id=1, source_target_pairs={{0,64},{16,80},{32,96},{48,112},{64,0},{80,16},{96,32},{112,48},{1... | collective-permute-start | bytes 663560 | tf_op jit(solution)/shard_map/ppermute | solution.py:18
  73.7 5.3 %collective-permute-start.13 = (bf16[32,1664]{1,0:T(8,128)(2,1)S(1)}, bf16[32,1664]{1,0:T(8,128)(2,1)S(1)}, u32[]{:S(2)}, u32[]{:S(2)}) collective-permute-start(bf16[32,1664]{1,0:T(8,128)(2,1)S(1)} %shard_map.128.refs_0_), channel_id=1, source_target_pairs={{0,64},{16,80},{32,96},{48,112},{64,0},{80,16},{96,32},{112,48},{1... | collective-permute-start | bytes 319496 | tf_op jit(solution)/shard_map/ppermute | solution.py:18
  76.3 6.5 %collective-permute-start.17 = (bf16[32,1664]{1,0:T(8,128)(2,1)S(1)}, bf16[32,1664]{1,0:T(8,128)(2,1)S(1)}, u32[]{:S(2)}, u32[]{:S(2)}) collective-permute-start(bf16[32,1664]{1,0:T(8,128)(2,1)S(1)} %shard_map.127.refs_2_.refs_0_), channel_id=1, source_target_pairs={{0,16},{16,32},{32,48},{48,0},{64,80},{80,96},{96,112},{112,64},{1... | collective-permute-start | bytes 319496 | tf_op jit(solution)/shard_map/ppermute | solution.py:18
  76.3 7.2 %collective-permute-start.18 = (bf16[32,1664]{1,0:T(8,128)(2,1)S(1)}, bf16[32,1664]{1,0:T(8,128)(2,1)S(1)}, u32[]{:S(2)}, u32[]{:S(2)}) collective-permute-start(bf16[32,1664]{1,0:T(8,128)(2,1)S(1)} %shard_map.127.refs_2_.refs_0_), channel_id=1, source_target_pairs={{0,32},{16,48},{32,0},{48,16},{64,96},{80,112},{96,64},{112,80},{1... | collective-permute-start | bytes 319496 | tf_op jit(solution)/shard_map/ppermute | solution.py:18
  77.3 6.3 %collective-permute-start.19 = (bf16[32,1664]{1,0:T(8,128)(2,1)S(1)}, bf16[32,1664]{1,0:T(8,128)(2,1)S(1)}, u32[]{:S(2)}, u32[]{:S(2)}) collective-permute-start(bf16[32,1664]{1,0:T(8,128)(2,1)S(1)} %shard_map.127.refs_2_.refs_0_), channel_id=1, source_target_pairs={{0,48},{16,0},{32,16},{48,32},{64,112},{80,64},{96,80},{112,96},{1... | collective-permute-start | bytes 319496 | tf_op jit(solution)/shard_map/ppermute | solution.py:18
  79.0 14.2 %collective-permute-start.14 = (bf16[64,1664]{1,0:T(8,128)(2,1)S(1)}, bf16[64,1664]{1,0:T(8,128)(2,1)S(1)}, u32[]{:S(2)}, u32[]{:S(2)}) collective-permute-start(bf16[64,1664]{1,0:T(8,128)(2,1)S(1)} %shard_map.129.refs_0_.refs_4_), channel_id=1, source_target_pairs={{0,16},{16,32},{32,48},{48,0},{64,80},{80,96},{96,112},{112,64},{1... | collective-permute-start | bytes 638984 | tf_op jit(solution)/shard_map/ppermute | solution.py:18
  79.6 13.6 %collective-permute-start.15 = (bf16[64,1664]{1,0:T(8,128)(2,1)S(1)}, bf16[64,1664]{1,0:T(8,128)(2,1)S(1)}, u32[]{:S(2)}, u32[]{:S(2)}) collective-permute-start(bf16[64,1664]{1,0:T(8,128)(2,1)S(1)} %shard_map.129.refs_0_.refs_4_), channel_id=1, source_target_pairs={{0,32},{16,48},{32,0},{48,16},{64,96},{80,112},{96,64},{112,80},{1... | collective-permute-start | bytes 638984 | tf_op jit(solution)/shard_map/ppermute | solution.py:18
  82.8 10.4 %collective-permute-start.16 = (bf16[64,1664]{1,0:T(8,128)(2,1)S(1)}, bf16[64,1664]{1,0:T(8,128)(2,1)S(1)}, u32[]{:S(2)}, u32[]{:S(2)}) collective-permute-start(bf16[64,1664]{1,0:T(8,128)(2,1)S(1)} %shard_map.129.refs_0_.refs_4_), channel_id=1, source_target_pairs={{0,48},{16,0},{32,16},{48,32},{64,112},{80,64},{96,80},{112,96},{1... | collective-permute-start | bytes 638984 | tf_op jit(solution)/shard_map/ppermute | solution.py:18
  83.7 10.2 %collective-permute-start.20 = (bf16[128,1664]{1,0:T(8,128)(2,1)S(1)}, bf16[128,1664]{1,0:T(8,128)(2,1)S(1)}, u32[]{:S(2)}, u32[]{:S(2)}) collective-permute-start(bf16[128,1664]{1,0:T(8,128)(2,1)S(1)} %shard_map.131.refs_0_), channel_id=1, source_target_pairs={{0,64},{16,80},{32,96},{48,112},{64,0},{80,16},{96,32},{112,48},{1... | collective-permute-start | bytes 1277960 | tf_op jit(solution)/shard_map/ppermute | solution.py:18
  98.4 6.0 %collective-permute-start.21 = (bf16[256,2048]{1,0:T(8,128)(2,1)S(1)}, bf16[256,2048]{1,0:T(8,128)(2,1)S(1)}, u32[]{:S(2)}, u32[]{:S(2)}) collective-permute-start(bf16[256,2048]{1,0:T(8,128)(2,1)S(1)} %get-tuple-element.49), channel_id=1, source_target_pairs={{0,1},{1,0},{2,3},{3,2},{4,5},{5,4},{6,7},{7,6},{8,9},{9,8},{10,11... | collective-permute-start | bytes 3145736 | tf_op jit(solution)/shard_map/ppermute | solution.py:22
  138.9 4.9 %collective-permute-start.22 = (bf16[256,2048]{1,0:T(8,128)(2,1)S(1)}, bf16[256,2048]{1,0:T(8,128)(2,1)S(1)}, u32[]{:S(2)}, u32[]{:S(2)}) collective-permute-start(bf16[256,2048]{1,0:T(8,128)(2,1)S(1)} %bitcast.89), channel_id=1, source_target_pairs={{0,1},{1,0},{2,3},{3,2},{4,5},{5,4},{6,7},{7,6},{8,9},{9,8},{10,11... | collective-permute-start | bytes 3145736 | tf_op jit(solution)/shard_map/ppermute | solution.py:22
  146.9 9.7 %collective-permute-start.23 = (bf16[64,768]{1,0:T(8,128)(2,1)S(1)}, bf16[64,768]{1,0:T(8,128)(2,1)S(1)}, u32[]{:S(2)}, u32[]{:S(2)}) collective-permute-start(bf16[64,768]{1,0:T(8,128)(2,1)S(1)} %get-tuple-element.51), channel_id=1, source_target_pairs={{0,96},{16,112},{32,64},{48,80},{64,32},{80,48},{96,0},{112,16},{1... | collective-permute-start | bytes 294920 | tf_op jit(solution)/shard_map/ppermute | solution.py:18
  149.9 8.7 %collective-permute-start.24 = (bf16[64,768]{1,0:T(8,128)(2,1)S(1)}, bf16[64,768]{1,0:T(8,128)(2,1)S(1)}, u32[]{:S(2)}, u32[]{:S(2)}) collective-permute-start(bf16[64,768]{1,0:T(8,128)(2,1)S(1)} %get-tuple-element.52), channel_id=1, source_target_pairs={{0,80},{16,96},{32,112},{48,64},{64,16},{80,32},{96,48},{112,0},{1... | collective-permute-start | bytes 294920 | tf_op jit(solution)/shard_map/ppermute | solution.py:18
  154.0 6.9 %collective-permute-start.25 = (bf16[64,768]{1,0:T(8,128)(2,1)S(1)}, bf16[64,768]{1,0:T(8,128)(2,1)S(1)}, u32[]{:S(2)}, u32[]{:S(2)}) collective-permute-start(bf16[64,768]{1,0:T(8,128)(2,1)S(1)} %get-tuple-element.53), channel_id=1, source_target_pairs={{0,112},{16,64},{32,80},{48,96},{64,48},{80,0},{96,16},{112,32},{1... | collective-permute-start | bytes 294920 | tf_op jit(solution)/shard_map/ppermute | solution.py:18
  155.0 5.8 %collective-permute-start.26 = (bf16[64,768]{1,0:T(8,128)(2,1)S(1)}, bf16[64,768]{1,0:T(8,128)(2,1)S(1)}, u32[]{:S(2)}, u32[]{:S(2)}) collective-permute-start(bf16[64,768]{1,0:T(8,128)(2,1)S(1)} %get-tuple-element.54), channel_id=1, source_target_pairs={{0,32},{16,48},{32,0},{48,16},{64,96},{80,112},{96,64},{112,80},{1... | collective-permute-start | bytes 294920 | tf_op jit(solution)/shard_map/ppermute | solution.py:18
  155.8 6.3 %collective-permute-start.27 = (bf16[64,768]{1,0:T(8,128)(2,1)S(1)}, bf16[64,768]{1,0:T(8,128)(2,1)S(1)}, u32[]{:S(2)}, u32[]{:S(2)}) collective-permute-start(bf16[64,768]{1,0:T(8,128)(2,1)S(1)} %get-tuple-element.55), channel_id=1, source_target_pairs={{0,64},{16,80},{32,96},{48,112},{64,0},{80,16},{96,32},{112,48},{1... | collective-permute-start | bytes 294920 | tf_op jit(solution)/shard_map/ppermute | solution.py:18
  156.6 6.4 %collective-permute-start.28 = (bf16[64,768]{1,0:T(8,128)(2,1)S(1)}, bf16[64,768]{1,0:T(8,128)(2,1)S(1)}, u32[]{:S(2)}, u32[]{:S(2)}) collective-permute-start(bf16[64,768]{1,0:T(8,128)(2,1)S(1)} %get-tuple-element.56), channel_id=1, source_target_pairs={{0,16},{16,32},{32,48},{48,0},{64,80},{80,96},{96,112},{112,64},{1... | collective-permute-start | bytes 294920 | tf_op jit(solution)/shard_map/ppermute | solution.py:18
  158.6 4.5 %collective-permute-start.29 = (bf16[64,768]{1,0:T(8,128)(2,1)S(1)}, bf16[64,768]{1,0:T(8,128)(2,1)S(1)}, u32[]{:S(2)}, u32[]{:S(2)}) collective-permute-start(bf16[64,768]{1,0:T(8,128)(2,1)S(1)} %get-tuple-element.57), channel_id=1, source_target_pairs={{0,48},{16,0},{32,16},{48,32},{64,112},{80,64},{96,80},{112,96},{1... | collective-permute-start | bytes 294920 | tf_op jit(solution)/shard_map/ppermute | solution.py:18
  168.5 21.3 %all-to-all-start.3 = ((f32[128,8,128]{2,1,0:T(8,128)}), f32[128,8,128]{2,1,0:T(8,128)S(1)}, u32[]{:S(2)}, u32[]{:S(2)}) async-start(f32[128,8,128]{2,1,0:T(8,128)} %broadcast_in_dim.118), calls=%async_computation.3 | async-start | bytes 1048576 | tf_op jit(solution)/shard_map/all_to_all | solution.py:444
  (5 other events, 74.7 us)
